TPU v7x, 256 devices: a whole 4x4x8 slice. The times are simulated.
256 devices in a mesh: wide: 32 (over z, x), narrow: 8 (over y, core).
Axes of the slice: x: 4, y: 4, z: 8, core: 2. Of those that a mesh axis runs over, the one named last changes fastest.
Arguments:
- hidden_in: bfloat16 [4096, 2048], P(('wide', 'narrow')), may hold values from -6 to 6
- queries: bfloat16 [4096, 2048], P(('wide', 'narrow')), may hold values from -6 to 6
- cache_key: bfloat16 [4096, 128, 256], P(('wide', 'narrow')), may hold values from -6 to 6
- cache_value: bfloat16 [4096, 128, 256], P(('wide', 'narrow')), may hold values from -6 to 6
- new_key: bfloat16 [4096, 256], P(('wide', 'narrow')), may hold values from -6 to 6
- new_value: bfloat16 [4096, 256], P(('wide', 'narrow')), may hold values from -6 to 6
- lengths: int32 [4096], P(('wide', 'narrow')), may hold values from 2 to 128, as said below
- norm_gain: bfloat16 [2048], replicated, may hold values from 0.5 to 1.5
- gate_codes: bfloat16 [256, 2048, 384], P(('wide', 'narrow')), may hold values from -4 to 4
- gate_scale: float32 [256, 16, 3], P(('wide', 'narrow')), may hold values from 0.011048543 to 0.044194173
- up_codes: bfloat16 [256, 2048, 384], P(('wide', 'narrow')), may hold values from -4 to 4
- up_scale: float32 [256, 16, 3], P(('wide', 'narrow')), may hold values from 0.011048543 to 0.044194173
- down_codes: bfloat16 [256, 384, 2048], P(('wide', 'narrow')), may hold values from -4 to 4
- down_scale: float32 [256, 3, 16], P(('wide', 'narrow')), may hold values from 0.018042196 to 0.07216878
- think_ids: int32 [4096, 8], P(('wide', 'narrow')), may hold values from 0 to 127, all different within a row; in each aligned block of 16 rows (0 to 15, 16 to 31, ...) at most 2 rows name the same one
- think_gates: float32 [4096, 8], P(('wide', 'narrow')), may hold values from 0.05 to 0.3
- talker_source: int32 [4096], P(('wide', 'narrow')), may hold values from 0 to 4095, as said below
- talker_gain: bfloat16 [2048], replicated, may hold values from 0.5 to 1.5
- talk_gate_w: bfloat16 [8, 2048, 384], P('narrow'), may hold values from -0.125 to 0.125
- talk_up_w: bfloat16 [8, 2048, 384], P('narrow'), may hold values from -0.125 to 0.125
- talk_down_w: bfloat16 [8, 384, 1024], P('narrow'), may hold values from -0.3125 to 0.3125
- talk_ids: int32 [4096, 2], P(('wide', 'narrow')), may hold values from 0 to 7, all different within a row; in each aligned block of 16 rows (0 to 15, 16 to 31, ...) at most 8 rows name the same one
- talk_gates: float32 [4096, 2], P(('wide', 'narrow')), may hold values from 0.3 to 0.7
Outputs:
- thinker_out: bfloat16 [4096, 2048], P(('wide', 'narrow'))
- talker_out: bfloat16 [4096, 1024], P(('wide', 'narrow'))
Inputs may be any that keep to these rules, and one draw needn't show every extreme that they name: `think_ids`: each row names 8 different thinker experts; among the rows of one device no expert is named by more than 2 rows. `talk_ids`: each position names 2 different talker experts; among the positions of one device no expert is named by more than 8. `lengths`: some row uses all 128 cached positions. `talker_source`: A permutation of the rows. The row feeding a talker position lies on the same narrow index as the position. The rows of one device feed positions on exactly 16 devices, 1 positions on each.
All inputs are finite; a program needn't handle non-finite values.
Results may differ from a plain program's by a relative error of at most 0.018.
Values may be sent and summed in bfloat16 or wider, within the bound.
No kernel may reach another device: no remote copies, remote signals or barrier semaphores. Data moves between devices by JAX's collectives and lax.ppermute only.
A program may use at most 64 MiB of HBM per device.

v0:
```python
import jax
import jax.numpy as jnp
from jax import lax
from jax.experimental import pallas as pl
from jax.experimental.pallas import tpu as pltpu
from jax.sharding import Mesh
from jax.sharding import PartitionSpec as P

HEADS = 16
HEAD_DIM = 128
BLK = 128
CHIPS = 128
LANES = 128
ROWS = 16
CTX = 128
D = 2048
FH = 384
TD = 1024
EPSILON = 1e-06
MSG = 40
INFO_ROW = 32
TWIDE = D + 2 * LANES

f32 = jnp.float32
bf16 = jnp.bfloat16
VM = pl.BlockSpec(memory_space=pltpu.VMEM)
SM = pl.BlockSpec(memory_space=pltpu.SMEM)
HB = pl.BlockSpec(memory_space=pl.ANY)


def lane_iota(rows):
    return lax.broadcasted_iota(jnp.int32, (rows, LANES), 1)


def slots(ids):
    expert = lax.broadcasted_iota(jnp.int32, (LANES, ROWS), 0)
    picked = jnp.zeros((LANES, ROWS), f32)
    for k in range(ids.shape[0]):
        picked = picked + jnp.where(ids[k : k + 1, :] == expert, 1.0, 0.0)
    before = lax.broadcasted_iota(jnp.int32, (ROWS, ROWS), 0) < lax.broadcasted_iota(
        jnp.int32, (ROWS, ROWS), 1
    )
    rank = jnp.dot(
        picked.astype(bf16), jnp.where(before, 1.0, 0.0).astype(bf16), preferred_element_type=f32
    )
    first = jnp.where((picked > 0.5) & (rank < 0.5), 1.0, 0.0)
    second = jnp.where((picked > 0.5) & (rank > 0.5) & (rank < 1.5), 1.0, 0.0)
    return first, second


def high_low(values):
    high = values.astype(bf16)
    low = (values - high.astype(f32)).astype(bf16)
    return high, low


def gather_t(onehot, values):
    return lax.dot_general(
        onehot, values, (((0,), (0,)), ((), ())), preferred_element_type=f32
    )


def attend_kernel(
    hidden, queries, cache_key, cache_value, new_key, new_value, lengths, gain, ids,
    source, talk_ids, talk_gates, residual, message, asked, mixed, spread_out, keys, vals, sems,
):
    copies = []
    for i in range(4):
        part = pl.ds(i * 4, 4)
        k_copy = pltpu.make_async_copy(cache_key.at[part], keys.at[part], sems.at[i])
        v_copy = pltpu.make_async_copy(cache_value.at[part], vals.at[part], sems.at[4 + i])
        k_copy.start()
        v_copy.start()
        copies.append((k_copy, v_copy))
    scaling = HEAD_DIM ** (-0.5)
    for h in range(HEADS):
        asked[pl.ds(h, ROWS, stride=HEADS), :] = queries[:, h * 128 : (h + 1) * 128].astype(f32)
    head = lax.broadcasted_iota(jnp.int32, (HEADS, LANES), 0)
    front = head < HEADS // 2
    lane = lane_iota(HEADS)
    fresh_key = new_key[...].astype(f32)
    fresh_value = new_value[...].astype(f32)
    for r in range(ROWS):
        if r % 4 == 0:
            copies[r // 4][0].wait()
            copies[r // 4][1].wait()
        query = asked[r * HEADS : (r + 1) * HEADS, :]
        split = jnp.concatenate(
            [jnp.where(front, query, 0.0), jnp.where(front, 0.0, query)], axis=1
        ).astype(bf16)
        scores = (
            lax.dot_general(
                split, keys[r], (((1,), (1,)), ((), ())), preferred_element_type=f32
            )
            * scaling
        )
        own_key = jnp.where(front, fresh_key[r : r + 1, :128], fresh_key[r : r + 1, 128:])
        own_val = jnp.where(front, fresh_value[r : r + 1, :128], fresh_value[r : r + 1, 128:])
        fresh = jnp.sum(query * own_key, axis=1, keepdims=True) * scaling
        scores = jnp.where(lane < lengths[r], scores, -jnp.inf)
        highest = jnp.maximum(jnp.max(scores, axis=1, keepdims=True), fresh)
        weights = jnp.exp(scores - highest)
        own = jnp.exp(fresh - highest)
        total = jnp.sum(weights, axis=1, keepdims=True) + own
        probs = (weights / total).astype(bf16)
        own_prob = (own / total).astype(bf16).astype(f32)
        both = jnp.dot(probs, vals[r], preferred_element_type=f32)
        mixed[r * HEADS : (r + 1) * HEADS, :] = (
            jnp.where(front, both[:, :128], both[:, 128:]) + own_prob * own_val
        )
    squares = jnp.zeros((ROWS, LANES), f32)
    for h in range(HEADS):
        cols = slice(h * 128, (h + 1) * 128)
        part = hidden[:, cols].astype(f32) + mixed[pl.ds(h, ROWS, stride=HEADS), :]
        residual[:, cols] = part
        squares = squares + part * part
    spread = jnp.sum(squares, axis=1, keepdims=True) * (1.0 / D)
    scale = lax.rsqrt(spread + EPSILON)
    first, second = slots(ids[...])
    both_slots = jnp.concatenate([first, second], axis=0).astype(bf16)
    for h in range(HEADS):
        cols = slice(h * 128, (h + 1) * 128)
        normed = (residual[:, cols] * scale * gain[h : h + 1, :].astype(f32)).astype(bf16)
        sent = jnp.dot(both_slots, normed, preferred_element_type=f32)
        spread_out[pl.ds(h, CHIPS, stride=32), :] = sent[:CHIPS]
        spread_out[pl.ds(HEADS + h, CHIPS, stride=32), :] = sent[CHIPS:]
    message[:, :INFO_ROW, :] = spread_out[...].reshape(CHIPS, 32, LANES).astype(bf16)
    origin = source[...]
    chip = lax.broadcasted_iota(jnp.int32, (CHIPS, ROWS), 0)
    onehot = jnp.where((origin // 32) == chip, 1.0, 0.0).astype(bf16)
    gates = talk_gates[...]
    high = gates.astype(bf16).astype(f32)
    low = gates - high
    fact = lax.broadcasted_iota(jnp.int32, (LANES, ROWS), 0)
    facts = jnp.where(fact == 16 + origin % ROWS, 1.0, 0.0)
    for k in range(2):
        chosen = talk_ids[k : k + 1, :]
        facts = facts + jnp.where(fact == chosen, high[k : k + 1, :], 0.0)
        facts = facts + jnp.where(fact == chosen + 8, low[k : k + 1, :], 0.0)
    told = lax.dot_general(
        onehot, facts.astype(bf16), (((1,), (1,)), ((), ())), preferred_element_type=f32
    )
    message[:, INFO_ROW:, :] = jnp.broadcast_to(
        told.reshape(CHIPS, 1, LANES), (CHIPS, MSG - INFO_ROW, LANES)
    ).astype(bf16)


def silu(x):
    return x * jax.nn.sigmoid(x)


def restore_kernel(gs0, us0, ds0, gs1, us1, ds1, g0, u0, d0, g1, u1, d1, gw, uw, dw):
    i = pl.program_id(0)
    for half, (gs, us, ds, g, u, d) in enumerate(
        [(gs0, us0, ds0, g0, u0, d0), (gs1, us1, ds1, g1, u1, d1)]
    ):
        for j in range(FH // BLK):
            cols = slice(j * BLK, (j + 1) * BLK)
            there = slice(half * FH + j * BLK, half * FH + (j + 1) * BLK)
            gw[:, there] = (g[0, :, cols].astype(f32) * gs[j, 0, i]).astype(bf16)
            uw[:, there] = (u[0, :, cols].astype(f32) * us[j, 0, i]).astype(bf16)
            dw[there, :] = (d[0, cols, :].astype(f32) * ds[j, 0, i]).astype(bf16)


def expert_kernel(
    arrived, g, u, d, produced, info, wide_in, rows_in, gw, uw, dw, out32, sems,
):
    copies = []
    for i, (src, dst) in enumerate([(g, gw), (u, uw), (d, dw)]):
        copy = pltpu.make_async_copy(src, dst, sems.at[i])
        copy.start()
        copies.append(copy)
    wide_in[...] = arrived[...].astype(f32).reshape(CHIPS * MSG, LANES)
    info[...] = wide_in[pl.ds(INFO_ROW, CHIPS, stride=MSG), :].astype(bf16)
    for s in range(2):
        for h in range(HEADS):
            rows_in[s * CHIPS : (s + 1) * CHIPS, h * 128 : (h + 1) * 128] = wide_in[
                pl.ds(s * HEADS + h, CHIPS, stride=MSG), :
            ].astype(bf16)
    copies[0].wait()
    gated = jnp.dot(rows_in[...], gw[...], preferred_element_type=f32)
    copies[1].wait()
    lifted = jnp.dot(rows_in[...], uw[...], preferred_element_type=f32)
    middle = (silu(gated) * lifted).astype(bf16)
    copies[2].wait()
    for h in range(HEADS // 2):
        part = jnp.dot(middle, dw[:, h * 256 : (h + 1) * 256], preferred_element_type=f32)
        for s in range(2):
            for k in range(2):
                spot = pl.ds(s * HEADS + 2 * h + k, CHIPS, stride=32)
                out32[spot, :] = part[s * CHIPS : (s + 1) * CHIPS, k * 128 : (k + 1) * 128]
    produced[...] = out32[...].reshape(CHIPS, 32, LANES).astype(bf16)


def combine_kernel(
    returned, residual, ids, gates, info, gain, thinker_out, onward, wide_in, rows_in,
):
    wide_in[...] = returned[...].astype(f32).reshape(CHIPS * 32, LANES)
    for s in range(2):
        for h in range(HEADS):
            rows_in[s * CHIPS : (s + 1) * CHIPS, h * 128 : (h + 1) * 128] = wide_in[
                pl.ds(s * HEADS + h, CHIPS, stride=32), :
            ].astype(bf16)
    expert = lax.broadcasted_iota(jnp.int32, (LANES, ROWS), 0)
    weight = jnp.zeros((LANES, ROWS), f32)
    for k in range(8):
        weight = weight + jnp.where(ids[k : k + 1, :] == expert, gates[k : k + 1, :], 0.0)
    first, second = slots(ids[...])
    high, low = high_low(jnp.concatenate([first * weight, second * weight], axis=0))
    both = gather_t(jnp.concatenate([high, low], axis=1), rows_in[...])
    routed = both[:ROWS] + both[ROWS:]
    outcome = (residual[...] + routed).astype(bf16)
    thinker_out[...] = outcome
    values = outcome.astype(f32)
    spread = jnp.sum(values * values, axis=1, keepdims=True) * (1.0 / D)
    scale = lax.rsqrt(spread + EPSILON)
    for h in range(HEADS):
        cols = slice(h * 128, (h + 1) * 128)
        onward[:, cols] = (values[:, cols] * scale * gain[h : h + 1, :].astype(f32)).astype(bf16)
    lane = lane_iota(ROWS)
    told = info[...]
    pick = jnp.where(
        lane == 16 + lax.broadcasted_iota(jnp.int32, (ROWS, LANES), 0), 1.0, 0.0
    ).astype(bf16)
    goal = lax.dot_general(
        pick, told, (((1,), (1,)), ((), ())), preferred_element_type=f32
    ).astype(bf16)
    onward[:, D : D + LANES] = goal
    onward[:, D + LANES :] = jnp.dot(goal, told, preferred_element_type=f32).astype(bf16)


def talker_kernel(
    place, m0, m1, m2, m3, g0, u0, d0, g1, u1, d1, relayed, rows_in, gw, uw, dw, out32, sems,
):
    copies = []
    for i, (src, dst) in enumerate(
        [
            (g0, gw.at[0]), (u0, uw.at[0]), (d0, dw.at[0]),
            (g1, gw.at[1]), (u1, uw.at[1]), (d1, dw.at[1]),
        ]
    ):
        copy = pltpu.make_async_copy(src.at[0], dst, sems.at[i])
        copy.start()
        copies.append(copy)
    for i, m in enumerate([m0, m1, m2, m3]):
        rows_in[i * ROWS : (i + 1) * ROWS, :] = m[...]
    inputs = rows_in[:, :D]
    goal = rows_in[:, D : D + LANES]
    shares = rows_in[:, D + LANES :].astype(f32)
    lane = lane_iota(4 * ROWS)
    total = jnp.zeros((4 * ROWS, TD), f32)
    for half in range(2):
        expert = place[0] if half == 0 else place[0] + 1 - 2 * (place[0] % 2)
        share = jnp.sum(
            jnp.where((lane == expert) | (lane == expert + 8), shares, 0.0), axis=1, keepdims=True
        )
        copies[3 * half].wait()
        gated = jnp.dot(inputs, gw[half], preferred_element_type=f32)
        copies[3 * half + 1].wait()
        lifted = jnp.dot(inputs, uw[half], preferred_element_type=f32)
        middle = (silu(gated) * lifted).astype(bf16)
        copies[3 * half + 2].wait()
        part = jnp.dot(middle, dw[half], preferred_element_type=f32)
        total = total + share * part.astype(bf16).astype(f32)
    total = total.astype(bf16)
    for h in range(TD // 128):
        out32[pl.ds(h, CHIPS, stride=8), :] = gather_t(goal, total[:, h * 128 : (h + 1) * 128])
    relayed[...] = out32[...].reshape(CHIPS, 8, LANES).astype(bf16)


def settle_kernel(returned, source, talker_out, wide_in):
    wide_in[...] = returned[...].astype(f32).reshape(CHIPS * 8, LANES)
    chip = lax.broadcasted_iota(jnp.int32, (CHIPS, ROWS), 0)
    onehot = jnp.where((chip // 4) == (source[...] // 128), 1.0, 0.0).astype(bf16)
    for h in range(TD // 128):
        rows = wide_in[pl.ds(h, CHIPS, stride=8), :].astype(bf16)
        talker_out[:, h * 128 : (h + 1) * 128] = gather_t(onehot, rows).astype(bf16)


def sds(shape, dtype):
    return jax.ShapeDtypeStruct(shape, dtype)


def swap(value):
    return lax.ppermute(value, "c", [(0, 1), (1, 0)])


def spread_chips(value):
    return lax.all_to_all(value, ("z", "x", "y"), 0, 0, tiled=True)


def local(
    hidden_in, queries, cache_key, cache_value, new_key, new_value, lengths, norm_gain,
    gate_codes, gate_scale, up_codes, up_scale, down_codes, down_scale, think_ids, think_gates,
    talker_source, talker_gain, talk_gate_w, talk_up_w, talk_down_w, talk_ids, talk_gates,
):
    own = (gate_codes, up_codes, down_codes)
    own_scale = (
        jnp.transpose(gate_scale, (2, 0, 1)),
        jnp.transpose(up_scale, (2, 0, 1)),
        jnp.transpose(down_scale, (1, 0, 2)),
    )
    other = tuple(swap(w) for w in own)
    other_scale = tuple(swap(s) for s in own_scale)
    source = talker_source.reshape(1, ROWS)
    ids = think_ids.T

    residual, message = pl.pallas_call(
        attend_kernel,
        out_shape=(sds((ROWS, D), f32), sds((CHIPS, MSG, LANES), bf16)),
        in_specs=[VM] * 2 + [HB] * 2 + [VM] * 2 + [SM] + [VM] * 5,
        out_specs=(VM, VM),
        scratch_shapes=[
            pltpu.VMEM((ROWS * HEADS, LANES), f32),
            pltpu.VMEM((ROWS * HEADS, LANES), f32),
            pltpu.VMEM((CHIPS * 32, LANES), f32),
            pltpu.VMEM((ROWS, CTX, 256), bf16),
            pltpu.VMEM((ROWS, CTX, 256), bf16),
            pltpu.SemaphoreType.DMA((8,)),
        ],
        name="attend",
    )(
        hidden_in, queries, cache_key, cache_value, new_key, new_value, lengths,
        norm_gain.reshape(HEADS, LANES), ids, source, talk_ids.T, talk_gates.T,
    )
    arrived = spread_chips(message)
    tall = pl.BlockSpec((1, BLK, FH), lambda i: (0, i, 0))
    flat = pl.BlockSpec((1, FH, BLK), lambda i: (0, 0, i))
    tall_out = pl.BlockSpec((BLK, 2 * FH), lambda i: (i, 0))
    flat_out = pl.BlockSpec((2 * FH, BLK), lambda i: (0, i))
    dense = pl.pallas_call(
        restore_kernel,
        grid=(D // BLK,),
        out_shape=(sds((D, 2 * FH), bf16), sds((D, 2 * FH), bf16), sds((2 * FH, D), bf16)),
        in_specs=[SM] * 6 + [tall, tall, flat] * 2,
        out_specs=(tall_out, tall_out, flat_out),
        cost_estimate=pl.CostEstimate(
            flops=6 * D * FH, bytes_accessed=24 * D * FH, transcendentals=0
        ),
        name="restore",
    )(*own_scale, *other_scale, *own, *other)
    produced, info = pl.pallas_call(
        expert_kernel,
        out_shape=(sds((CHIPS, 32, LANES), bf16), sds((CHIPS, LANES), bf16)),
        in_specs=[VM] + [HB] * 3,
        out_specs=(VM, VM),
        scratch_shapes=[
            pltpu.VMEM((CHIPS * MSG, LANES), f32),
            pltpu.VMEM((2 * CHIPS, D), bf16),
            pltpu.VMEM((D, 2 * FH), bf16),
            pltpu.VMEM((D, 2 * FH), bf16),
            pltpu.VMEM((2 * FH, D), bf16),
            pltpu.VMEM((CHIPS * 32, LANES), f32),
            pltpu.SemaphoreType.DMA((3,)),
        ],
        name="experts",
    )(arrived, *dense)
    returned = spread_chips(produced)
    talk_own = (talk_gate_w, talk_up_w, talk_down_w)
    talk_held = lax.optimization_barrier((*talk_own, arrived))[:3]
    talk_other = tuple(swap(w) for w in talk_held)
    thinker_out, onward = pl.pallas_call(
        combine_kernel,
        out_shape=(sds((ROWS, D), bf16), sds((ROWS, TWIDE), bf16)),
        in_specs=[VM] * 6,
        out_specs=(VM, VM),
        scratch_shapes=[
            pltpu.VMEM((CHIPS * 32, LANES), f32),
            pltpu.VMEM((2 * CHIPS, D), bf16),
        ],
        name="combine",
    )(returned, residual, ids, think_gates.T, info, talker_gain.reshape(HEADS, LANES))
    peers = [
        lax.ppermute(onward, "y", [(i, (i + o) % 4) for i in range(4)]) for o in (1, 2, 3)
    ]
    place = (lax.axis_index("y") * 2 + lax.axis_index("c")).astype(jnp.int32).reshape(1)
    relayed = pl.pallas_call(
        talker_kernel,
        out_shape=sds((CHIPS, 8, LANES), bf16),
        in_specs=[SM] + [VM] * 4 + [HB] * 6,
        out_specs=VM,
        scratch_shapes=[
            pltpu.VMEM((4 * ROWS, TWIDE), bf16),
            pltpu.VMEM((2, D, FH), bf16),
            pltpu.VMEM((2, D, FH), bf16),
            pltpu.VMEM((2, FH, TD), bf16),
            pltpu.VMEM((CHIPS * 8, LANES), f32),
            pltpu.SemaphoreType.DMA((6,)),
        ],
        name="talkers",
    )(place, onward, *peers, *talk_own, *talk_other)
    settled = spread_chips(relayed)
    talker_out = pl.pallas_call(
        settle_kernel,
        out_shape=sds((ROWS, TD), bf16),
        in_specs=[VM, VM],
        out_specs=VM,
        scratch_shapes=[pltpu.VMEM((CHIPS * 8, LANES), f32)],
        name="settle",
    )(settled, source)
    return (thinker_out, talker_out)


def solution(mesh):
    fine = Mesh(mesh.devices.reshape(8, 4, 4, 2), ("z", "x", "y", "c"))
    every = ("z", "x", "y", "c")
    two = P(every, None)
    three = P(every, None, None)
    talk = P(("y", "c"), None, None)
    return jax.shard_map(
        local,
        mesh=fine,
        in_specs=(
            two, two, three, three, two, two, P(every), P(),
            three, three, three, three, three, three, two, two,
            P(every), P(), talk, talk, talk, two, two,
        ),
        out_specs=(two, two),
        check_vma=False,
    )
```

profile of v0, /device:TPU:2, one launch (start us, length us, event | category | flops | bytes accessed | tf_op | source)
XLA Modules:
  0.0 151.8 jit_solution(5884068055500267398)
XLA Ops:
  0.6 10.5 %attend.1 = (f32[16,2048]{1,0:T(8,128)}, bf16[128,40,128]{2,1,0:T(8,128)(2,1)}) custom-call(bf16[16,2048]{1,0:T(8,128)(2,1)} %hidden.1, bf16[16,2048]{1,0:T(8,128)(2,1)} %queries.1, bf16[16,128,256]{2,1,0:T(8,128)(2,1)} %cache_key.1, bf16[16,128,256]{2,1,0:T(8,128)(2,1)} %cache_value.1, bf16[16,256]{1,0:T(8,128)(2,1)} %new_key.1, bf16[16,256]{1,0:T(8,128)(2,1)} %new_value.1, ...), custom_call_target="tpu_custom_call" | custom-call | tf_op jit(solution)/shard_map/attend/pallas_call | solution.py:308
  11.2 0.0 copy-start.3
  11.2 0.0 copy-start.10
  11.2 0.0 copy-start.11
  11.2 0.0 copy-start.12
  11.2 15.6 %all-to-all-start = ((bf16[128,40,128]{2,1,0:T(8,128)(2,1)}), bf16[128,40,128]{2,1,0:T(8,128)(2,1)S(1)}, u32[]{:S(2)}, u32[]{:S(2)}) async-start(bf16[128,40,128]{2,1,0:T(8,128)(2,1)} %get-tuple-element.14), calls=%async_computation | async-start | bytes 2621440 | tf_op jit(solution)/shard_map/all_to_all | solution.py:289
  26.8 0.1 collective-permute-start.3
  26.9 0.5 collective-permute-start.4
  27.4 0.1 collective-permute-start.5
  27.5 0.4 collective-permute-start
  27.9 0.1 collective-permute-start.1
  28.0 6.9 %collective-permute-done.gs1 = f32[3,1,16]{2,1,0:T(1,128)S(1)} collective-permute-done((f32[3,1,16]{2,1,0:T(1,128)S(1)}, f32[3,1,16]{2,1,0:T(1,128)S(1)}, u32[]{:S(2)}, u32[]{:S(2)}) %collective-permute-start) | collective-permute-done | bytes 224 | tf_op jit(solution)/shard_map/ppermute | solution.py:285
  34.9 0.0 copy-done.12
  34.9 0.1 collective-permute-start.2
  35.1 0.0 collective-permute-done.1.us1
  35.1 1.0 collective-permute-done.2.ds1
  36.1 0.0 collective-permute-done.3.g1
  36.1 1.1 copy-done.4
  37.2 0.0 collective-permute-done.4.u1
  37.3 1.2 copy-done.5
  38.5 0.0 collective-permute-done.5.d1
  38.5 0.0 copy-done.15
  38.5 12.5 %restore.1 = (bf16[2048,768]{1,0:T(8,128)(2,1)}, bf16[2048,768]{1,0:T(8,128)(2,1)}, bf16[768,2048]{1,0:T(8,128)(2,1)}) custom-call(f32[3,1,16]{2,1,0:T(1,128)} %bitcast.18, f32[3,1,16]{2,1,0:T(1,128)} %bitcast.20, f32[3,1,16]{2,1,0:T(1,128)} %bitcast.22, f32[3,1,16]{2,1,0:T(1,128)} %copy-done.13, f32[3,1,16]{2,1,0:T(1,128)} %copy-done.14, ...), custom_call_target="tpu_custom_call" | custom-call | flops 4718592 | bytes 18874368 | tf_op jit(solution)/shard_map/restore/pallas_call | solution.py:331
  51.0 12.1 %all-to-all-done.arrived = bf16[128,40,128]{2,1,0:T(8,128)(2,1)S(1)} async-done(((bf16[128,40,128]{2,1,0:T(8,128)(2,1)}), bf16[128,40,128]{2,1,0:T(8,128)(2,1)S(1)}, u32[]{:S(2)}, u32[]{:S(2)}) %all-to-all-start) | async-done | bytes 1310752 | tf_op jit(solution)/shard_map/all_to_all | solution.py:289
  63.1 1.0 copy-done
  64.1 8.8 %experts.1 = (bf16[128,32,128]{2,1,0:T(8,128)(2,1)}, bf16[128,128]{1,0:T(8,128)(2,1)}) custom-call(bf16[128,40,128]{2,1,0:T(8,128)(2,1)} %copy-done, bf16[2048,768]{1,0:T(8,128)(2,1)} %get-tuple-element.15.g, bf16[2048,768]{1,0:T(8,128)(2,1)} %get-tuple-element.16.u, bf16[768,2048]{1,0:T(8,128)(2,1)} %get-tuple-element.17.d), custom_call_target="tpu_custom_call" | custom-call | tf_op jit(solution)/shard_map/experts/pallas_call | solution.py:342
  72.9 0.0 copy-start.2
  72.9 7.1 %all-to-all-start.1 = ((bf16[128,32,128]{2,1,0:T(8,128)(2,1)}), bf16[128,32,128]{2,1,0:T(8,128)(2,1)S(1)}, u32[]{:S(2)}, u32[]{:S(2)}) async-start(bf16[128,32,128]{2,1,0:T(8,128)(2,1)} %get-tuple-element.18), calls=%async_computation.1 | async-start | bytes 2097152 | tf_op jit(solution)/shard_map/all_to_all | solution.py:289
  80.0 0.1 collective-permute-start.10
  80.1 0.0 copy-done.2
  80.1 0.5 collective-permute-start.9
  80.6 0.1 collective-permute-start.11
  80.7 29.4 %all-to-all-done.1.returned = bf16[128,32,128]{2,1,0:T(8,128)(2,1)S(1)} async-done(((bf16[128,32,128]{2,1,0:T(8,128)(2,1)}), bf16[128,32,128]{2,1,0:T(8,128)(2,1)S(1)}, u32[]{:S(2)}, u32[]{:S(2)}) %all-to-all-start.1) | async-done | bytes 1048608 | tf_op jit(solution)/shard_map/all_to_all | solution.py:289
  110.2 1.0 copy-done.1
  111.2 4.0 %combine.1 = (bf16[16,2048]{1,0:T(8,128)(2,1)}, bf16[16,2304]{1,0:T(8,128)(2,1)}) custom-call(bf16[128,32,128]{2,1,0:T(8,128)(2,1)} %copy-done.1, f32[16,2048]{1,0:T(8,128)} %get-tuple-element.19.residual, s32[8,16]{1,0:T(8,128)} %bitcast.12, f32[8,16]{1,0:T(8,128)} %bitcast.14, bf16[128,128]{1,0:T(8,128)(2,1)} %get-tuple-element.20.info, ...), custom_call_target="tpu_custom_call" | custom-call | tf_op jit(solution)/shard_map/combine/pallas_call | solution.py:362
  115.2 0.5 collective-permute-start.6
  115.7 1.0 collective-permute-start.7
  116.7 0.0 collective-permute-done.11.d1
  116.7 1.7 %collective-permute-start.8 = (bf16[16,2304]{1,0:T(8,128)(2,1)}, bf16[16,2304]{1,0:T(8,128)(2,1)S(1)}, u32[]{:S(2)}, u32[]{:S(2)}) collective-permute-start(bf16[16,2304]{1,0:T(8,128)(2,1)} %get-tuple-element.22.m0), channel_id=1, source_target_pairs={{0,6},{2,0},{4,2},{6,4},{1,7},{3,1},{5,3},{7,5},{8,14},{10,8},{12,... | collective-permute-start | bytes 221192 | tf_op jit(solution)/shard_map/ppermute | solution.py:374
  118.4 0.0 collective-permute-done.10.u1
  118.4 0.0 collective-permute-done.9.g1
  118.4 2.5 %collective-permute-done.6.m1 = bf16[16,2304]{1,0:T(8,128)(2,1)S(1)} collective-permute-done((bf16[16,2304]{1,0:T(8,128)(2,1)}, bf16[16,2304]{1,0:T(8,128)(2,1)S(1)}, u32[]{:S(2)}, u32[]{:S(2)}) %collective-permute-start.6) | collective-permute-done | bytes 73760 | tf_op jit(solution)/shard_map/ppermute | solution.py:374
  120.9 0.8 collective-permute-done.7.m2
  121.8 0.8 collective-permute-done.8.m3
  122.6 0.6 copy-done.9
  123.2 5.7 %talkers.1 = bf16[128,8,128]{2,1,0:T(8,128)(2,1)} custom-call(s32[1]{0:T(128)} %bitcast.10.place, bf16[16,2304]{1,0:T(8,128)(2,1)} %get-tuple-element.22.m0, bf16[16,2304]{1,0:T(8,128)(2,1)} %copy-done.7, bf16[16,2304]{1,0:T(8,128)(2,1)} %copy-done.8, bf16[16,2304]{1,0:T(8,128)(2,1)} %copy-done.9, bf16[1,2048,384]{2,1,0:T(8,128)(2,1)} %g0.3, ...), custom_call_target="tpu_custom_call" | custom-call | tf_op jit(solution)/shard_map/talkers/pallas_call | solution.py:377
  128.9 21.1 %all_to_all.15.returned = bf16[128,8,128]{2,1,0:T(8,128)(2,1)} all-to-all(bf16[128,8,128]{2,1,0:T(8,128)(2,1)} %talkers.1), channel_id=1, replica_groups=mesh['z'=8,'x'=4,'y'=4,'c'=2] {'z','x','y'}, dimensions={0} | all-to-all | bytes 524288 | tf_op jit(solution)/shard_map/all_to_all | solution.py:289
  150.0 1.8 %settle.1 = bf16[16,1024]{1,0:T(8,128)(2,1)} custom-call(bf16[128,8,128]{2,1,0:T(8,128)(2,1)} %all_to_all.15.returned, s32[1,16]{1,0:T(1,128)} %bitcast.17), custom_call_target="tpu_custom_call" | custom-call | tf_op jit(solution)/shard_map/settle/pallas_call | solution.py:393
  (19 shorter events, 0.0 us)
Async XLA Ops:
  11.2 15.6 %copy-start.3 = (bf16[1,2048,384]{2,1,0:T(8,128)(2,1)S(1)}, bf16[1,2048,384]{2,1,0:T(8,128)(2,1)}, u32[]{:S(2)}) copy-start(bf16[1,2048,384]{2,1,0:T(8,128)(2,1)} %g0.2) | copy-start | bytes 4718596
  11.2 16.3 %copy-start.10 = (f32[1,16,3]{1,0,2:T(1,128)S(1)}, f32[1,16,3]{1,0,2:T(1,128)}, u32[]{:S(2)}) copy-start(f32[1,16,3]{1,0,2:T(1,128)} %param.32) | copy-start | bytes 580
  11.2 16.7 %copy-start.11 = (f32[1,16,3]{1,0,2:T(1,128)S(1)}, f32[1,16,3]{1,0,2:T(1,128)}, u32[]{:S(2)}) copy-start(f32[1,16,3]{1,0,2:T(1,128)} %param.34) | copy-start | bytes 580
  11.2 23.7 %copy-start.12 = (f32[1,3,16]{2,0,1:T(1,128)S(1)}, f32[1,3,16]{2,0,1:T(1,128)}, u32[]{:S(2)}) copy-start(f32[1,3,16]{2,0,1:T(1,128)} %param.36) | copy-start | bytes 580
  11.2 51.8 %all-to-all-start = ((bf16[128,40,128]{2,1,0:T(8,128)(2,1)}), bf16[128,40,128]{2,1,0:T(8,128)(2,1)S(1)}, u32[]{:S(2)}, u32[]{:S(2)}) async-start(bf16[128,40,128]{2,1,0:T(8,128)(2,1)} %get-tuple-element.14), calls=%async_computation | async-start | bytes 2621440 | tf_op jit(solution)/shard_map/all_to_all | solution.py:289
  26.8 9.3 %collective-permute-start.3 = (bf16[1,2048,384]{2,1,0:T(8,128)(2,1)S(1)}, bf16[1,2048,384]{2,1,0:T(8,128)(2,1)S(1)}, u32[]{:S(2)}, u32[]{:S(2)}) collective-permute-start(bf16[1,2048,384]{2,1,0:T(8,128)(2,1)S(1)} %copy-done.3), channel_id=1, source_target_pairs={{0,1},{1,0},{2,3},{3,2},{4,5},{5,4},{6,7},{7,6},{8,9},{9,8},{10,11... | collective-permute-start | bytes 4718600 | tf_op jit(solution)/shard_map/ppermute | solution.py:285
  26.9 10.3 %collective-permute-start.4 = (bf16[1,2048,384]{2,1,0:T(8,128)(2,1)}, bf16[1,2048,384]{2,1,0:T(8,128)(2,1)S(1)}, u32[]{:S(2)}, u32[]{:S(2)}) collective-permute-start(bf16[1,2048,384]{2,1,0:T(8,128)(2,1)} %u0.2), channel_id=1, source_target_pairs={{0,1},{1,0},{2,3},{3,2},{4,5},{5,4},{6,7},{7,6},{8,9},{9,8},{10,11... | collective-permute-start | bytes 4718600 | tf_op jit(solution)/shard_map/ppermute | solution.py:285
  27.4 11.1 %collective-permute-start.5 = (bf16[1,384,2048]{2,1,0:T(8,128)(2,1)}, bf16[1,384,2048]{2,1,0:T(8,128)(2,1)}, u32[]{:S(2)}, u32[]{:S(2)}) collective-permute-start(bf16[1,384,2048]{2,1,0:T(8,128)(2,1)} %d0.2), channel_id=1, source_target_pairs={{0,1},{1,0},{2,3},{3,2},{4,5},{5,4},{6,7},{7,6},{8,9},{9,8},{10,11... | collective-permute-start | bytes 4718600 | tf_op jit(solution)/shard_map/ppermute | solution.py:285
  27.5 7.4 %collective-permute-start = (f32[3,1,16]{2,1,0:T(1,128)S(1)}, f32[3,1,16]{2,1,0:T(1,128)S(1)}, u32[]{:S(2)}, u32[]{:S(2)}) collective-permute-start(f32[3,1,16]{2,1,0:T(1,128)S(1)} %bitcast.19), channel_id=1, source_target_pairs={{0,1},{1,0},{2,3},{3,2},{4,5},{5,4},{6,7},{7,6},{8,9},{9,8},{10,11... | collective-permute-start | bytes 584 | tf_op jit(solution)/shard_map/ppermute | solution.py:285
  27.9 7.2 %collective-permute-start.1 = (f32[3,1,16]{2,1,0:T(1,128)S(1)}, f32[3,1,16]{2,1,0:T(1,128)S(1)}, u32[]{:S(2)}, u32[]{:S(2)}) collective-permute-start(f32[3,1,16]{2,1,0:T(1,128)S(1)} %bitcast.21), channel_id=1, source_target_pairs={{0,1},{1,0},{2,3},{3,2},{4,5},{5,4},{6,7},{7,6},{8,9},{9,8},{10,11... | collective-permute-start | bytes 584 | tf_op jit(solution)/shard_map/ppermute | solution.py:285
  34.9 3.5 %copy-start.13 = (f32[3,1,16]{2,1,0:T(1,128)}, f32[3,1,16]{2,1,0:T(1,128)S(1)}, u32[]{:S(2)}) copy-start(f32[3,1,16]{2,1,0:T(1,128)S(1)} %collective-permute-done.gs1) | copy-start | bytes 580
  34.9 1.2 collective-permute-start.2
  35.1 3.4 %copy-start.14 = (f32[3,1,16]{2,1,0:T(1,128)}, f32[3,1,16]{2,1,0:T(1,128)S(1)}, u32[]{:S(2)}) copy-start(f32[3,1,16]{2,1,0:T(1,128)S(1)} %collective-permute-done.1.us1) | copy-start | bytes 580
  36.1 2.4 %copy-start.15 = (f32[3,1,16]{2,1,0:T(1,128)}, f32[3,1,16]{2,1,0:T(1,128)S(1)}, u32[]{:S(2)}) copy-start(f32[3,1,16]{2,1,0:T(1,128)S(1)} %collective-permute-done.2.ds1) | copy-start | bytes 580
  36.1 1.1 copy-start.4
  37.2 1.2 copy-start.5
  63.1 1.1 copy-start
  64.1 16.5 %copy-start.6 = (bf16[1,384,1024]{2,1,0:T(8,128)(2,1)S(1)}, bf16[1,384,1024]{2,1,0:T(8,128)(2,1)}, u32[]{:S(2)}) copy-start(bf16[1,384,1024]{2,1,0:T(8,128)(2,1)} %d0.3) | copy-start | bytes 2359300
  72.9 7.2 %copy-start.2 = (bf16[1,2048,384]{2,1,0:T(8,128)(2,1)S(1)}, bf16[1,2048,384]{2,1,0:T(8,128)(2,1)}, u32[]{:S(2)}) copy-start(bf16[1,2048,384]{2,1,0:T(8,128)(2,1)} %g0.3) | copy-start | bytes 4718596
  72.9 37.2 %all-to-all-start.1 = ((bf16[128,32,128]{2,1,0:T(8,128)(2,1)}), bf16[128,32,128]{2,1,0:T(8,128)(2,1)S(1)}, u32[]{:S(2)}, u32[]{:S(2)}) async-start(bf16[128,32,128]{2,1,0:T(8,128)(2,1)} %get-tuple-element.18), calls=%async_computation.1 | async-start | bytes 2097152 | tf_op jit(solution)/shard_map/all_to_all | solution.py:289
  80.0 38.4 %collective-permute-start.10 = (bf16[1,2048,384]{2,1,0:T(8,128)(2,1)}, bf16[1,2048,384]{2,1,0:T(8,128)(2,1)}, u32[]{:S(2)}, u32[]{:S(2)}) collective-permute-start(bf16[1,2048,384]{2,1,0:T(8,128)(2,1)} %u0.3), channel_id=1, source_target_pairs={{0,1},{1,0},{2,3},{3,2},{4,5},{5,4},{6,7},{7,6},{8,9},{9,8},{10,11... | collective-permute-start | bytes 4718600 | tf_op jit(solution)/shard_map/ppermute | solution.py:285
  80.1 38.3 %collective-permute-start.9 = (bf16[1,2048,384]{2,1,0:T(8,128)(2,1)S(1)}, bf16[1,2048,384]{2,1,0:T(8,128)(2,1)}, u32[]{:S(2)}, u32[]{:S(2)}) collective-permute-start(bf16[1,2048,384]{2,1,0:T(8,128)(2,1)S(1)} %copy-done.2), channel_id=1, source_target_pairs={{0,1},{1,0},{2,3},{3,2},{4,5},{5,4},{6,7},{7,6},{8,9},{9,8},{10,11... | collective-permute-start | bytes 4718600 | tf_op jit(solution)/shard_map/ppermute | solution.py:285
  80.6 36.1 %collective-permute-start.11 = (bf16[1,384,1024]{2,1,0:T(8,128)(2,1)S(1)}, bf16[1,384,1024]{2,1,0:T(8,128)(2,1)}, u32[]{:S(2)}, u32[]{:S(2)}) collective-permute-start(bf16[1,384,1024]{2,1,0:T(8,128)(2,1)S(1)} %copy-done.6), channel_id=1, source_target_pairs={{0,1},{1,0},{2,3},{3,2},{4,5},{5,4},{6,7},{7,6},{8,9},{9,8},{10,11... | collective-permute-start | bytes 2359304 | tf_op jit(solution)/shard_map/ppermute | solution.py:285
  110.2 1.0 copy-start.1
  115.2 5.8 %collective-permute-start.6 = (bf16[16,2304]{1,0:T(8,128)(2,1)}, bf16[16,2304]{1,0:T(8,128)(2,1)S(1)}, u32[]{:S(2)}, u32[]{:S(2)}) collective-permute-start(bf16[16,2304]{1,0:T(8,128)(2,1)} %get-tuple-element.22.m0), channel_id=1, source_target_pairs={{0,2},{2,4},{4,6},{6,0},{1,3},{3,5},{5,7},{7,1},{8,10},{10,12},{12... | collective-permute-start | bytes 221192 | tf_op jit(solution)/shard_map/ppermute | solution.py:374
  115.7 6.1 %collective-permute-start.7 = (bf16[16,2304]{1,0:T(8,128)(2,1)}, bf16[16,2304]{1,0:T(8,128)(2,1)S(1)}, u32[]{:S(2)}, u32[]{:S(2)}) collective-permute-start(bf16[16,2304]{1,0:T(8,128)(2,1)} %get-tuple-element.22.m0), channel_id=1, source_target_pairs={{0,4},{2,6},{4,0},{6,2},{1,5},{3,7},{5,1},{7,3},{8,12},{10,14},{12... | collective-permute-start | bytes 221192 | tf_op jit(solution)/shard_map/ppermute | solution.py:374
  116.7 5.9 %collective-permute-start.8 = (bf16[16,2304]{1,0:T(8,128)(2,1)}, bf16[16,2304]{1,0:T(8,128)(2,1)S(1)}, u32[]{:S(2)}, u32[]{:S(2)}) collective-permute-start(bf16[16,2304]{1,0:T(8,128)(2,1)} %get-tuple-element.22.m0), channel_id=1, source_target_pairs={{0,6},{2,0},{4,2},{6,4},{1,7},{3,1},{5,3},{7,5},{8,14},{10,8},{12,... | collective-permute-start | bytes 221192 | tf_op jit(solution)/shard_map/ppermute | solution.py:374
  120.9 1.7 %copy-start.7 = (bf16[16,2304]{1,0:T(8,128)(2,1)}, bf16[16,2304]{1,0:T(8,128)(2,1)S(1)}, u32[]{:S(2)}) copy-start(bf16[16,2304]{1,0:T(8,128)(2,1)S(1)} %collective-permute-done.6.m1) | copy-start | bytes 221188
  121.8 0.8 copy-start.8
  122.6 0.6 copy-start.9
where the time goes:
time: 153 us; the launch traced here: 152 us
  waiting for transfers between devices  53.6 us (35%)
  Pallas kernels  43.3 us (28%)
  starting transfers between devices  27.9 us (18%)
  blocking collectives  21.1 us (14%)
  local copies, waits for them, and re-layouts  5.04 us (3%)
    all_to_all x2, waiting for transfers between devices, spread_chips(): return lax.all_to_all(value, ('z', 'x', 'y'), 0, 0, tiled=True)  41.5 us
    all_to_all x2, starting transfers between devices, spread_chips(): return lax.all_to_all(value, ('z', 'x', 'y'), 0, 0, tiled=True)  22.7 us
    all_to_all x1, blocking collectives, spread_chips(): return lax.all_to_all(value, ('z', 'x', 'y'), 0, 0, tiled=True)  21.1 us
    pallas_call x1, Pallas kernels, local(): pl.pallas_call(restore_kernel, grid=(D // BLK,), out_shape=(sds((D, 2 * F...  12.5 us
    pallas_call x1, Pallas kernels, local(): pl.pallas_call(attend_kernel, out_shape=(sds((ROWS, D), f32), sds((CHIPS,...  10.5 us
    pallas_call x1, Pallas kernels, local(): pl.pallas_call(expert_kernel, out_shape=(sds((CHIPS, 32, LANES), bf16), s...  8.81 us
    ppermute x9, waiting for transfers between devices, swap(): return lax.ppermute(value, 'c', [(0, 1), (1, 0)])  7.95 us
    pallas_call x1, Pallas kernels, local(): pl.pallas_call(talker_kernel, out_shape=sds((CHIPS, 8, LANES), bf16), in_...  5.69 us
  transfers between devices with their start and end apart: 14, of which 7 were waited for; matrix products, arithmetic and copies ran while one was open for 0% of the time, Pallas kernels for 11%

commit v1 on v0

v1 whole, which is shorter than its diff:
```python
import jax
import jax.numpy as jnp
from jax import lax
from jax.experimental import pallas as pl
from jax.experimental.pallas import tpu as pltpu
from jax.sharding import Mesh
from jax.sharding import PartitionSpec as P

HEADS = 16
HEAD_DIM = 128
BLK = 128
CHIPS = 128
LANES = 128
ROWS = 16
CTX = 128
D = 2048
FH = 384
TD = 1024
EPSILON = 1e-06
WIDE = D + LANES
TWIDE = D + 2 * LANES
N_Z = 8
N_XY = 16

f32 = jnp.float32
bf16 = jnp.bfloat16
VM = pl.BlockSpec(memory_space=pltpu.VMEM)
SM = pl.BlockSpec(memory_space=pltpu.SMEM)
HB = pl.BlockSpec(memory_space=pl.ANY)


def lane_iota(rows):
    return lax.broadcasted_iota(jnp.int32, (rows, LANES), 1)


def gather_t(onehot, values):
    return lax.dot_general(
        onehot, values, (((0,), (0,)), ((), ())), preferred_element_type=f32
    )


def attend_kernel(
    hidden, queries, cache_key, cache_value, new_key, new_value, lengths, gain, ids,
    think_gates, source, talk_ids, talk_gates, residual, message, asked, mixed, keys, vals, sems,
):
    copies = []
    for i in range(4):
        part = pl.ds(i * 4, 4)
        k_copy = pltpu.make_async_copy(cache_key.at[part], keys.at[part], sems.at[i])
        v_copy = pltpu.make_async_copy(cache_value.at[part], vals.at[part], sems.at[4 + i])
        k_copy.start()
        v_copy.start()
        copies.append((k_copy, v_copy))
    scaling = HEAD_DIM ** (-0.5)
    for h in range(HEADS):
        asked[pl.ds(h, ROWS, stride=HEADS), :] = queries[:, h * 128 : (h + 1) * 128].astype(f32)
    head = lax.broadcasted_iota(jnp.int32, (HEADS, LANES), 0)
    front = head < HEADS // 2
    lane = lane_iota(HEADS)
    fresh_key = new_key[...].astype(f32)
    fresh_value = new_value[...].astype(f32)
    for r in range(ROWS):
        if r % 4 == 0:
            copies[r // 4][0].wait()
            copies[r // 4][1].wait()
        query = asked[r * HEADS : (r + 1) * HEADS, :]
        split = jnp.concatenate(
            [jnp.where(front, query, 0.0), jnp.where(front, 0.0, query)], axis=1
        ).astype(bf16)
        scores = (
            lax.dot_general(
                split, keys[r], (((1,), (1,)), ((), ())), preferred_element_type=f32
            )
            * scaling
        )
        own_key = jnp.where(front, fresh_key[r : r + 1, :128], fresh_key[r : r + 1, 128:])
        own_val = jnp.where(front, fresh_value[r : r + 1, :128], fresh_value[r : r + 1, 128:])
        fresh = jnp.sum(query * own_key, axis=1, keepdims=True) * scaling
        scores = jnp.where(lane < lengths[r], scores, -jnp.inf)
        highest = jnp.maximum(jnp.max(scores, axis=1, keepdims=True), fresh)
        weights = jnp.exp(scores - highest)
        own = jnp.exp(fresh - highest)
        total = jnp.sum(weights, axis=1, keepdims=True) + own
        probs = (weights / total).astype(bf16)
        own_prob = (own / total).astype(bf16).astype(f32)
        both = jnp.dot(probs, vals[r], preferred_element_type=f32)
        mixed[r * HEADS : (r + 1) * HEADS, :] = (
            jnp.where(front, both[:, :128], both[:, 128:]) + own_prob * own_val
        )
    squares = jnp.zeros((ROWS, LANES), f32)
    for h in range(HEADS):
        cols = slice(h * 128, (h + 1) * 128)
        part = hidden[:, cols].astype(f32) + mixed[pl.ds(h, ROWS, stride=HEADS), :]
        residual[:, cols] = part
        squares = squares + part * part
    spread = jnp.sum(squares, axis=1, keepdims=True) * (1.0 / D)
    scale = lax.rsqrt(spread + EPSILON)
    for h in range(HEADS):
        cols = slice(h * 128, (h + 1) * 128)
        normed = (residual[:, cols] * scale * gain[h : h + 1, :].astype(f32)).astype(bf16)
        for z in range(N_Z):
            message[z, :, cols] = normed
    origin = source[...]
    fact = lax.broadcasted_iota(jnp.int32, (40, ROWS), 0)
    gates = talk_gates[...]
    high = gates.astype(bf16).astype(f32)
    low = gates - high
    facts = jnp.where(fact == 16 + origin % ROWS, 1.0, 0.0)
    facts = facts + jnp.where(fact == 32, (origin // 32).astype(f32), 0.0)
    for k in range(2):
        chosen = talk_ids[k : k + 1, :]
        facts = facts + jnp.where(fact == chosen, high[k : k + 1, :], 0.0)
        facts = facts + jnp.where(fact == chosen + 8, low[k : k + 1, :], 0.0)
    weights = think_gates[...]
    high = weights.astype(bf16).astype(f32)
    low = weights - high
    upright = jnp.concatenate(
        [facts, ids[...].astype(f32), high, low, jnp.zeros((64, ROWS), f32)], axis=0
    ).astype(bf16)
    same = lax.broadcasted_iota(jnp.int32, (ROWS, ROWS), 0) == lax.broadcasted_iota(
        jnp.int32, (ROWS, ROWS), 1
    )
    told = lax.dot_general(
        jnp.where(same, 1.0, 0.0).astype(bf16), upright, (((1,), (1,)), ((), ())),
        preferred_element_type=f32,
    ).astype(bf16)
    for z in range(N_Z):
        message[z, :, D:] = told


def select_kernel(plane, gathered, message, shares):
    rows = N_Z * ROWS
    inputs = gathered[:, :, :D].reshape(rows, D)
    told = gathered[:, :, D:].reshape(rows, LANES)
    facts = told.astype(f32)
    shape = (rows, 2 * LANES)
    col = lax.broadcasted_iota(jnp.int32, shape, 1)
    row = lax.broadcasted_iota(jnp.int32, shape, 0)
    chip = (plane[0] * N_XY + col // 16).astype(f32)
    turn = (col % 16) // 8
    level = (col % 8) == (row // ROWS)
    picked = jnp.zeros(shape, f32)
    high = jnp.zeros(shape, f32)
    low = jnp.zeros(shape, f32)
    for k in range(8):
        match = level & (facts[:, 40 + k : 41 + k] == chip)
        picked = jnp.where(match, 1.0, picked)
        high = jnp.where(match, facts[:, 48 + k : 49 + k], high)
        low = jnp.where(match, facts[:, 56 + k : 57 + k], low)
    below = lax.broadcasted_iota(jnp.int32, (rows, rows), 1) < lax.broadcasted_iota(
        jnp.int32, (rows, rows), 0
    )
    rank = jnp.dot(
        jnp.where(below, 1.0, 0.0).astype(bf16), picked.astype(bf16), preferred_element_type=f32
    )
    chosen = (picked > 0.5) & (jnp.abs(rank - turn.astype(f32)) < 0.5)
    onehot = jnp.where(chosen, 1.0, 0.0).astype(bf16)
    shares[:rows, :] = jnp.where(chosen, high, 0.0).astype(bf16)
    shares[rows:, :] = jnp.where(chosen, low, 0.0).astype(bf16)
    message[:, :, :D] = gather_t(onehot, inputs).astype(bf16).reshape(N_XY, 16, D)
    owned = level & (turn == 0) & (facts[:, 32:33] == chip)
    message[:, :, D:] = (
        gather_t(jnp.where(owned, 1.0, 0.0).astype(bf16), told)
        .astype(bf16)
        .reshape(N_XY, 16, LANES)
    )


def silu(x):
    return x * jax.nn.sigmoid(x)


def restore_kernel(gs0, us0, ds0, gs1, us1, ds1, g0, u0, d0, g1, u1, d1, gw, uw, dw):
    i = pl.program_id(0)
    for half, (gs, us, ds, g, u, d) in enumerate(
        [(gs0, us0, ds0, g0, u0, d0), (gs1, us1, ds1, g1, u1, d1)]
    ):
        for j in range(FH // BLK):
            cols = slice(j * BLK, (j + 1) * BLK)
            there = slice(half * FH + j * BLK, half * FH + (j + 1) * BLK)
            for k in range(2):
                near = slice(k * BLK, (k + 1) * BLK)
                at = 2 * i + k
                gw[near, there] = (g[0, near, cols].astype(f32) * gs[j, 0, at]).astype(bf16)
                uw[near, there] = (u[0, near, cols].astype(f32) * us[j, 0, at]).astype(bf16)
                dw[there, near] = (d[0, cols, near].astype(f32) * ds[j, 0, at]).astype(bf16)


def expert_kernel(arrived, g, u, d, produced, rows_in, gw, uw, dw, sems):
    copies = []
    for i, (src, dst) in enumerate(
        [(arrived.at[:, :, pl.ds(0, D)], rows_in), (g, gw), (u, uw), (d, dw)]
    ):
        copy = pltpu.make_async_copy(src, dst, sems.at[i])
        copy.start()
        copies.append(copy)
    copies[0].wait()
    inputs = rows_in[...].reshape(2 * CHIPS, D)
    copies[1].wait()
    gated = jnp.dot(inputs, gw[...], preferred_element_type=f32)
    copies[2].wait()
    lifted = jnp.dot(inputs, uw[...], preferred_element_type=f32)
    middle = (silu(gated) * lifted).astype(bf16)
    copies[3].wait()
    for h in range(HEADS // 2):
        cols = slice(h * 256, (h + 1) * 256)
        part = jnp.dot(middle, dw[:, cols], preferred_element_type=f32)
        produced[:, :, cols] = part.astype(bf16).reshape(N_XY, 16, 256)


def partial_kernel(returned, shares, partial):
    both = jnp.dot(
        shares[...], returned[...].reshape(2 * CHIPS, D), preferred_element_type=f32
    )
    partial[...] = (both[:CHIPS] + both[CHIPS:]).astype(bf16).reshape(N_Z, ROWS, D)


def combine_kernel(collected, residual, owned, gain, thinker_out, onward):
    routed = residual[...]
    for z in range(N_Z):
        routed = routed + collected[z].astype(f32)
    outcome = routed.astype(bf16)
    thinker_out[...] = outcome
    values = outcome.astype(f32)
    spread = jnp.sum(values * values, axis=1, keepdims=True) * (1.0 / D)
    scale = lax.rsqrt(spread + EPSILON)
    for h in range(HEADS):
        cols = slice(h * 128, (h + 1) * 128)
        onward[:, cols] = (values[:, cols] * scale * gain[h : h + 1, :].astype(f32)).astype(bf16)
    told = owned[...].astype(f32)[:, :8, :].reshape(CHIPS, LANES).astype(bf16)
    pick = jnp.where(
        lane_iota(ROWS) == 16 + lax.broadcasted_iota(jnp.int32, (ROWS, LANES), 0), 1.0, 0.0
    ).astype(bf16)
    goal = lax.dot_general(
        pick, told, (((1,), (1,)), ((), ())), preferred_element_type=f32
    ).astype(bf16)
    onward[:, D : D + LANES] = goal
    onward[:, D + LANES :] = jnp.dot(goal, told, preferred_element_type=f32).astype(bf16)


def talker_kernel(
    place, m0, m1, m2, m3, g0, u0, d0, g1, u1, d1, relayed, rows_in, gw, uw, dw, sems,
):
    copies = []
    for i, (src, dst) in enumerate(
        [
            (g0, gw.at[0]), (u0, uw.at[0]), (d0, dw.at[0]),
            (g1, gw.at[1]), (u1, uw.at[1]), (d1, dw.at[1]),
        ]
    ):
        copy = pltpu.make_async_copy(src.at[0], dst, sems.at[i])
        copy.start()
        copies.append(copy)
    for i, m in enumerate([m0, m1, m2, m3]):
        rows_in[i * ROWS : (i + 1) * ROWS, :] = m[...]
    inputs = rows_in[:, :D]
    goal = rows_in[:, D : D + LANES]
    shares = rows_in[:, D + LANES :].astype(f32)
    lane = lane_iota(4 * ROWS)
    total = jnp.zeros((4 * ROWS, TD), f32)
    for half in range(2):
        expert = place[0] if half == 0 else place[0] + 1 - 2 * (place[0] % 2)
        share = jnp.sum(
            jnp.where((lane == expert) | (lane == expert + 8), shares, 0.0), axis=1, keepdims=True
        )
        copies[3 * half].wait()
        gated = jnp.dot(inputs, gw[half], preferred_element_type=f32)
        copies[3 * half + 1].wait()
        lifted = jnp.dot(inputs, uw[half], preferred_element_type=f32)
        middle = (silu(gated) * lifted).astype(bf16)
        copies[3 * half + 2].wait()
        part = jnp.dot(middle, dw[half], preferred_element_type=f32)
        total = total + share * part.astype(bf16).astype(f32)
    relayed[...] = gather_t(goal, total.astype(bf16)).astype(bf16).reshape(N_XY, 8, TD)


def cross_kernel(returned, relayed):
    line = lax.broadcasted_iota(jnp.int32, (64, CHIPS), 0)
    came = lax.broadcasted_iota(jnp.int32, (64, CHIPS), 1)
    pick = ((line // 8) == (came % 8)) & ((line % 8) == (came // 32))
    out = jnp.dot(
        jnp.where(pick, 1.0, 0.0).astype(bf16), returned[...].reshape(CHIPS, TD),
        preferred_element_type=f32,
    )
    relayed[...] = out.astype(bf16).reshape(N_Z, 8, TD)


def settle_kernel(returned, source, talker_out):
    line = lax.broadcasted_iota(jnp.int32, (64, ROWS), 0)
    wide = source[...] // 128
    pick = ((line // 8) == (wide // 4)) & ((line % 8) == (wide % 4))
    talker_out[...] = gather_t(
        jnp.where(pick, 1.0, 0.0).astype(bf16), returned[...].reshape(64, TD)
    ).astype(bf16)


def sds(shape, dtype):
    return jax.ShapeDtypeStruct(shape, dtype)


def swap(value):
    return lax.ppermute(value, "c", [(0, 1), (1, 0)])


def exchange(value, axes):
    return lax.all_to_all(value, axes, 0, 0, tiled=True)


SMALL = pltpu.CompilerParams(vmem_limit_bytes=24 << 20)


def local(
    hidden_in, queries, cache_key, cache_value, new_key, new_value, lengths, norm_gain,
    gate_codes, gate_scale, up_codes, up_scale, down_codes, down_scale, think_ids, think_gates,
    talker_source, talker_gain, talk_gate_w, talk_up_w, talk_down_w, talk_ids, talk_gates,
):
    own = (gate_codes, up_codes, down_codes)
    own_scale = (
        jnp.transpose(gate_scale, (2, 0, 1)),
        jnp.transpose(up_scale, (2, 0, 1)),
        jnp.transpose(down_scale, (1, 0, 2)),
    )
    other = tuple(swap(w) for w in own)
    other_scale = tuple(swap(s) for s in own_scale)
    source = talker_source.reshape(1, ROWS)

    residual, message = pl.pallas_call(
        attend_kernel,
        out_shape=(sds((ROWS, D), f32), sds((N_Z, ROWS, WIDE), bf16)),
        in_specs=[VM] * 2 + [HB] * 2 + [VM] * 2 + [SM] + [VM] * 6,
        out_specs=(VM, VM),
        scratch_shapes=[
            pltpu.VMEM((ROWS * HEADS, LANES), f32),
            pltpu.VMEM((ROWS * HEADS, LANES), f32),
            pltpu.VMEM((ROWS, CTX, 256), bf16),
            pltpu.VMEM((ROWS, CTX, 256), bf16),
            pltpu.SemaphoreType.DMA((8,)),
        ],
        name="attend",
    )(
        hidden_in, queries, cache_key, cache_value, new_key, new_value, lengths,
        norm_gain.reshape(HEADS, LANES), think_ids.T, think_gates.T, source,
        talk_ids.T, talk_gates.T,
    )
    gathered = exchange(message, "z")
    plane = lax.axis_index("z").astype(jnp.int32).reshape(1)
    chosen, shares = pl.pallas_call(
        select_kernel,
        out_shape=(sds((N_XY, 16, WIDE), bf16), sds((2 * CHIPS, 2 * LANES), bf16)),
        in_specs=[SM, VM],
        out_specs=(VM, VM),
        compiler_params=SMALL,
        name="select",
    )(plane, gathered)
    arrived = exchange(chosen, ("x", "y"))
    tall = pl.BlockSpec((1, 2 * BLK, FH), lambda i: (0, i, 0))
    flat = pl.BlockSpec((1, FH, 2 * BLK), lambda i: (0, 0, i))
    tall_out = pl.BlockSpec((2 * BLK, 2 * FH), lambda i: (i, 0))
    flat_out = pl.BlockSpec((2 * FH, 2 * BLK), lambda i: (0, i))
    dense = pl.pallas_call(
        restore_kernel,
        grid=(D // BLK // 2,),
        out_shape=(sds((D, 2 * FH), bf16), sds((D, 2 * FH), bf16), sds((2 * FH, D), bf16)),
        in_specs=[SM] * 6 + [tall, tall, flat] * 2,
        out_specs=(tall_out, tall_out, flat_out),
        cost_estimate=pl.CostEstimate(
            flops=6 * D * FH, bytes_accessed=24 * D * FH, transcendentals=0
        ),
        name="restore",
    )(*own_scale, *other_scale, *own, *other)
    produced = pl.pallas_call(
        expert_kernel,
        out_shape=sds((N_XY, 16, D), bf16),
        in_specs=[HB] * 4,
        out_specs=VM,
        scratch_shapes=[
            pltpu.VMEM((N_XY, 16, D), bf16),
            pltpu.VMEM((D, 2 * FH), bf16),
            pltpu.VMEM((D, 2 * FH), bf16),
            pltpu.VMEM((2 * FH, D), bf16),
            pltpu.SemaphoreType.DMA((4,)),
        ],
        name="experts",
    )(arrived, *dense)
    returned = exchange(produced, ("x", "y"))
    partial = pl.pallas_call(
        partial_kernel,
        out_shape=sds((N_Z, ROWS, D), bf16),
        in_specs=[VM, VM],
        out_specs=VM,
        compiler_params=SMALL,
        name="partial",
    )(returned, shares)
    collected = exchange(partial, "z")
    talk_own = (talk_gate_w, talk_up_w, talk_down_w)
    talk_held = lax.optimization_barrier((*talk_own, arrived))[:3]
    talk_other = tuple(swap(w) for w in talk_held)
    thinker_out, onward = pl.pallas_call(
        combine_kernel,
        grid=(1,),
        out_shape=(sds((ROWS, D), bf16), sds((ROWS, TWIDE), bf16)),
        in_specs=[
            pl.BlockSpec((N_Z, ROWS, D), lambda i: (0, 0, 0)),
            pl.BlockSpec((ROWS, D), lambda i: (0, 0)),
            pl.BlockSpec((N_XY, 16, LANES), lambda i: (0, 0, D // LANES)),
            pl.BlockSpec((HEADS, LANES), lambda i: (0, 0)),
        ],
        out_specs=(
            pl.BlockSpec((ROWS, D), lambda i: (0, 0)),
            pl.BlockSpec((ROWS, TWIDE), lambda i: (0, 0)),
        ),
        name="combine",
    )(collected, residual, arrived, talker_gain.reshape(HEADS, LANES))
    peers = [
        lax.ppermute(onward, "y", [(i, (i + o) % 4) for i in range(4)]) for o in (1, 2, 3)
    ]
    place = (lax.axis_index("y") * 2 + lax.axis_index("c")).astype(jnp.int32).reshape(1)
    relayed = pl.pallas_call(
        talker_kernel,
        out_shape=sds((N_XY, 8, TD), bf16),
        in_specs=[SM] + [VM] * 4 + [HB] * 6,
        out_specs=VM,
        scratch_shapes=[
            pltpu.VMEM((4 * ROWS, TWIDE), bf16),
            pltpu.VMEM((2, D, FH), bf16),
            pltpu.VMEM((2, D, FH), bf16),
            pltpu.VMEM((2, FH, TD), bf16),
            pltpu.SemaphoreType.DMA((6,)),
        ],
        name="talkers",
    )(place, onward, *peers, *talk_own, *talk_other)
    crossing = exchange(relayed, ("x", "y"))
    crossed = pl.pallas_call(
        cross_kernel,
        out_shape=sds((N_Z, 8, TD), bf16),
        in_specs=[VM],
        out_specs=VM,
        compiler_params=SMALL,
        name="cross",
    )(crossing)
    settled = exchange(crossed, "z")
    talker_out = pl.pallas_call(
        settle_kernel,
        out_shape=sds((ROWS, TD), bf16),
        in_specs=[VM, VM],
        out_specs=VM,
        compiler_params=SMALL,
        name="settle",
    )(settled, source)
    return (thinker_out, talker_out)


def solution(mesh):
    fine = Mesh(mesh.devices.reshape(8, 4, 4, 2), ("z", "x", "y", "c"))
    every = ("z", "x", "y", "c")
    two = P(every, None)
    three = P(every, None, None)
    talk = P(("y", "c"), None, None)
    return jax.shard_map(
        local,
        mesh=fine,
        in_specs=(
            two, two, three, three, two, two, P(every), P(),
            three, three, three, three, three, three, two, two,
            P(every), P(), talk, talk, talk, two, two,
        ),
        out_specs=(two, two),
        check_vma=False,
    )
```

time: 153 us -> 154 us (level)
  the two profiles are of different devices: /device:TPU:2 before, /device:TPU:8 now
where the time goes in v1:
time: 154 us; the launch traced here: 153 us
  waiting for transfers between devices  56.7 us (37%)
  Pallas kernels  37.1 us (24%)
  starting transfers between devices  30.2 us (20%)
  blocking collectives  25.1 us (16%)
  local copies, waits for them, and re-layouts  3.04 us (2%)
    all_to_all x4, waiting for transfers between devices, exchange(): return lax.all_to_all(value, axes, 0, 0, tiled=True)  50.7 us
    all_to_all x2, blocking collectives, exchange(): return lax.all_to_all(value, axes, 0, 0, tiled=True)  25.1 us
    all_to_all x4, starting transfers between devices, exchange(): return lax.all_to_all(value, axes, 0, 0, tiled=True)  24.4 us
    pallas_call x1, Pallas kernels, local(): pl.pallas_call(restore_kernel, grid=(D // BLK // 2,), out_shape=(sds((D,...  9.84 us
    pallas_call x1, Pallas kernels, local(): pl.pallas_call(attend_kernel, out_shape=(sds((ROWS, D), f32), sds((N_Z, R...  8.66 us
    pallas_call x1, Pallas kernels, local(): pl.pallas_call(expert_kernel, out_shape=sds((N_XY, 16, D), bf16), in_spec...  6.68 us
    pallas_call x1, Pallas kernels, local(): pl.pallas_call(talker_kernel, out_shape=sds((N_XY, 8, TD), bf16), in_spec...  5.7 us
    ppermute x3, waiting for transfers between devices, local(): lax.ppermute(onward, 'y', [(i, (i + o) % 4) for i in range(4)])  4.29 us
  transfers between devices with their start and end apart: 16, of which 9 were waited for; matrix products, arithmetic and copies ran while one was open for 0% of the time, Pallas kernels for 10%

profile of v1, /device:TPU:8, one launch (start us, length us, event | category | flops | bytes accessed | tf_op | source)
XLA Modules:
  0.0 152.9 jit_solution(10643602111209062773)
XLA Ops:
  0.6 0.0 copy-start.4
  0.6 8.7 %attend.1 = (f32[16,2048]{1,0:T(8,128)}, bf16[8,16,2176]{2,1,0:T(8,128)(2,1)}) custom-call(bf16[16,2048]{1,0:T(8,128)(2,1)} %hidden.1, bf16[16,2048]{1,0:T(8,128)(2,1)} %queries.1, bf16[16,128,256]{2,1,0:T(8,128)(2,1)} %cache_key.1, bf16[16,128,256]{2,1,0:T(8,128)(2,1)} %cache_value.1, bf16[16,256]{1,0:T(8,128)(2,1)} %new_key.1, bf16[16,256]{1,0:T(8,128)(2,1)} %new_value.1, ...), custom_call_target="tpu_custom_call" | custom-call | tf_op jit(solution)/shard_map/attend/pallas_call | solution.py:327
  9.3 8.5 %all-to-all-start = ((bf16[8,16,2176]{2,1,0:T(8,128)(2,1)}), bf16[8,16,2176]{2,1,0:T(8,128)(2,1)S(1)}, u32[]{:S(2)}, u32[]{:S(2)}) async-start(bf16[8,16,2176]{2,1,0:T(8,128)(2,1)} %get-tuple-element.14), calls=%async_computation | async-start | bytes 1114112 | tf_op jit(solution)/shard_map/all_to_all | solution.py:306
  17.8 0.0 copy-start.9
  17.8 0.0 copy-start.10
  17.8 0.0 copy-start.11
  17.8 0.1 collective-permute-start.3
  17.9 0.5 collective-permute-start.4
  18.4 0.1 collective-permute-start.5
  18.5 17.5 %all-to-all-done.gathered = bf16[8,16,2176]{2,1,0:T(8,128)(2,1)S(1)} async-done(((bf16[8,16,2176]{2,1,0:T(8,128)(2,1)}), bf16[8,16,2176]{2,1,0:T(8,128)(2,1)S(1)}, u32[]{:S(2)}, u32[]{:S(2)}) %all-to-all-start) | async-done | bytes 557088 | tf_op jit(solution)/shard_map/all_to_all | solution.py:306
  36.0 2.0 %select.1 = (bf16[16,16,2176]{2,1,0:T(8,128)(2,1)}, bf16[256,256]{1,0:T(8,128)(2,1)S(1)}) custom-call(s32[1]{0:T(128)} %bitcast.plane, bf16[8,16,2176]{2,1,0:T(8,128)(2,1)S(1)} %all-to-all-done.gathered), custom_call_target="tpu_custom_call" | custom-call | tf_op jit(solution)/shard_map/select/pallas_call | solution.py:347
  38.0 7.4 %all-to-all-start.1 = ((bf16[16,16,2176]{2,1,0:T(8,128)(2,1)}), bf16[16,16,2176]{2,1,0:T(8,128)(2,1)S(1)}, u32[]{:S(2)}, u32[]{:S(2)}) async-start(bf16[16,16,2176]{2,1,0:T(8,128)(2,1)} %get-tuple-element.15), calls=%async_computation.1 | async-start | bytes 2228224 | tf_op jit(solution)/shard_map/all_to_all | solution.py:306
  45.4 0.1 collective-permute-start
  45.5 0.5 collective-permute-start.1
  46.0 0.6 collective-permute-done.gs1
  46.7 0.2 collective-permute-start.2
  46.8 0.0 collective-permute-done.1.us1
  46.8 1.0 collective-permute-done.2.ds1
  47.8 0.0 collective-permute-done.3.g1
  47.8 0.0 collective-permute-done.4.u1
  47.9 0.6 copy-done.14
  48.4 9.8 %restore.1 = (bf16[2048,768]{1,0:T(8,128)(2,1)}, bf16[2048,768]{1,0:T(8,128)(2,1)}, bf16[768,2048]{1,0:T(8,128)(2,1)}) custom-call(f32[3,1,16]{2,1,0:T(1,128)} %bitcast.18, f32[3,1,16]{2,1,0:T(1,128)} %bitcast.20, f32[3,1,16]{2,1,0:T(1,128)} %bitcast.22, f32[3,1,16]{2,1,0:T(1,128)} %copy-done.12, f32[3,1,16]{2,1,0:T(1,128)} %copy-done.13, ...), custom_call_target="tpu_custom_call" | custom-call | flops 4718592 | bytes 18874368 | tf_op jit(solution)/shard_map/restore/pallas_call | solution.py:360
  58.3 4.5 %all-to-all-done.1.arrived.owned = bf16[16,16,2176]{2,1,0:T(8,128)(2,1)S(1)} async-done(((bf16[16,16,2176]{2,1,0:T(8,128)(2,1)}), bf16[16,16,2176]{2,1,0:T(8,128)(2,1)S(1)}, u32[]{:S(2)}, u32[]{:S(2)}) %all-to-all-start.1) | async-done | bytes 1114144 | tf_op jit(solution)/shard_map/all_to_all | solution.py:306
  62.8 1.0 copy-done.1
  63.8 6.7 %experts.1 = bf16[16,16,2048]{2,1,0:T(8,128)(2,1)} custom-call(bf16[16,16,2176]{2,1,0:T(8,128)(2,1)} %copy-done.1, bf16[2048,768]{1,0:T(8,128)(2,1)} %get-tuple-element.16.g, bf16[2048,768]{1,0:T(8,128)(2,1)} %get-tuple-element.17.u, bf16[768,2048]{1,0:T(8,128)(2,1)} %get-tuple-element.18.d), custom_call_target="tpu_custom_call" | custom-call | tf_op jit(solution)/shard_map/experts/pallas_call | solution.py:371
  70.5 0.0 copy-start.3
  70.5 5.0 %all-to-all-start.2 = ((bf16[16,16,2048]{2,1,0:T(8,128)(2,1)}), bf16[16,16,2048]{2,1,0:T(8,128)(2,1)S(1)}, u32[]{:S(2)}, u32[]{:S(2)}) async-start(bf16[16,16,2048]{2,1,0:T(8,128)(2,1)} %experts.1), calls=%async_computation.2 | async-start | bytes 2097152 | tf_op jit(solution)/shard_map/all_to_all | solution.py:306
  75.5 0.1 collective-permute-start.10
  75.6 0.5 collective-permute-start.9
  76.1 13.8 %all-to-all-done.2.returned = bf16[16,16,2048]{2,1,0:T(8,128)(2,1)S(1)} async-done(((bf16[16,16,2048]{2,1,0:T(8,128)(2,1)}), bf16[16,16,2048]{2,1,0:T(8,128)(2,1)S(1)}, u32[]{:S(2)}, u32[]{:S(2)}) %all-to-all-start.2) | async-done | bytes 1048608 | tf_op jit(solution)/shard_map/all_to_all | solution.py:306
  89.9 1.2 partial.1
  91.1 3.5 %all-to-all-start.3 = ((bf16[8,16,2048]{2,1,0:T(8,128)(2,1)}), bf16[8,16,2048]{2,1,0:T(8,128)(2,1)S(1)}, u32[]{:S(2)}, u32[]{:S(2)}) async-start(bf16[8,16,2048]{2,1,0:T(8,128)(2,1)} %partial.1), calls=%async_computation.3 | async-start | bytes 1048576 | tf_op jit(solution)/shard_map/all_to_all | solution.py:306
  94.6 0.1 collective-permute-start.11
  94.7 15.0 %all-to-all-done.3.collected = bf16[8,16,2048]{2,1,0:T(8,128)(2,1)S(1)} async-done(((bf16[8,16,2048]{2,1,0:T(8,128)(2,1)}), bf16[8,16,2048]{2,1,0:T(8,128)(2,1)S(1)}, u32[]{:S(2)}, u32[]{:S(2)}) %all-to-all-start.3) | async-done | bytes 524320 | tf_op jit(solution)/shard_map/all_to_all | solution.py:306
  109.7 0.8 copy-done.2
  110.5 2.0 %combine.1 = (bf16[16,2048]{1,0:T(8,128)(2,1)}, bf16[16,2304]{1,0:T(8,128)(2,1)}) custom-call(bf16[8,16,2048]{2,1,0:T(8,128)(2,1)} %copy-done.2, f32[16,2048]{1,0:T(8,128)} %get-tuple-element.20.residual, bf16[16,16,2176]{2,1,0:T(8,128)(2,1)} %copy-done.1, bf16[16,128]{1,0:T(8,128)(2,1)} %bitcast.17), custom_call_target="tpu_custom_call" | custom-call | tf_op jit(solution)/shard_map/combine/pallas_call | solution.py:398
  112.5 0.4 collective-permute-start.6
  112.9 3.0 %collective-permute-start.7 = (bf16[16,2304]{1,0:T(8,128)(2,1)}, bf16[16,2304]{1,0:T(8,128)(2,1)S(1)}, u32[]{:S(2)}, u32[]{:S(2)}) collective-permute-start(bf16[16,2304]{1,0:T(8,128)(2,1)} %get-tuple-element.22.m0), channel_id=1, source_target_pairs={{0,4},{2,6},{4,0},{6,2},{1,5},{3,7},{5,1},{7,3},{8,12},{10,14},{12... | collective-permute-start | bytes 221192 | tf_op jit(solution)/shard_map/ppermute | solution.py:415
  116.0 0.3 collective-permute-start.8
  116.2 0.9 collective-permute-done.6.m1
  117.1 1.9 %collective-permute-done.7.m2 = bf16[16,2304]{1,0:T(8,128)(2,1)S(1)} collective-permute-done((bf16[16,2304]{1,0:T(8,128)(2,1)}, bf16[16,2304]{1,0:T(8,128)(2,1)S(1)}, u32[]{:S(2)}, u32[]{:S(2)}) %collective-permute-start.7) | collective-permute-done | bytes 73760 | tf_op jit(solution)/shard_map/ppermute | solution.py:415
  119.0 1.5 collective-permute-done.8.m3
  120.5 0.6 copy-done.8
  121.2 5.7 %talkers.1 = bf16[16,8,1024]{2,1,0:T(8,128)(2,1)} custom-call(s32[1]{0:T(128)} %bitcast.11.place, bf16[16,2304]{1,0:T(8,128)(2,1)} %get-tuple-element.22.m0, bf16[16,2304]{1,0:T(8,128)(2,1)} %copy-done.6, bf16[16,2304]{1,0:T(8,128)(2,1)} %copy-done.7, bf16[16,2304]{1,0:T(8,128)(2,1)} %copy-done.8, bf16[1,2048,384]{2,1,0:T(8,128)(2,1)} %g0.3, ...), custom_call_target="tpu_custom_call" | custom-call | tf_op jit(solution)/shard_map/talkers/pallas_call | solution.py:418
  126.9 13.6 %all_to_all.30.returned = bf16[16,8,1024]{2,1,0:T(8,128)(2,1)S(1)} all-to-all(bf16[16,8,1024]{2,1,0:T(8,128)(2,1)} %talkers.1), channel_id=1, replica_groups=mesh['z'=8,'x'=4,'y'=4,'c'=2] {'x','y'}, dimensions={0} | all-to-all | bytes 524288 | tf_op jit(solution)/shard_map/all_to_all | solution.py:306
  140.5 0.2 cross.1
  140.7 11.5 %all_to_all.31.returned = bf16[8,8,1024]{2,1,0:T(8,128)(2,1)S(1)} all-to-all(bf16[8,8,1024]{2,1,0:T(8,128)(2,1)S(1)} %cross.1), channel_id=1, replica_groups=mesh['z'=8,'x'=4,'y'=4,'c'=2] {'z'}, dimensions={0} | all-to-all | bytes 262144 | tf_op jit(solution)/shard_map/all_to_all | solution.py:306
  152.1 0.8 settle.1
  (25 shorter events, 0.0 us)
Async XLA Ops:
  0.6 17.2 %copy-start.4 = (bf16[1,2048,384]{2,1,0:T(8,128)(2,1)S(1)}, bf16[1,2048,384]{2,1,0:T(8,128)(2,1)}, u32[]{:S(2)}) copy-start(bf16[1,2048,384]{2,1,0:T(8,128)(2,1)} %g0.2) | copy-start | bytes 4718596
  9.3 26.7 %all-to-all-start = ((bf16[8,16,2176]{2,1,0:T(8,128)(2,1)}), bf16[8,16,2176]{2,1,0:T(8,128)(2,1)S(1)}, u32[]{:S(2)}, u32[]{:S(2)}) async-start(bf16[8,16,2176]{2,1,0:T(8,128)(2,1)} %get-tuple-element.14), calls=%async_computation | async-start | bytes 1114112 | tf_op jit(solution)/shard_map/all_to_all | solution.py:306
  17.8 27.6 %copy-start.9 = (f32[1,16,3]{1,0,2:T(1,128)S(1)}, f32[1,16,3]{1,0,2:T(1,128)}, u32[]{:S(2)}) copy-start(f32[1,16,3]{1,0,2:T(1,128)} %param.32) | copy-start | bytes 580
  17.8 27.7 %copy-start.10 = (f32[1,16,3]{1,0,2:T(1,128)S(1)}, f32[1,16,3]{1,0,2:T(1,128)}, u32[]{:S(2)}) copy-start(f32[1,16,3]{1,0,2:T(1,128)} %param.34) | copy-start | bytes 580
  17.8 28.8 %copy-start.11 = (f32[1,3,16]{2,0,1:T(1,128)S(1)}, f32[1,3,16]{2,0,1:T(1,128)}, u32[]{:S(2)}) copy-start(f32[1,3,16]{2,0,1:T(1,128)} %param.36) | copy-start | bytes 580
  17.8 30.0 %collective-permute-start.3 = (bf16[1,2048,384]{2,1,0:T(8,128)(2,1)S(1)}, bf16[1,2048,384]{2,1,0:T(8,128)(2,1)}, u32[]{:S(2)}, u32[]{:S(2)}) collective-permute-start(bf16[1,2048,384]{2,1,0:T(8,128)(2,1)S(1)} %copy-done.4), channel_id=1, source_target_pairs={{0,1},{1,0},{2,3},{3,2},{4,5},{5,4},{6,7},{7,6},{8,9},{9,8},{10,11... | collective-permute-start | bytes 4718600 | tf_op jit(solution)/shard_map/ppermute | solution.py:302
  17.9 29.9 %collective-permute-start.4 = (bf16[1,2048,384]{2,1,0:T(8,128)(2,1)}, bf16[1,2048,384]{2,1,0:T(8,128)(2,1)}, u32[]{:S(2)}, u32[]{:S(2)}) collective-permute-start(bf16[1,2048,384]{2,1,0:T(8,128)(2,1)} %u0.2), channel_id=1, source_target_pairs={{0,1},{1,0},{2,3},{3,2},{4,5},{5,4},{6,7},{7,6},{8,9},{9,8},{10,11... | collective-permute-start | bytes 4718600 | tf_op jit(solution)/shard_map/ppermute | solution.py:302
  18.4 29.4 %collective-permute-start.5 = (bf16[1,384,2048]{2,1,0:T(8,128)(2,1)}, bf16[1,384,2048]{2,1,0:T(8,128)(2,1)}, u32[]{:S(2)}, u32[]{:S(2)}) collective-permute-start(bf16[1,384,2048]{2,1,0:T(8,128)(2,1)} %d0.2), channel_id=1, source_target_pairs={{0,1},{1,0},{2,3},{3,2},{4,5},{5,4},{6,7},{7,6},{8,9},{9,8},{10,11... | collective-permute-start | bytes 4718600 | tf_op jit(solution)/shard_map/ppermute | solution.py:302
  38.0 24.8 %all-to-all-start.1 = ((bf16[16,16,2176]{2,1,0:T(8,128)(2,1)}), bf16[16,16,2176]{2,1,0:T(8,128)(2,1)S(1)}, u32[]{:S(2)}, u32[]{:S(2)}) async-start(bf16[16,16,2176]{2,1,0:T(8,128)(2,1)} %get-tuple-element.15), calls=%async_computation.1 | async-start | bytes 2228224 | tf_op jit(solution)/shard_map/all_to_all | solution.py:306
  45.4 1.2 collective-permute-start
  45.5 1.3 collective-permute-start.1
  46.7 1.2 copy-start.12
  46.7 1.2 collective-permute-start.2
  46.8 1.0 copy-start.13
  47.8 0.6 copy-start.14
  62.8 1.0 copy-start.1
  70.5 5.2 %copy-start.3 = (bf16[1,2048,384]{2,1,0:T(8,128)(2,1)S(1)}, bf16[1,2048,384]{2,1,0:T(8,128)(2,1)}, u32[]{:S(2)}) copy-start(bf16[1,2048,384]{2,1,0:T(8,128)(2,1)} %g0.3) | copy-start | bytes 4718596
  70.5 19.4 %all-to-all-start.2 = ((bf16[16,16,2048]{2,1,0:T(8,128)(2,1)}), bf16[16,16,2048]{2,1,0:T(8,128)(2,1)S(1)}, u32[]{:S(2)}, u32[]{:S(2)}) async-start(bf16[16,16,2048]{2,1,0:T(8,128)(2,1)} %experts.1), calls=%async_computation.2 | async-start | bytes 2097152 | tf_op jit(solution)/shard_map/all_to_all | solution.py:306
  75.5 19.1 %copy-start.5 = (bf16[1,384,1024]{2,1,0:T(8,128)(2,1)S(1)}, bf16[1,384,1024]{2,1,0:T(8,128)(2,1)}, u32[]{:S(2)}) copy-start(bf16[1,384,1024]{2,1,0:T(8,128)(2,1)} %d0.3) | copy-start | bytes 2359300
  75.5 40.7 %collective-permute-start.10 = (bf16[1,2048,384]{2,1,0:T(8,128)(2,1)}, bf16[1,2048,384]{2,1,0:T(8,128)(2,1)}, u32[]{:S(2)}, u32[]{:S(2)}) collective-permute-start(bf16[1,2048,384]{2,1,0:T(8,128)(2,1)} %u0.3), channel_id=1, source_target_pairs={{0,1},{1,0},{2,3},{3,2},{4,5},{5,4},{6,7},{7,6},{8,9},{9,8},{10,11... | collective-permute-start | bytes 4718600 | tf_op jit(solution)/shard_map/ppermute | solution.py:302
  75.6 40.6 %collective-permute-start.9 = (bf16[1,2048,384]{2,1,0:T(8,128)(2,1)S(1)}, bf16[1,2048,384]{2,1,0:T(8,128)(2,1)}, u32[]{:S(2)}, u32[]{:S(2)}) collective-permute-start(bf16[1,2048,384]{2,1,0:T(8,128)(2,1)S(1)} %copy-done.3), channel_id=1, source_target_pairs={{0,1},{1,0},{2,3},{3,2},{4,5},{5,4},{6,7},{7,6},{8,9},{9,8},{10,11... | collective-permute-start | bytes 4718600 | tf_op jit(solution)/shard_map/ppermute | solution.py:302
  91.1 18.6 %all-to-all-start.3 = ((bf16[8,16,2048]{2,1,0:T(8,128)(2,1)}), bf16[8,16,2048]{2,1,0:T(8,128)(2,1)S(1)}, u32[]{:S(2)}, u32[]{:S(2)}) async-start(bf16[8,16,2048]{2,1,0:T(8,128)(2,1)} %partial.1), calls=%async_computation.3 | async-start | bytes 1048576 | tf_op jit(solution)/shard_map/all_to_all | solution.py:306
  94.6 21.3 %collective-permute-start.11 = (bf16[1,384,1024]{2,1,0:T(8,128)(2,1)S(1)}, bf16[1,384,1024]{2,1,0:T(8,128)(2,1)}, u32[]{:S(2)}, u32[]{:S(2)}) collective-permute-start(bf16[1,384,1024]{2,1,0:T(8,128)(2,1)S(1)} %copy-done.5), channel_id=1, source_target_pairs={{0,1},{1,0},{2,3},{3,2},{4,5},{5,4},{6,7},{7,6},{8,9},{9,8},{10,11... | collective-permute-start | bytes 2359304 | tf_op jit(solution)/shard_map/ppermute | solution.py:302
  109.7 0.8 copy-start.2
  112.5 4.6 %collective-permute-start.6 = (bf16[16,2304]{1,0:T(8,128)(2,1)}, bf16[16,2304]{1,0:T(8,128)(2,1)S(1)}, u32[]{:S(2)}, u32[]{:S(2)}) collective-permute-start(bf16[16,2304]{1,0:T(8,128)(2,1)} %get-tuple-element.22.m0), channel_id=1, source_target_pairs={{0,2},{2,4},{4,6},{6,0},{1,3},{3,5},{5,7},{7,1},{8,10},{10,12},{12... | collective-permute-start | bytes 221192 | tf_op jit(solution)/shard_map/ppermute | solution.py:415
  112.9 6.1 %collective-permute-start.7 = (bf16[16,2304]{1,0:T(8,128)(2,1)}, bf16[16,2304]{1,0:T(8,128)(2,1)S(1)}, u32[]{:S(2)}, u32[]{:S(2)}) collective-permute-start(bf16[16,2304]{1,0:T(8,128)(2,1)} %get-tuple-element.22.m0), channel_id=1, source_target_pairs={{0,4},{2,6},{4,0},{6,2},{1,5},{3,7},{5,1},{7,3},{8,12},{10,14},{12... | collective-permute-start | bytes 221192 | tf_op jit(solution)/shard_map/ppermute | solution.py:415
  116.0 4.6 %collective-permute-start.8 = (bf16[16,2304]{1,0:T(8,128)(2,1)}, bf16[16,2304]{1,0:T(8,128)(2,1)S(1)}, u32[]{:S(2)}, u32[]{:S(2)}) collective-permute-start(bf16[16,2304]{1,0:T(8,128)(2,1)} %get-tuple-element.22.m0), channel_id=1, source_target_pairs={{0,6},{2,0},{4,2},{6,4},{1,7},{3,1},{5,3},{7,5},{8,14},{10,8},{12,... | collective-permute-start | bytes 221192 | tf_op jit(solution)/shard_map/ppermute | solution.py:415
  117.1 3.4 %copy-start.6 = (bf16[16,2304]{1,0:T(8,128)(2,1)}, bf16[16,2304]{1,0:T(8,128)(2,1)S(1)}, u32[]{:S(2)}) copy-start(bf16[16,2304]{1,0:T(8,128)(2,1)S(1)} %collective-permute-done.6.m1) | copy-start | bytes 221188
  119.0 1.5 copy-start.7
  120.5 0.6 copy-start.8
  121.2 31.0 %copy-start = (s32[16]{0:T(128)S(1)}, s32[16]{0:T(128)}, u32[]{:S(2)}) copy-start(s32[16]{0:T(128)} %param.39) | copy-start | bytes 196

commit v2 on v1

v2 whole, which is shorter than its diff:
```python
import jax
import jax.numpy as jnp
from jax import lax
from jax.experimental import pallas as pl
from jax.experimental.pallas import tpu as pltpu
from jax.sharding import Mesh
from jax.sharding import PartitionSpec as P

HEADS = 16
HEAD_DIM = 128
BLK = 128
CHIPS = 128
LANES = 128
ROWS = 16
CTX = 128
D = 2048
FH = 384
TD = 1024
EPSILON = 1e-06
WIDE = (D + LANES) // LANES * ROWS
TWIDE = (D + 2 * LANES) // LANES * ROWS
PLAIN = D // LANES * ROWS
N_Z = 8
N_XY = 16

f32 = jnp.float32
bf16 = jnp.bfloat16
VM = pl.BlockSpec(memory_space=pltpu.VMEM)
SM = pl.BlockSpec(memory_space=pltpu.SMEM)
HB = pl.BlockSpec(memory_space=pl.ANY)


def tile(h, rows=ROWS):
    return slice(h * rows, (h + 1) * rows)


def lane_iota(rows):
    return lax.broadcasted_iota(jnp.int32, (rows, LANES), 1)


def gather_t(onehot, values):
    return lax.dot_general(
        onehot, values, (((0,), (0,)), ((), ())), preferred_element_type=f32
    )


def attend_kernel(
    hidden, queries, cache_key, cache_value, new_key, new_value, lengths, gain, ids,
    think_gates, source, talk_ids, talk_gates, residual, message, asked, fresh_key, fresh_value,
    mixed, probs, keys, vals, sems,
):
    k_copy = pltpu.make_async_copy(cache_key, keys, sems.at[0])
    v_copy = pltpu.make_async_copy(cache_value, vals, sems.at[1])
    k_copy.start()
    v_copy.start()
    scaling = HEAD_DIM ** (-0.5)
    for h in range(HEADS):
        spot = pl.ds(h, ROWS, stride=HEADS)
        group = slice(h // 8 * 128, (h // 8 + 1) * 128)
        asked[spot, :] = queries[:, h * 128 : (h + 1) * 128].astype(f32)
        fresh_key[spot, :] = new_key[:, group].astype(f32)
        fresh_value[spot, :] = new_value[:, group].astype(f32)
    front = lax.broadcasted_iota(jnp.int32, (HEADS, LANES), 0) < HEADS // 2
    lane = lane_iota(HEADS)
    fresh = jnp.sum(asked[...] * fresh_key[...], axis=1, keepdims=True) * scaling
    k_copy.wait()
    for r in range(ROWS):
        rows = slice(r * HEADS, (r + 1) * HEADS)
        query = asked[rows, :]
        split = jnp.concatenate(
            [jnp.where(front, query, 0.0), jnp.where(front, 0.0, query)], axis=1
        ).astype(bf16)
        found = lax.dot_general(
            split, keys[r], (((1,), (1,)), ((), ())), preferred_element_type=f32
        )
        mixed[rows, :] = jnp.where(lane < lengths[r], found * scaling, -jnp.inf)
    scores = mixed[...]
    highest = jnp.maximum(jnp.max(scores, axis=1, keepdims=True), fresh)
    weights = jnp.exp(scores - highest)
    own = jnp.exp(fresh - highest)
    total = jnp.sum(weights, axis=1, keepdims=True) + own
    probs[...] = (weights / total).astype(bf16)
    added = (own / total).astype(bf16).astype(f32) * fresh_value[...]
    v_copy.wait()
    for r in range(ROWS):
        rows = slice(r * HEADS, (r + 1) * HEADS)
        both = jnp.dot(probs[rows, :], vals[r], preferred_element_type=f32)
        mixed[rows, :] = jnp.where(front, both[:, :128], both[:, 128:])
    mixed[...] = mixed[...] + added
    squares = jnp.zeros((ROWS, LANES), f32)
    for h in range(HEADS):
        cols = slice(h * 128, (h + 1) * 128)
        part = hidden[:, cols].astype(f32) + mixed[pl.ds(h, ROWS, stride=HEADS), :]
        residual[:, cols] = part
        squares = squares + part * part
    spread = jnp.sum(squares, axis=1, keepdims=True) * (1.0 / D)
    scale = lax.rsqrt(spread + EPSILON)
    for h in range(HEADS):
        cols = slice(h * 128, (h + 1) * 128)
        normed = (residual[:, cols] * scale * gain[h : h + 1, :].astype(f32)).astype(bf16)
        for z in range(N_Z):
            message[z, tile(h), :] = normed
    origin = source[...]
    fact = lax.broadcasted_iota(jnp.int32, (40, ROWS), 0)
    gates = talk_gates[...]
    high = gates.astype(bf16).astype(f32)
    low = gates - high
    facts = jnp.where(fact == 16 + origin % ROWS, 1.0, 0.0)
    facts = facts + jnp.where(fact == 32, (origin // 32).astype(f32), 0.0)
    for k in range(2):
        chosen = talk_ids[k : k + 1, :]
        facts = facts + jnp.where(fact == chosen, high[k : k + 1, :], 0.0)
        facts = facts + jnp.where(fact == chosen + 8, low[k : k + 1, :], 0.0)
    weights = think_gates[...]
    high = weights.astype(bf16).astype(f32)
    low = weights - high
    upright = jnp.concatenate(
        [facts, ids[...].astype(f32), high, low, jnp.zeros((64, ROWS), f32)], axis=0
    ).astype(bf16)
    same = lax.broadcasted_iota(jnp.int32, (ROWS, ROWS), 0) == lax.broadcasted_iota(
        jnp.int32, (ROWS, ROWS), 1
    )
    told = lax.dot_general(
        jnp.where(same, 1.0, 0.0).astype(bf16), upright, (((1,), (1,)), ((), ())),
        preferred_element_type=f32,
    ).astype(bf16)
    for z in range(N_Z):
        message[z, tile(HEADS), :] = told


def select_kernel(plane, ready, gathered, message, shares, inputs):
    rows = N_Z * ROWS
    for h in range(HEADS):
        inputs[:, h * 128 : (h + 1) * 128] = gathered[:, tile(h), :].reshape(rows, LANES)
    told = gathered[:, tile(HEADS), :].reshape(rows, LANES)
    facts = told.astype(f32)
    shape = (rows, 2 * LANES)
    col = lax.broadcasted_iota(jnp.int32, shape, 1)
    row = lax.broadcasted_iota(jnp.int32, shape, 0)
    chip = (plane[0] * N_XY + col // 16).astype(f32)
    turn = (col % 16) // 8
    level = (col % 8) == (row // ROWS)
    picked = jnp.zeros(shape, f32)
    high = jnp.zeros(shape, f32)
    low = jnp.zeros(shape, f32)
    for k in range(8):
        match = level & (facts[:, 40 + k : 41 + k] == chip)
        picked = jnp.where(match, 1.0, picked)
        high = jnp.where(match, facts[:, 48 + k : 49 + k], high)
        low = jnp.where(match, facts[:, 56 + k : 57 + k], low)
    below = lax.broadcasted_iota(jnp.int32, (rows, rows), 1) < lax.broadcasted_iota(
        jnp.int32, (rows, rows), 0
    )
    rank = jnp.dot(
        jnp.where(below, 1.0, 0.0).astype(bf16), picked.astype(bf16), preferred_element_type=f32
    )
    chosen = (picked > 0.5) & (jnp.abs(rank - turn.astype(f32)) < 0.5)
    onehot = jnp.where(chosen, 1.0, 0.0).astype(bf16)
    shares[:rows, :] = jnp.where(chosen, high, 0.0).astype(bf16)
    shares[rows:, :] = jnp.where(chosen, low, 0.0).astype(bf16)
    sent = gather_t(onehot, inputs[...]).astype(bf16)
    for h in range(HEADS):
        message[:, tile(h), :] = sent[:, h * 128 : (h + 1) * 128].reshape(N_XY, 16, LANES)
    owned = level & (turn == 0) & (facts[:, 32:33] == chip)
    message[:, tile(HEADS), :] = (
        gather_t(jnp.where(owned, 1.0, 0.0).astype(bf16), told)
        .astype(bf16)
        .reshape(N_XY, 16, LANES)
    )


def silu(x):
    return x * jax.nn.sigmoid(x)


def scaled(block, scale):
    return (block.astype(f32) * scale).astype(bf16)


def restore_tall_kernel(gs0, us0, gs1, us1, g0, u0, g1, u1, gw, uw, token):
    i = pl.program_id(0)
    token[...] = jnp.zeros_like(token)
    for half, (gs, us, g, u) in enumerate([(gs0, us0, g0, u0), (gs1, us1, g1, u1)]):
        for j in range(FH // BLK):
            cols = slice(j * BLK, (j + 1) * BLK)
            there = slice(half * FH + j * BLK, half * FH + (j + 1) * BLK)
            for k in range(2):
                near = slice(k * BLK, (k + 1) * BLK)
                gw[near, there] = scaled(g[0, near, cols], gs[j, 0, 2 * i + k])
                uw[near, there] = scaled(u[0, near, cols], us[j, 0, 2 * i + k])


def restore_flat_kernel(ds0, ds1, d0, d1, dw):
    i = pl.program_id(0)
    for half, (ds, d) in enumerate([(ds0, d0), (ds1, d1)]):
        for j in range(FH // BLK):
            rows = slice(j * BLK, (j + 1) * BLK)
            there = slice(half * FH + j * BLK, half * FH + (j + 1) * BLK)
            for k in range(4):
                near = slice(k * BLK, (k + 1) * BLK)
                dw[there, near] = scaled(d[0, rows, near], ds[j, 0, 4 * i + k])


def expert_kernel(arrived, g, u, d, produced, wide_in, rows_in, gw, uw, dw, sems):
    copies = []
    for i, (src, dst) in enumerate(
        [(arrived.at[:, pl.ds(0, PLAIN), :], wide_in), (g, gw), (u, uw), (d, dw)]
    ):
        copy = pltpu.make_async_copy(src, dst, sems.at[i])
        copy.start()
        copies.append(copy)
    copies[0].wait()
    for h in range(HEADS):
        rows_in[:, h * 128 : (h + 1) * 128] = wide_in[:, tile(h), :].reshape(2 * CHIPS, LANES)
    inputs = rows_in[...]
    copies[1].wait()
    gated = jnp.dot(inputs, gw[...], preferred_element_type=f32)
    copies[2].wait()
    lifted = jnp.dot(inputs, uw[...], preferred_element_type=f32)
    middle = (silu(gated) * lifted).astype(bf16)
    copies[3].wait()
    for h in range(HEADS // 2):
        cols = slice(h * 256, (h + 1) * 256)
        part = jnp.dot(middle, dw[:, cols], preferred_element_type=f32)
        for k in range(2):
            produced[:, tile(2 * h + k), :] = (
                part[:, k * 128 : (k + 1) * 128].astype(bf16).reshape(N_XY, 16, LANES)
            )


def partial_kernel(returned, shares, partial, rows_in):
    for h in range(HEADS):
        rows_in[:, h * 128 : (h + 1) * 128] = returned[:, tile(h), :].reshape(2 * CHIPS, LANES)
    both = jnp.dot(shares[...], rows_in[...], preferred_element_type=f32)
    total = (both[:CHIPS] + both[CHIPS:]).astype(bf16)
    for h in range(HEADS):
        partial[:, tile(h), :] = total[:, h * 128 : (h + 1) * 128].reshape(N_Z, ROWS, LANES)


def combine_kernel(collected, residual, owned, gain, thinker_out, onward):
    squares = jnp.zeros((ROWS, LANES), f32)
    for h in range(HEADS):
        cols = slice(h * 128, (h + 1) * 128)
        part = residual[:, cols]
        for z in range(N_Z):
            part = part + collected[z, tile(h), :].astype(f32)
        part = part.astype(bf16)
        thinker_out[:, cols] = part
        part = part.astype(f32)
        squares = squares + part * part
    scale = lax.rsqrt(jnp.sum(squares, axis=1, keepdims=True) * (1.0 / D) + EPSILON)
    for h in range(HEADS):
        part = thinker_out[:, h * 128 : (h + 1) * 128].astype(f32)
        onward[tile(h), :] = (part * scale * gain[h : h + 1, :].astype(f32)).astype(bf16)
    told = owned[...].astype(f32)[:, :8, :].reshape(CHIPS, LANES).astype(bf16)
    pick = jnp.where(
        lane_iota(ROWS) == 16 + lax.broadcasted_iota(jnp.int32, (ROWS, LANES), 0), 1.0, 0.0
    ).astype(bf16)
    goal = lax.dot_general(
        pick, told, (((1,), (1,)), ((), ())), preferred_element_type=f32
    ).astype(bf16)
    onward[tile(HEADS), :] = goal
    onward[tile(HEADS + 1), :] = jnp.dot(goal, told, preferred_element_type=f32).astype(bf16)


def talker_kernel(
    place, m0, m1, m2, m3, g0, u0, d0, g1, u1, d1, relayed, rows_in, gw, uw, dw, sems,
):
    copies = []
    for i, (src, dst) in enumerate(
        [
            (g0, gw.at[0]), (u0, uw.at[0]), (d0, dw.at[0]),
            (g1, gw.at[1]), (u1, uw.at[1]), (d1, dw.at[1]),
        ]
    ):
        copy = pltpu.make_async_copy(src.at[0], dst, sems.at[i])
        copy.start()
        copies.append(copy)
    for i, m in enumerate([m0, m1, m2, m3]):
        for h in range(HEADS + 2):
            rows_in[tile(i), h * 128 : (h + 1) * 128] = m[tile(h), :]
    inputs = rows_in[:, :D]
    goal = rows_in[:, D : D + LANES]
    shares = rows_in[:, D + LANES :].astype(f32)
    lane = lane_iota(4 * ROWS)
    total = jnp.zeros((4 * ROWS, TD), f32)
    for half in range(2):
        expert = place[0] if half == 0 else place[0] + 1 - 2 * (place[0] % 2)
        share = jnp.sum(
            jnp.where((lane == expert) | (lane == expert + 8), shares, 0.0), axis=1, keepdims=True
        )
        copies[3 * half].wait()
        gated = jnp.dot(inputs, gw[half], preferred_element_type=f32)
        copies[3 * half + 1].wait()
        lifted = jnp.dot(inputs, uw[half], preferred_element_type=f32)
        middle = (silu(gated) * lifted).astype(bf16)
        copies[3 * half + 2].wait()
        part = jnp.dot(middle, dw[half], preferred_element_type=f32)
        total = total + share * part.astype(bf16).astype(f32)
    sent = gather_t(goal, total.astype(bf16))
    for h in range(TD // 128):
        relayed[:, tile(h, 8), :] = (
            sent[:, h * 128 : (h + 1) * 128].reshape(N_XY, 8, LANES).astype(bf16)
        )


def cross_kernel(returned, relayed):
    line = lax.broadcasted_iota(jnp.int32, (64, CHIPS), 0)
    came = lax.broadcasted_iota(jnp.int32, (64, CHIPS), 1)
    pick = ((line // 8) == (came % 8)) & ((line % 8) == (came // 32))
    pick = jnp.where(pick, 1.0, 0.0).astype(bf16)
    for h in range(TD // 128):
        rows = returned[:, tile(h, 8), :].astype(f32).reshape(CHIPS, LANES).astype(bf16)
        out = jnp.dot(pick, rows, preferred_element_type=f32)
        relayed[:, tile(h, 8), :] = out.reshape(N_Z, 8, LANES).astype(bf16)


def settle_kernel(returned, source, talker_out):
    line = lax.broadcasted_iota(jnp.int32, (64, ROWS), 0)
    wide = source[...] // 128
    pick = ((line // 8) == (wide // 4)) & ((line % 8) == (wide % 4))
    pick = jnp.where(pick, 1.0, 0.0).astype(bf16)
    for h in range(TD // 128):
        rows = returned[:, tile(h, 8), :].astype(f32).reshape(64, LANES).astype(bf16)
        talker_out[:, h * 128 : (h + 1) * 128] = gather_t(pick, rows).astype(bf16)


def sds(shape, dtype):
    return jax.ShapeDtypeStruct(shape, dtype)


def swap(value):
    return lax.ppermute(value, "c", [(0, 1), (1, 0)])


def exchange(value, axes):
    return lax.all_to_all(value, axes, 0, 0, tiled=True)


SMALL = pltpu.CompilerParams(vmem_limit_bytes=24 << 20)


def local(
    hidden_in, queries, cache_key, cache_value, new_key, new_value, lengths, norm_gain,
    gate_codes, gate_scale, up_codes, up_scale, down_codes, down_scale, think_ids, think_gates,
    talker_source, talker_gain, talk_gate_w, talk_up_w, talk_down_w, talk_ids, talk_gates,
):
    own = (gate_codes, up_codes, down_codes)
    own_scale = (
        jnp.transpose(gate_scale, (2, 0, 1)),
        jnp.transpose(up_scale, (2, 0, 1)),
        jnp.transpose(down_scale, (1, 0, 2)),
    )
    other = tuple(swap(w) for w in own)
    other_scale = tuple(swap(s) for s in own_scale)
    source = talker_source.reshape(1, ROWS)

    residual, message = pl.pallas_call(
        attend_kernel,
        out_shape=(sds((ROWS, D), f32), sds((N_Z, WIDE, LANES), bf16)),
        in_specs=[VM] * 2 + [HB] * 2 + [VM] * 2 + [SM] + [VM] * 6,
        out_specs=(VM, VM),
        scratch_shapes=[
            pltpu.VMEM((ROWS * HEADS, LANES), f32),
            pltpu.VMEM((ROWS * HEADS, LANES), f32),
            pltpu.VMEM((ROWS * HEADS, LANES), f32),
            pltpu.VMEM((ROWS * HEADS, LANES), f32),
            pltpu.VMEM((ROWS * HEADS, LANES), bf16),
            pltpu.VMEM((ROWS, CTX, 256), bf16),
            pltpu.VMEM((ROWS, CTX, 256), bf16),
            pltpu.SemaphoreType.DMA((2,)),
        ],
        name="attend",
    )(
        hidden_in, queries, cache_key, cache_value, new_key, new_value, lengths,
        norm_gain.reshape(HEADS, LANES), think_ids.T, think_gates.T, source,
        talk_ids.T, talk_gates.T,
    )
    gathered = exchange(message, "z")
    tall = pl.BlockSpec((1, 2 * BLK, FH), lambda i: (0, i, 0))
    tall_out = pl.BlockSpec((2 * BLK, 2 * FH), lambda i: (i, 0))
    gate_dense, up_dense, token = pl.pallas_call(
        restore_tall_kernel,
        grid=(D // BLK // 2,),
        out_shape=(sds((D, 2 * FH), bf16), sds((D, 2 * FH), bf16), sds((8, LANES), f32)),
        in_specs=[SM] * 4 + [tall] * 4,
        out_specs=(tall_out, tall_out, pl.BlockSpec((8, LANES), lambda i: (0, 0))),
        cost_estimate=pl.CostEstimate(
            flops=4 * D * FH, bytes_accessed=16 * D * FH, transcendentals=0
        ),
        name="restore_tall",
    )(*own_scale[:2], *other_scale[:2], *own[:2], *other[:2])
    flat = pl.BlockSpec((1, FH, 4 * BLK), lambda i: (0, 0, i))
    flat_out = pl.BlockSpec((2 * FH, 4 * BLK), lambda i: (0, i))
    down_dense = pl.pallas_call(
        restore_flat_kernel,
        grid=(D // BLK // 4,),
        out_shape=sds((2 * FH, D), bf16),
        in_specs=[SM] * 2 + [flat] * 2,
        out_specs=flat_out,
        cost_estimate=pl.CostEstimate(
            flops=2 * D * FH, bytes_accessed=8 * D * FH, transcendentals=0
        ),
        name="restore_flat",
    )(own_scale[2], other_scale[2], own[2], other[2])
    plane = lax.axis_index("z").astype(jnp.int32).reshape(1)
    chosen, shares = pl.pallas_call(
        select_kernel,
        out_shape=(sds((N_XY, WIDE, LANES), bf16), sds((2 * CHIPS, 2 * LANES), bf16)),
        in_specs=[SM, HB, VM],
        out_specs=(VM, VM),
        scratch_shapes=[pltpu.VMEM((CHIPS, D), bf16)],
        compiler_params=SMALL,
        name="select",
    )(plane, token, gathered)
    arrived = exchange(chosen, ("x", "y"))
    produced = pl.pallas_call(
        expert_kernel,
        out_shape=sds((N_XY, PLAIN, LANES), bf16),
        in_specs=[HB] * 4,
        out_specs=VM,
        scratch_shapes=[
            pltpu.VMEM((N_XY, PLAIN, LANES), bf16),
            pltpu.VMEM((2 * CHIPS, D), bf16),
            pltpu.VMEM((D, 2 * FH), bf16),
            pltpu.VMEM((D, 2 * FH), bf16),
            pltpu.VMEM((2 * FH, D), bf16),
            pltpu.SemaphoreType.DMA((4,)),
        ],
        name="experts",
    )(arrived, gate_dense, up_dense, down_dense)
    returned = exchange(produced, ("x", "y"))
    partial = pl.pallas_call(
        partial_kernel,
        out_shape=sds((N_Z, PLAIN, LANES), bf16),
        in_specs=[VM, VM],
        out_specs=VM,
        scratch_shapes=[pltpu.VMEM((2 * CHIPS, D), bf16)],
        compiler_params=SMALL,
        name="partial",
    )(returned, shares)
    collected = exchange(partial, "z")
    talk_own = (talk_gate_w, talk_up_w, talk_down_w)
    talk_held = lax.optimization_barrier((*talk_own, arrived))[:3]
    talk_other = tuple(swap(w) for w in talk_held)
    thinker_out, onward = pl.pallas_call(
        combine_kernel,
        grid=(1,),
        out_shape=(sds((ROWS, D), bf16), sds((TWIDE, LANES), bf16)),
        in_specs=[
            pl.BlockSpec((N_Z, PLAIN, LANES), lambda i: (0, 0, 0)),
            pl.BlockSpec((ROWS, D), lambda i: (0, 0)),
            pl.BlockSpec((N_XY, 16, LANES), lambda i: (0, HEADS, 0)),
            pl.BlockSpec((HEADS, LANES), lambda i: (0, 0)),
        ],
        out_specs=(
            pl.BlockSpec((ROWS, D), lambda i: (0, 0)),
            pl.BlockSpec((TWIDE, LANES), lambda i: (0, 0)),
        ),
        name="combine",
    )(collected, residual, arrived, talker_gain.reshape(HEADS, LANES))
    peers = [
        lax.ppermute(onward, "y", [(i, (i + o) % 4) for i in range(4)]) for o in (1, 2, 3)
    ]
    place = (lax.axis_index("y") * 2 + lax.axis_index("c")).astype(jnp.int32).reshape(1)
    relayed = pl.pallas_call(
        talker_kernel,
        out_shape=sds((N_XY, 64, LANES), bf16),
        in_specs=[SM] + [VM] * 4 + [HB] * 6,
        out_specs=VM,
        scratch_shapes=[
            pltpu.VMEM((4 * ROWS, D + 2 * LANES), bf16),
            pltpu.VMEM((2, D, FH), bf16),
            pltpu.VMEM((2, D, FH), bf16),
            pltpu.VMEM((2, FH, TD), bf16),
            pltpu.SemaphoreType.DMA((6,)),
        ],
        name="talkers",
    )(place, onward, *peers, *talk_own, *talk_other)
    crossing = exchange(relayed, ("x", "y"))
    crossed = pl.pallas_call(
        cross_kernel,
        out_shape=sds((N_Z, 64, LANES), bf16),
        in_specs=[VM],
        out_specs=VM,
        compiler_params=SMALL,
        name="cross",
    )(crossing)
    settled = exchange(crossed, "z")
    talker_out = pl.pallas_call(
        settle_kernel,
        out_shape=sds((ROWS, TD), bf16),
        in_specs=[VM, VM],
        out_specs=VM,
        compiler_params=SMALL,
        name="settle",
    )(settled, source)
    return (thinker_out, talker_out)


def solution(mesh):
    fine = Mesh(mesh.devices.reshape(8, 4, 4, 2), ("z", "x", "y", "c"))
    every = ("z", "x", "y", "c")
    two = P(every, None)
    three = P(every, None, None)
    talk = P(("y", "c"), None, None)
    return jax.shard_map(
        local,
        mesh=fine,
        in_specs=(
            two, two, three, three, two, two, P(every), P(),
            three, three, three, three, three, three, two, two,
            P(every), P(), talk, talk, talk, two, two,
        ),
        out_specs=(two, two),
        check_vma=False,
    )
```

time: 154 us -> 151 us (0.981)
  waiting for transfers between devices: 56.7 us -> 54 us
    all_to_all x4, waiting for transfers between devices: 50.7 us -> 45.7 us  [exchange(): return lax.all_to_all(value, axes, 0, 0, tiled=True)]
    ppermute x9, waiting for transfers between devices: 1.66 us -> 4.08 us  [swap(): return lax.ppermute(value, 'c', [(0, 1), (1, 0)])]
    pallas_call x7 -> x8, Pallas kernels: 34.3 us -> 32.9 us  [the longest x1 8.33 us: local(): pl.pallas_call(restore_tall_kernel, grid=(D // BLK // 2,), out_shape=(sds...]
    unnamed x30 -> x32, local copies, waits for them, and re-layouts: 3.04 us -> 4.28 us
  transfers between devices with their start and end apart: 16 -> 16, of which waited for: 9 -> 9; matrix products, arithmetic and copies ran while one was open for 0% -> 0% of each run, Pallas kernels for 10% -> 15%
where the time goes in v2:
time: 151 us; the launch traced here: 150 us
  waiting for transfers between devices  54 us (36%)
  Pallas kernels  35.7 us (24%)
  starting transfers between devices  30.1 us (20%)
  blocking collectives  25.1 us (17%)
  local copies, waits for them, and re-layouts  4.28 us (3%)
    all_to_all x4, waiting for transfers between devices, exchange(): return lax.all_to_all(value, axes, 0, 0, tiled=True)  45.7 us
    all_to_all x2, blocking collectives, exchange(): return lax.all_to_all(value, axes, 0, 0, tiled=True)  25.1 us
    all_to_all x4, starting transfers between devices, exchange(): return lax.all_to_all(value, axes, 0, 0, tiled=True)  24.4 us
    pallas_call x1, Pallas kernels, local(): pl.pallas_call(restore_tall_kernel, grid=(D // BLK // 2,), out_shape=(sds...  8.33 us
    pallas_call x1, Pallas kernels, local(): pl.pallas_call(expert_kernel, out_shape=sds((N_XY, PLAIN, LANES), bf16),...  6.68 us
    pallas_call x1, Pallas kernels, local(): pl.pallas_call(talker_kernel, out_shape=sds((N_XY, 64, LANES), bf16), in_...  5.73 us
    pallas_call x1, Pallas kernels, local(): pl.pallas_call(restore_flat_kernel, grid=(D // BLK // 4,), out_shape=sds(...  4.54 us
    ppermute x3, waiting for transfers between devices, local(): lax.ppermute(onward, 'y', [(i, (i + o) % 4) for i in range(4)])  4.28 us
  transfers between devices with their start and end apart: 16, of which 9 were waited for; matrix products, arithmetic and copies ran while one was open for 0% of the time, Pallas kernels for 15%

profile of v2, /device:TPU:8, one launch (start us, length us, event | category | flops | bytes accessed | tf_op | source)
XLA Modules:
  0.0 150.0 jit_solution(12780699409591197399)
XLA Ops:
  0.6 0.1 collective-permute-start.2
  0.7 0.5 collective-permute-start.3
  1.2 4.1 %attend.1 = (f32[16,2048]{1,0:T(8,128)}, bf16[8,272,128]{2,1,0:T(8,128)(2,1)}) custom-call(bf16[16,2048]{1,0:T(8,128)(2,1)} %hidden.1, bf16[16,2048]{1,0:T(8,128)(2,1)} %queries.1, bf16[16,128,256]{2,1,0:T(8,128)(2,1)} %cache_key.1, bf16[16,128,256]{2,1,0:T(8,128)(2,1)} %cache_value.1, bf16[16,256]{1,0:T(8,128)(2,1)} %new_key.1, bf16[16,256]{1,0:T(8,128)(2,1)} %new_value.1, ...), custom_call_target="tpu_custom_call" | custom-call | tf_op jit(solution)/shard_map/attend/pallas_call | solution.py:358
  5.3 8.5 %all-to-all-start = ((bf16[8,272,128]{2,1,0:T(8,128)(2,1)}), bf16[8,272,128]{2,1,0:T(8,128)(2,1)S(1)}, u32[]{:S(2)}, u32[]{:S(2)}) async-start(bf16[8,272,128]{2,1,0:T(8,128)(2,1)} %get-tuple-element.15), calls=%async_computation | async-start | bytes 1114112 | tf_op jit(solution)/shard_map/all_to_all | solution.py:337
  13.8 0.1 collective-permute-start.5
  13.9 0.5 collective-permute-start
  14.4 0.1 collective-permute-start.1
  14.5 2.9 %collective-permute-done.gs1 = f32[3,1,16]{2,1,0:T(1,128)S(1)} collective-permute-done((f32[3,1,16]{2,1,0:T(1,128)S(1)}, f32[3,1,16]{2,1,0:T(1,128)S(1)}, u32[]{:S(2)}, u32[]{:S(2)}) %collective-permute-start) | collective-permute-done | bytes 224 | tf_op jit(solution)/shard_map/ppermute | solution.py:333
  17.4 0.0 collective-permute-done.1.us1
  17.4 0.0 collective-permute-done.3.u1
  17.4 0.5 copy-done.13
  18.0 0.0 copy-done.14
  18.0 8.3 %restore_tall.1 = (bf16[2048,768]{1,0:T(8,128)(2,1)}, bf16[2048,768]{1,0:T(8,128)(2,1)}, f32[8,128]{1,0:T(8,128)}) custom-call(f32[3,1,16]{2,1,0:T(1,128)} %bitcast.18, f32[3,1,16]{2,1,0:T(1,128)} %bitcast.20, f32[3,1,16]{2,1,0:T(1,128)} %copy-done.13, f32[3,1,16]{2,1,0:T(1,128)} %copy-done.14, bf16[1,2048,384]{2,1,0:T(8,128)(2,1)} %g0.2, ...), custom_call_target="tpu_custom_call" | custom-call | flops 3145728 | bytes 12582912 | tf_op jit(solution)/shard_map/restore_tall/pallas_call | solution.py:382
  26.3 5.9 %all-to-all-done.gathered = bf16[8,272,128]{2,1,0:T(8,128)(2,1)S(1)} async-done(((bf16[8,272,128]{2,1,0:T(8,128)(2,1)}), bf16[8,272,128]{2,1,0:T(8,128)(2,1)S(1)}, u32[]{:S(2)}, u32[]{:S(2)}) %all-to-all-start) | async-done | bytes 557088 | tf_op jit(solution)/shard_map/all_to_all | solution.py:337
  32.3 0.7 copy-done
  32.9 2.1 %select.1 = (bf16[16,272,128]{2,1,0:T(8,128)(2,1)}, bf16[256,256]{1,0:T(8,128)(2,1)S(1)}) custom-call(s32[1]{0:T(128)} %bitcast.plane, f32[8,128]{1,0:T(8,128)S(1)} %copy-done, bf16[8,272,128]{2,1,0:T(8,128)(2,1)S(1)} %all-to-all-done.gathered), custom_call_target="tpu_custom_call" | custom-call | tf_op jit(solution)/shard_map/select/pallas_call | solution.py:407
  35.0 7.4 %all-to-all-start.1 = ((bf16[16,272,128]{2,1,0:T(8,128)(2,1)}), bf16[16,272,128]{2,1,0:T(8,128)(2,1)S(1)}, u32[]{:S(2)}, u32[]{:S(2)}) async-start(bf16[16,272,128]{2,1,0:T(8,128)(2,1)} %get-tuple-element.16), calls=%async_computation.1 | async-start | bytes 2228224 | tf_op jit(solution)/shard_map/all_to_all | solution.py:337
  42.4 0.1 collective-permute-start.4
  42.5 1.1 collective-permute-done.4.ds1
  43.7 0.0 collective-permute-done.5.d1
  43.7 0.6 copy-done.15
  44.2 4.5 %restore_flat.1.d = bf16[768,2048]{1,0:T(8,128)(2,1)} custom-call(f32[3,1,16]{2,1,0:T(1,128)} %bitcast.22, f32[3,1,16]{2,1,0:T(1,128)} %copy-done.15, bf16[1,384,2048]{2,1,0:T(8,128)(2,1)} %d0.2, bf16[1,384,2048]{2,1,0:T(8,128)(2,1)} %collective-permute-done.5.d1), custom_call_target="tpu_custom_call" | custom-call | flops 1572864 | bytes 6291456 | tf_op jit(solution)/shard_map/restore_flat/pallas_call | solution.py:395
  48.8 11.0 %all-to-all-done.1.arrived.owned = bf16[16,272,128]{2,1,0:T(8,128)(2,1)S(1)} async-done(((bf16[16,272,128]{2,1,0:T(8,128)(2,1)}), bf16[16,272,128]{2,1,0:T(8,128)(2,1)S(1)}, u32[]{:S(2)}, u32[]{:S(2)}) %all-to-all-start.1) | async-done | bytes 1114144 | tf_op jit(solution)/shard_map/all_to_all | solution.py:337
  59.8 1.0 copy-done.2
  60.8 6.7 %experts.1 = bf16[16,256,128]{2,1,0:T(8,128)(2,1)} custom-call(bf16[16,272,128]{2,1,0:T(8,128)(2,1)} %copy-done.2, bf16[2048,768]{1,0:T(8,128)(2,1)} %get-tuple-element.17.g, bf16[2048,768]{1,0:T(8,128)(2,1)} %get-tuple-element.18.u, bf16[768,2048]{1,0:T(8,128)(2,1)} %restore_flat.1.d), custom_call_target="tpu_custom_call" | custom-call | tf_op jit(solution)/shard_map/experts/pallas_call | solution.py:417
  67.5 0.0 copy-start.4
  67.5 5.0 %all-to-all-start.2 = ((bf16[16,256,128]{2,1,0:T(8,128)(2,1)}), bf16[16,256,128]{2,1,0:T(8,128)(2,1)S(1)}, u32[]{:S(2)}, u32[]{:S(2)}) async-start(bf16[16,256,128]{2,1,0:T(8,128)(2,1)} %experts.1), calls=%async_computation.2 | async-start | bytes 2097152 | tf_op jit(solution)/shard_map/all_to_all | solution.py:337
  72.5 0.1 collective-permute-start.10
  72.6 0.5 collective-permute-start.9
  73.1 13.8 %all-to-all-done.2.returned = bf16[16,256,128]{2,1,0:T(8,128)(2,1)S(1)} async-done(((bf16[16,256,128]{2,1,0:T(8,128)(2,1)}), bf16[16,256,128]{2,1,0:T(8,128)(2,1)S(1)}, u32[]{:S(2)}, u32[]{:S(2)}) %all-to-all-start.2) | async-done | bytes 1048608 | tf_op jit(solution)/shard_map/all_to_all | solution.py:337
  86.9 1.3 partial.1
  88.2 3.5 %all-to-all-start.3 = ((bf16[8,256,128]{2,1,0:T(8,128)(2,1)}), bf16[8,256,128]{2,1,0:T(8,128)(2,1)S(1)}, u32[]{:S(2)}, u32[]{:S(2)}) async-start(bf16[8,256,128]{2,1,0:T(8,128)(2,1)} %partial.1), calls=%async_computation.3 | async-start | bytes 1048576 | tf_op jit(solution)/shard_map/all_to_all | solution.py:337
  91.7 0.1 collective-permute-start.11
  91.8 15.0 %all-to-all-done.3.collected = bf16[8,256,128]{2,1,0:T(8,128)(2,1)S(1)} async-done(((bf16[8,256,128]{2,1,0:T(8,128)(2,1)}), bf16[8,256,128]{2,1,0:T(8,128)(2,1)S(1)}, u32[]{:S(2)}, u32[]{:S(2)}) %all-to-all-start.3) | async-done | bytes 524320 | tf_op jit(solution)/shard_map/all_to_all | solution.py:337
  106.8 0.8 copy-done.3
  107.6 2.0 %combine.1 = (bf16[16,2048]{1,0:T(8,128)(2,1)}, bf16[288,128]{1,0:T(8,128)(2,1)}) custom-call(bf16[8,256,128]{2,1,0:T(8,128)(2,1)} %copy-done.3, f32[16,2048]{1,0:T(8,128)} %get-tuple-element.20.residual, bf16[16,272,128]{2,1,0:T(8,128)(2,1)} %copy-done.2, bf16[16,128]{1,0:T(8,128)(2,1)} %bitcast.17), custom_call_target="tpu_custom_call" | custom-call | tf_op jit(solution)/shard_map/combine/pallas_call | solution.py:446
  109.6 0.4 collective-permute-start.6
  110.0 3.0 %collective-permute-start.7 = (bf16[288,128]{1,0:T(8,128)(2,1)}, bf16[288,128]{1,0:T(8,128)(2,1)S(1)}, u32[]{:S(2)}, u32[]{:S(2)}) collective-permute-start(bf16[288,128]{1,0:T(8,128)(2,1)} %get-tuple-element.22.m0), channel_id=1, source_target_pairs={{0,4},{2,6},{4,0},{6,2},{1,5},{3,7},{5,1},{7,3},{8,12},{10,14},{12... | collective-permute-start | bytes 221192 | tf_op jit(solution)/shard_map/ppermute | solution.py:463
  113.0 0.3 collective-permute-start.8
  113.2 0.9 collective-permute-done.6.m1
  114.1 1.9 %collective-permute-done.7.m2 = bf16[288,128]{1,0:T(8,128)(2,1)S(1)} collective-permute-done((bf16[288,128]{1,0:T(8,128)(2,1)}, bf16[288,128]{1,0:T(8,128)(2,1)S(1)}, u32[]{:S(2)}, u32[]{:S(2)}) %collective-permute-start.7) | collective-permute-done | bytes 73760 | tf_op jit(solution)/shard_map/ppermute | solution.py:463
  116.0 1.5 collective-permute-done.8.m3
  117.5 0.6 copy-done.9
  118.2 5.7 %talkers.1 = bf16[16,64,128]{2,1,0:T(8,128)(2,1)} custom-call(s32[1]{0:T(128)} %bitcast.11.place, bf16[288,128]{1,0:T(8,128)(2,1)} %get-tuple-element.22.m0, bf16[288,128]{1,0:T(8,128)(2,1)} %copy-done.7, bf16[288,128]{1,0:T(8,128)(2,1)} %copy-done.8, bf16[288,128]{1,0:T(8,128)(2,1)} %copy-done.9, bf16[1,2048,384]{2,1,0:T(8,128)(2,1)} %g0.3, ...), custom_call_target="tpu_custom_call" | custom-call | tf_op jit(solution)/shard_map/talkers/pallas_call | solution.py:466
  123.9 13.6 %all_to_all.30.returned = bf16[16,64,128]{2,1,0:T(8,128)(2,1)S(1)} all-to-all(bf16[16,64,128]{2,1,0:T(8,128)(2,1)} %talkers.1), channel_id=1, replica_groups=mesh['z'=8,'x'=4,'y'=4,'c'=2] {'x','y'}, dimensions={0} | all-to-all | bytes 524288 | tf_op jit(solution)/shard_map/all_to_all | solution.py:337
  137.5 0.2 cross.1
  137.7 11.5 %all_to_all.31.returned = bf16[8,64,128]{2,1,0:T(8,128)(2,1)S(1)} all-to-all(bf16[8,64,128]{2,1,0:T(8,128)(2,1)S(1)} %cross.1), channel_id=1, replica_groups=mesh['z'=8,'x'=4,'y'=4,'c'=2] {'z'}, dimensions={0} | all-to-all | bytes 262144 | tf_op jit(solution)/shard_map/all_to_all | solution.py:337
  149.2 0.8 settle.1
  (28 shorter events, 0.1 us)
Async XLA Ops:
  0.6 16.8 %collective-permute-start.2 = (bf16[1,2048,384]{2,1,0:T(8,128)(2,1)}, bf16[1,2048,384]{2,1,0:T(8,128)(2,1)}, u32[]{:S(2)}, u32[]{:S(2)}) collective-permute-start(bf16[1,2048,384]{2,1,0:T(8,128)(2,1)} %g0.2), channel_id=1, source_target_pairs={{0,1},{1,0},{2,3},{3,2},{4,5},{5,4},{6,7},{7,6},{8,9},{9,8},{10,11... | collective-permute-start | bytes 4718600 | tf_op jit(solution)/shard_map/ppermute | solution.py:333
  0.7 16.7 %collective-permute-start.3 = (bf16[1,2048,384]{2,1,0:T(8,128)(2,1)}, bf16[1,2048,384]{2,1,0:T(8,128)(2,1)}, u32[]{:S(2)}, u32[]{:S(2)}) collective-permute-start(bf16[1,2048,384]{2,1,0:T(8,128)(2,1)} %u0.2), channel_id=1, source_target_pairs={{0,1},{1,0},{2,3},{3,2},{4,5},{5,4},{6,7},{7,6},{8,9},{9,8},{10,11... | collective-permute-start | bytes 4718600 | tf_op jit(solution)/shard_map/ppermute | solution.py:333
  1.2 12.6 %copy-start.5 = (bf16[1,384,2048]{2,1,0:T(8,128)(2,1)S(1)}, bf16[1,384,2048]{2,1,0:T(8,128)(2,1)}, u32[]{:S(2)}) copy-start(bf16[1,384,2048]{2,1,0:T(8,128)(2,1)} %d0.2) | copy-start | bytes 4718596
  1.2 12.7 %copy-start.10 = (f32[1,16,3]{1,0,2:T(1,128)S(1)}, f32[1,16,3]{1,0,2:T(1,128)}, u32[]{:S(2)}) copy-start(f32[1,16,3]{1,0,2:T(1,128)} %param.32) | copy-start | bytes 580
  1.2 13.2 %copy-start.11 = (f32[1,16,3]{1,0,2:T(1,128)S(1)}, f32[1,16,3]{1,0,2:T(1,128)}, u32[]{:S(2)}) copy-start(f32[1,16,3]{1,0,2:T(1,128)} %param.34) | copy-start | bytes 580
  5.3 26.9 %all-to-all-start = ((bf16[8,272,128]{2,1,0:T(8,128)(2,1)}), bf16[8,272,128]{2,1,0:T(8,128)(2,1)S(1)}, u32[]{:S(2)}, u32[]{:S(2)}) async-start(bf16[8,272,128]{2,1,0:T(8,128)(2,1)} %get-tuple-element.15), calls=%async_computation | async-start | bytes 1114112 | tf_op jit(solution)/shard_map/all_to_all | solution.py:337
  13.8 29.9 %collective-permute-start.5 = (bf16[1,384,2048]{2,1,0:T(8,128)(2,1)S(1)}, bf16[1,384,2048]{2,1,0:T(8,128)(2,1)}, u32[]{:S(2)}, u32[]{:S(2)}) collective-permute-start(bf16[1,384,2048]{2,1,0:T(8,128)(2,1)S(1)} %copy-done.5), channel_id=1, source_target_pairs={{0,1},{1,0},{2,3},{3,2},{4,5},{5,4},{6,7},{7,6},{8,9},{9,8},{10,11... | collective-permute-start | bytes 4718600 | tf_op jit(solution)/shard_map/ppermute | solution.py:333
  13.9 3.5 %collective-permute-start = (f32[3,1,16]{2,1,0:T(1,128)S(1)}, f32[3,1,16]{2,1,0:T(1,128)S(1)}, u32[]{:S(2)}, u32[]{:S(2)}) collective-permute-start(f32[3,1,16]{2,1,0:T(1,128)S(1)} %bitcast.19), channel_id=1, source_target_pairs={{0,1},{1,0},{2,3},{3,2},{4,5},{5,4},{6,7},{7,6},{8,9},{9,8},{10,11... | collective-permute-start | bytes 584 | tf_op jit(solution)/shard_map/ppermute | solution.py:333
  14.4 3.0 %collective-permute-start.1 = (f32[3,1,16]{2,1,0:T(1,128)S(1)}, f32[3,1,16]{2,1,0:T(1,128)S(1)}, u32[]{:S(2)}, u32[]{:S(2)}) collective-permute-start(f32[3,1,16]{2,1,0:T(1,128)S(1)} %bitcast.21), channel_id=1, source_target_pairs={{0,1},{1,0},{2,3},{3,2},{4,5},{5,4},{6,7},{7,6},{8,9},{9,8},{10,11... | collective-permute-start | bytes 584 | tf_op jit(solution)/shard_map/ppermute | solution.py:333
  17.4 0.6 copy-start.13
  17.4 0.6 copy-start.14
  26.3 16.1 %copy-start.12 = (f32[1,3,16]{2,0,1:T(1,128)S(1)}, f32[1,3,16]{2,0,1:T(1,128)}, u32[]{:S(2)}) copy-start(f32[1,3,16]{2,0,1:T(1,128)} %param.36) | copy-start | bytes 580
  32.3 0.7 copy-start
  35.0 24.8 %all-to-all-start.1 = ((bf16[16,272,128]{2,1,0:T(8,128)(2,1)}), bf16[16,272,128]{2,1,0:T(8,128)(2,1)S(1)}, u32[]{:S(2)}, u32[]{:S(2)}) async-start(bf16[16,272,128]{2,1,0:T(8,128)(2,1)} %get-tuple-element.16), calls=%async_computation.1 | async-start | bytes 2228224 | tf_op jit(solution)/shard_map/all_to_all | solution.py:337
  42.4 1.2 collective-permute-start.4
  43.7 0.6 copy-start.15
  59.8 1.0 copy-start.2
  67.5 5.2 %copy-start.4 = (bf16[1,2048,384]{2,1,0:T(8,128)(2,1)S(1)}, bf16[1,2048,384]{2,1,0:T(8,128)(2,1)}, u32[]{:S(2)}) copy-start(bf16[1,2048,384]{2,1,0:T(8,128)(2,1)} %g0.3) | copy-start | bytes 4718596
  67.5 19.4 %all-to-all-start.2 = ((bf16[16,256,128]{2,1,0:T(8,128)(2,1)}), bf16[16,256,128]{2,1,0:T(8,128)(2,1)S(1)}, u32[]{:S(2)}, u32[]{:S(2)}) async-start(bf16[16,256,128]{2,1,0:T(8,128)(2,1)} %experts.1), calls=%async_computation.2 | async-start | bytes 2097152 | tf_op jit(solution)/shard_map/all_to_all | solution.py:337
  72.5 19.2 %copy-start.6 = (bf16[1,384,1024]{2,1,0:T(8,128)(2,1)S(1)}, bf16[1,384,1024]{2,1,0:T(8,128)(2,1)}, u32[]{:S(2)}) copy-start(bf16[1,384,1024]{2,1,0:T(8,128)(2,1)} %d0.3) | copy-start | bytes 2359300
  72.5 40.7 %collective-permute-start.10 = (bf16[1,2048,384]{2,1,0:T(8,128)(2,1)}, bf16[1,2048,384]{2,1,0:T(8,128)(2,1)}, u32[]{:S(2)}, u32[]{:S(2)}) collective-permute-start(bf16[1,2048,384]{2,1,0:T(8,128)(2,1)} %u0.3), channel_id=1, source_target_pairs={{0,1},{1,0},{2,3},{3,2},{4,5},{5,4},{6,7},{7,6},{8,9},{9,8},{10,11... | collective-permute-start | bytes 4718600 | tf_op jit(solution)/shard_map/ppermute | solution.py:333
  72.6 40.6 %collective-permute-start.9 = (bf16[1,2048,384]{2,1,0:T(8,128)(2,1)S(1)}, bf16[1,2048,384]{2,1,0:T(8,128)(2,1)}, u32[]{:S(2)}, u32[]{:S(2)}) collective-permute-start(bf16[1,2048,384]{2,1,0:T(8,128)(2,1)S(1)} %copy-done.4), channel_id=1, source_target_pairs={{0,1},{1,0},{2,3},{3,2},{4,5},{5,4},{6,7},{7,6},{8,9},{9,8},{10,11... | collective-permute-start | bytes 4718600 | tf_op jit(solution)/shard_map/ppermute | solution.py:333
  88.2 18.6 %all-to-all-start.3 = ((bf16[8,256,128]{2,1,0:T(8,128)(2,1)}), bf16[8,256,128]{2,1,0:T(8,128)(2,1)S(1)}, u32[]{:S(2)}, u32[]{:S(2)}) async-start(bf16[8,256,128]{2,1,0:T(8,128)(2,1)} %partial.1), calls=%async_computation.3 | async-start | bytes 1048576 | tf_op jit(solution)/shard_map/all_to_all | solution.py:337
  91.7 21.2 %collective-permute-start.11 = (bf16[1,384,1024]{2,1,0:T(8,128)(2,1)S(1)}, bf16[1,384,1024]{2,1,0:T(8,128)(2,1)}, u32[]{:S(2)}, u32[]{:S(2)}) collective-permute-start(bf16[1,384,1024]{2,1,0:T(8,128)(2,1)S(1)} %copy-done.6), channel_id=1, source_target_pairs={{0,1},{1,0},{2,3},{3,2},{4,5},{5,4},{6,7},{7,6},{8,9},{9,8},{10,11... | collective-permute-start | bytes 2359304 | tf_op jit(solution)/shard_map/ppermute | solution.py:333
  106.8 0.8 copy-start.3
  109.6 4.6 %collective-permute-start.6 = (bf16[288,128]{1,0:T(8,128)(2,1)}, bf16[288,128]{1,0:T(8,128)(2,1)S(1)}, u32[]{:S(2)}, u32[]{:S(2)}) collective-permute-start(bf16[288,128]{1,0:T(8,128)(2,1)} %get-tuple-element.22.m0), channel_id=1, source_target_pairs={{0,2},{2,4},{4,6},{6,0},{1,3},{3,5},{5,7},{7,1},{8,10},{10,12},{12... | collective-permute-start | bytes 221192 | tf_op jit(solution)/shard_map/ppermute | solution.py:463
  110.0 6.1 %collective-permute-start.7 = (bf16[288,128]{1,0:T(8,128)(2,1)}, bf16[288,128]{1,0:T(8,128)(2,1)S(1)}, u32[]{:S(2)}, u32[]{:S(2)}) collective-permute-start(bf16[288,128]{1,0:T(8,128)(2,1)} %get-tuple-element.22.m0), channel_id=1, source_target_pairs={{0,4},{2,6},{4,0},{6,2},{1,5},{3,7},{5,1},{7,3},{8,12},{10,14},{12... | collective-permute-start | bytes 221192 | tf_op jit(solution)/shard_map/ppermute | solution.py:463
  113.0 4.6 %collective-permute-start.8 = (bf16[288,128]{1,0:T(8,128)(2,1)}, bf16[288,128]{1,0:T(8,128)(2,1)S(1)}, u32[]{:S(2)}, u32[]{:S(2)}) collective-permute-start(bf16[288,128]{1,0:T(8,128)(2,1)} %get-tuple-element.22.m0), channel_id=1, source_target_pairs={{0,6},{2,0},{4,2},{6,4},{1,7},{3,1},{5,3},{7,5},{8,14},{10,8},{12,... | collective-permute-start | bytes 221192 | tf_op jit(solution)/shard_map/ppermute | solution.py:463
  114.1 3.4 %copy-start.7 = (bf16[288,128]{1,0:T(8,128)(2,1)}, bf16[288,128]{1,0:T(8,128)(2,1)S(1)}, u32[]{:S(2)}) copy-start(bf16[288,128]{1,0:T(8,128)(2,1)S(1)} %collective-permute-done.6.m1) | copy-start | bytes 221188
  116.0 1.5 %copy-start.8 = (bf16[288,128]{1,0:T(8,128)(2,1)}, bf16[288,128]{1,0:T(8,128)(2,1)S(1)}, u32[]{:S(2)}) copy-start(bf16[288,128]{1,0:T(8,128)(2,1)S(1)} %collective-permute-done.7.m2) | copy-start | bytes 221188
  117.5 0.6 copy-start.9
  118.2 31.0 %copy-start.1 = (s32[16]{0:T(128)S(1)}, s32[16]{0:T(128)}, u32[]{:S(2)}) copy-start(s32[16]{0:T(128)} %param.39) | copy-start | bytes 196

commit v3 on v0

v3 whole, which is shorter than its diff:
```python
import jax
import jax.numpy as jnp
from jax import lax
from jax.experimental import pallas as pl
from jax.experimental.pallas import tpu as pltpu
from jax.sharding import Mesh
from jax.sharding import PartitionSpec as P

HEADS = 16
HEAD_DIM = 128
BLK = 128
CHIPS = 128
LANES = 128
ROWS = 16
CTX = 128
D = 2048
FH = 384
TD = 1024
EPSILON = 1e-06
MSG = 40
INFO_ROW = 32
TWIDE = (D + 2 * LANES) // LANES * ROWS

f32 = jnp.float32
bf16 = jnp.bfloat16
VM = pl.BlockSpec(memory_space=pltpu.VMEM)
SM = pl.BlockSpec(memory_space=pltpu.SMEM)
HB = pl.BlockSpec(memory_space=pl.ANY)


def tile(h, rows=ROWS):
    return slice(h * rows, (h + 1) * rows)


def lane_iota(rows):
    return lax.broadcasted_iota(jnp.int32, (rows, LANES), 1)


def slots(ids):
    expert = lax.broadcasted_iota(jnp.int32, (LANES, ROWS), 0)
    picked = jnp.zeros((LANES, ROWS), f32)
    for k in range(ids.shape[0]):
        picked = picked + jnp.where(ids[k : k + 1, :] == expert, 1.0, 0.0)
    before = lax.broadcasted_iota(jnp.int32, (ROWS, ROWS), 0) < lax.broadcasted_iota(
        jnp.int32, (ROWS, ROWS), 1
    )
    rank = jnp.dot(
        picked.astype(bf16), jnp.where(before, 1.0, 0.0).astype(bf16), preferred_element_type=f32
    )
    first = jnp.where((picked > 0.5) & (rank < 0.5), 1.0, 0.0)
    second = jnp.where((picked > 0.5) & (rank > 0.5) & (rank < 1.5), 1.0, 0.0)
    return first, second


def high_low(values):
    high = values.astype(bf16)
    low = (values - high.astype(f32)).astype(bf16)
    return high, low


def gather_t(onehot, values):
    return lax.dot_general(
        onehot, values, (((0,), (0,)), ((), ())), preferred_element_type=f32
    )


def attend_kernel(
    hidden, queries, cache_key, cache_value, new_key, new_value, lengths, gain, ids, source, talk_ids, talk_gates, residual, message, asked, fresh_key, fresh_value,
    mixed, probs, spread_out, keys, vals, sems,
):
    k_copy = pltpu.make_async_copy(cache_key, keys, sems.at[0])
    v_copy = pltpu.make_async_copy(cache_value, vals, sems.at[1])
    k_copy.start()
    v_copy.start()
    scaling = HEAD_DIM ** (-0.5)
    for h in range(HEADS):
        spot = pl.ds(h, ROWS, stride=HEADS)
        group = slice(h // 8 * 128, (h // 8 + 1) * 128)
        asked[spot, :] = queries[:, h * 128 : (h + 1) * 128].astype(f32)
        fresh_key[spot, :] = new_key[:, group].astype(f32)
        fresh_value[spot, :] = new_value[:, group].astype(f32)
    front = lax.broadcasted_iota(jnp.int32, (HEADS, LANES), 0) < HEADS // 2
    lane = lane_iota(HEADS)
    fresh = jnp.sum(asked[...] * fresh_key[...], axis=1, keepdims=True) * scaling
    k_copy.wait()
    for r in range(ROWS):
        rows = slice(r * HEADS, (r + 1) * HEADS)
        query = asked[rows, :]
        split = jnp.concatenate(
            [jnp.where(front, query, 0.0), jnp.where(front, 0.0, query)], axis=1
        ).astype(bf16)
        found = lax.dot_general(
            split, keys[r], (((1,), (1,)), ((), ())), preferred_element_type=f32
        )
        mixed[rows, :] = jnp.where(lane < lengths[r], found * scaling, -jnp.inf)
    scores = mixed[...]
    highest = jnp.maximum(jnp.max(scores, axis=1, keepdims=True), fresh)
    weights = jnp.exp(scores - highest)
    own = jnp.exp(fresh - highest)
    total = jnp.sum(weights, axis=1, keepdims=True) + own
    probs[...] = (weights / total).astype(bf16)
    added = (own / total).astype(bf16).astype(f32) * fresh_value[...]
    v_copy.wait()
    for r in range(ROWS):
        rows = slice(r * HEADS, (r + 1) * HEADS)
        both = jnp.dot(probs[rows, :], vals[r], preferred_element_type=f32)
        mixed[rows, :] = jnp.where(front, both[:, :128], both[:, 128:])
    mixed[...] = mixed[...] + added
    squares = jnp.zeros((ROWS, LANES), f32)
    for h in range(HEADS):
        cols = slice(h * 128, (h + 1) * 128)
        part = hidden[:, cols].astype(f32) + mixed[pl.ds(h, ROWS, stride=HEADS), :]
        residual[:, cols] = part
        squares = squares + part * part
    spread = jnp.sum(squares, axis=1, keepdims=True) * (1.0 / D)
    scale = lax.rsqrt(spread + EPSILON)
    first, second = slots(ids[...])
    both_slots = jnp.concatenate([first, second], axis=0).astype(bf16)
    for h in range(HEADS // 2):
        pair = []
        for k in range(2):
            cols = slice((2 * h + k) * 128, (2 * h + k + 1) * 128)
            line = gain[2 * h + k : 2 * h + k + 1, :].astype(f32)
            pair.append((residual[:, cols] * scale * line).astype(bf16))
        sent = jnp.dot(both_slots, jnp.concatenate(pair, axis=1), preferred_element_type=f32)
        for k in range(2):
            cols = slice(k * 128, (k + 1) * 128)
            spread_out[pl.ds(2 * h + k, CHIPS, stride=32), :] = sent[:CHIPS, cols]
            spread_out[pl.ds(HEADS + 2 * h + k, CHIPS, stride=32), :] = sent[CHIPS:, cols]
    message[:, :INFO_ROW, :] = spread_out[...].reshape(CHIPS, 32, LANES).astype(bf16)
    origin = source[...]
    chip = lax.broadcasted_iota(jnp.int32, (CHIPS, ROWS), 0)
    onehot = jnp.where((origin // 32) == chip, 1.0, 0.0).astype(bf16)
    gates = talk_gates[...]
    high = gates.astype(bf16).astype(f32)
    low = gates - high
    fact = lax.broadcasted_iota(jnp.int32, (LANES, ROWS), 0)
    facts = jnp.where(fact == 16 + origin % ROWS, 1.0, 0.0)
    for k in range(2):
        chosen = talk_ids[k : k + 1, :]
        facts = facts + jnp.where(fact == chosen, high[k : k + 1, :], 0.0)
        facts = facts + jnp.where(fact == chosen + 8, low[k : k + 1, :], 0.0)
    told = lax.dot_general(
        onehot, facts.astype(bf16), (((1,), (1,)), ((), ())), preferred_element_type=f32
    )
    message[:, INFO_ROW:, :] = jnp.broadcast_to(
        told.reshape(CHIPS, 1, LANES), (CHIPS, MSG - INFO_ROW, LANES)
    ).astype(bf16)


def silu(x):
    return x * jax.nn.sigmoid(x)


def scaled(block, scale):
    return (block.astype(f32) * scale).astype(bf16)


def restore_tall_kernel(gs0, us0, gs1, us1, g0, u0, g1, u1, gw, uw):
    i = pl.program_id(0)
    for half, (gs, us, g, u) in enumerate([(gs0, us0, g0, u0), (gs1, us1, g1, u1)]):
        for j in range(FH // BLK):
            cols = slice(j * BLK, (j + 1) * BLK)
            there = slice(half * FH + j * BLK, half * FH + (j + 1) * BLK)
            for k in range(2):
                near = slice(k * BLK, (k + 1) * BLK)
                gw[near, there] = scaled(g[0, near, cols], gs[j, 0, 2 * i + k])
                uw[near, there] = scaled(u[0, near, cols], us[j, 0, 2 * i + k])


def restore_flat_kernel(ds0, ds1, d0, d1, dw):
    i = pl.program_id(0)
    for half, (ds, d) in enumerate([(ds0, d0), (ds1, d1)]):
        for j in range(FH // BLK):
            rows = slice(j * BLK, (j + 1) * BLK)
            there = slice(half * FH + j * BLK, half * FH + (j + 1) * BLK)
            for k in range(4):
                near = slice(k * BLK, (k + 1) * BLK)
                dw[there, near] = scaled(d[0, rows, near], ds[j, 0, 4 * i + k])


def expert_kernel(arrived, g, u, d, produced, message, wide_in, rows_in, gw, uw, dw, out32, sems):
    copies = []
    for i, (src, dst) in enumerate([(arrived, message), (g, gw), (u, uw), (d, dw)]):
        copy = pltpu.make_async_copy(src, dst, sems.at[i])
        copy.start()
        copies.append(copy)
    copies[0].wait()
    wide_in[...] = message[:, :INFO_ROW, :].astype(f32).reshape(CHIPS * 32, LANES)
    for s in range(2):
        for h in range(HEADS):
            rows_in[s * CHIPS : (s + 1) * CHIPS, h * 128 : (h + 1) * 128] = wide_in[
                pl.ds(s * HEADS + h, CHIPS, stride=32), :
            ].astype(bf16)
    copies[1].wait()
    gated = jnp.dot(rows_in[...], gw[...], preferred_element_type=f32)
    copies[2].wait()
    lifted = jnp.dot(rows_in[...], uw[...], preferred_element_type=f32)
    middle = (silu(gated) * lifted).astype(bf16)
    copies[3].wait()
    for h in range(HEADS // 2):
        part = jnp.dot(middle, dw[:, h * 256 : (h + 1) * 256], preferred_element_type=f32)
        for s in range(2):
            for k in range(2):
                spot = pl.ds(s * HEADS + 2 * h + k, CHIPS, stride=32)
                out32[spot, :] = part[s * CHIPS : (s + 1) * CHIPS, k * 128 : (k + 1) * 128]
    produced[...] = out32[...].reshape(CHIPS, 32, LANES).astype(bf16)


def combine_kernel(
    returned, residual, ids, gates, owned, gain, thinker_out, onward, wide_in, rows_in, facts_in,
):
    wide_in[...] = returned[...].astype(f32).reshape(CHIPS * 32, LANES)
    facts_in[...] = owned[...].astype(f32).reshape(CHIPS * 8, LANES)
    for s in range(2):
        for h in range(HEADS):
            rows_in[s * CHIPS : (s + 1) * CHIPS, h * 128 : (h + 1) * 128] = wide_in[
                pl.ds(s * HEADS + h, CHIPS, stride=32), :
            ].astype(bf16)
    expert = lax.broadcasted_iota(jnp.int32, (LANES, ROWS), 0)
    weight = jnp.zeros((LANES, ROWS), f32)
    for k in range(8):
        weight = weight + jnp.where(ids[k : k + 1, :] == expert, gates[k : k + 1, :], 0.0)
    first, second = slots(ids[...])
    high, low = high_low(jnp.concatenate([first * weight, second * weight], axis=0))
    both = gather_t(jnp.concatenate([high, low], axis=1), rows_in[...])
    outcome = (residual[...] + both[:ROWS] + both[ROWS:]).astype(bf16)
    thinker_out[...] = outcome
    values = outcome.astype(f32)
    scale = lax.rsqrt(
        jnp.sum(values * values, axis=1, keepdims=True) * (1.0 / D) + EPSILON
    )
    for h in range(HEADS):
        part = values[:, h * 128 : (h + 1) * 128]
        onward[tile(h), :] = (part * scale * gain[h : h + 1, :].astype(f32)).astype(bf16)
    told = facts_in[pl.ds(0, CHIPS, stride=8), :].astype(bf16)
    pick = jnp.where(
        lane_iota(ROWS) == 16 + lax.broadcasted_iota(jnp.int32, (ROWS, LANES), 0), 1.0, 0.0
    ).astype(bf16)
    goal = lax.dot_general(
        pick, told, (((1,), (1,)), ((), ())), preferred_element_type=f32
    ).astype(bf16)
    onward[tile(HEADS), :] = goal
    onward[tile(HEADS + 1), :] = jnp.dot(goal, told, preferred_element_type=f32).astype(bf16)


def talker_kernel(
    place, m0, m1, m2, m3, g0, u0, d0, g1, u1, d1, relayed, rows_in, gw, uw, dw, out32, sems,
):
    copies = []
    for i, (src, dst) in enumerate(
        [
            (g0, gw.at[0]), (u0, uw.at[0]), (d0, dw.at[0]),
            (g1, gw.at[1]), (u1, uw.at[1]), (d1, dw.at[1]),
        ]
    ):
        copy = pltpu.make_async_copy(src.at[0], dst, sems.at[i])
        copy.start()
        copies.append(copy)
    for i, m in enumerate([m0, m1, m2, m3]):
        for h in range(HEADS + 2):
            rows_in[tile(i), h * 128 : (h + 1) * 128] = m[tile(h), :]
    inputs = rows_in[:, :D]
    goal = rows_in[:, D : D + LANES]
    shares = rows_in[:, D + LANES :].astype(f32)
    lane = lane_iota(4 * ROWS)
    total = jnp.zeros((4 * ROWS, TD), f32)
    for half in range(2):
        expert = place[0] if half == 0 else place[0] + 1 - 2 * (place[0] % 2)
        share = jnp.sum(
            jnp.where((lane == expert) | (lane == expert + 8), shares, 0.0), axis=1, keepdims=True
        )
        copies[3 * half].wait()
        gated = jnp.dot(inputs, gw[half], preferred_element_type=f32)
        copies[3 * half + 1].wait()
        lifted = jnp.dot(inputs, uw[half], preferred_element_type=f32)
        middle = (silu(gated) * lifted).astype(bf16)
        copies[3 * half + 2].wait()
        part = jnp.dot(middle, dw[half], preferred_element_type=f32)
        total = total + share * part.astype(bf16).astype(f32)
    sent = gather_t(goal, total.astype(bf16))
    for h in range(TD // 128):
        out32[pl.ds(h, CHIPS, stride=8), :] = sent[:, h * 128 : (h + 1) * 128]
    relayed[...] = out32[...].reshape(CHIPS, 8, LANES).astype(bf16)


def settle_kernel(returned, source, talker_out, wide_in):
    wide_in[...] = returned[...].astype(f32).reshape(CHIPS * 8, LANES)
    came = lax.broadcasted_iota(jnp.int32, (CHIPS, ROWS), 0)
    pick = jnp.where((came // 4) == (source[...] // 128), 1.0, 0.0).astype(bf16)
    for h in range(TD // 128):
        rows = wide_in[pl.ds(h, CHIPS, stride=8), :].astype(bf16)
        talker_out[:, h * 128 : (h + 1) * 128] = gather_t(pick, rows).astype(bf16)


def sds(shape, dtype):
    return jax.ShapeDtypeStruct(shape, dtype)


def swap(value):
    return lax.ppermute(value, "c", [(0, 1), (1, 0)])


def exchange(value, axes):
    return lax.all_to_all(value, axes, 0, 0, tiled=True)


CHIP_AXES = ("z", "x", "y")
SMALL = pltpu.CompilerParams(vmem_limit_bytes=24 << 20)


def local(
    hidden_in, queries, cache_key, cache_value, new_key, new_value, lengths, norm_gain,
    gate_codes, gate_scale, up_codes, up_scale, down_codes, down_scale, think_ids, think_gates,
    talker_source, talker_gain, talk_gate_w, talk_up_w, talk_down_w, talk_ids, talk_gates,
):
    own = (gate_codes, up_codes, down_codes)
    own_scale = (
        jnp.transpose(gate_scale, (2, 0, 1)),
        jnp.transpose(up_scale, (2, 0, 1)),
        jnp.transpose(down_scale, (1, 0, 2)),
    )
    other = tuple(swap(w) for w in own)
    other_scale = tuple(swap(s) for s in own_scale)
    source = talker_source.reshape(1, ROWS)

    residual, message = pl.pallas_call(
        attend_kernel,
        out_shape=(sds((ROWS, D), f32), sds((CHIPS, MSG, LANES), bf16)),
        in_specs=[VM] * 2 + [HB] * 2 + [VM] * 2 + [SM] + [VM] * 5,
        out_specs=(VM, VM),
        scratch_shapes=[
            pltpu.VMEM((ROWS * HEADS, LANES), f32),
            pltpu.VMEM((ROWS * HEADS, LANES), f32),
            pltpu.VMEM((ROWS * HEADS, LANES), f32),
            pltpu.VMEM((ROWS * HEADS, LANES), f32),
            pltpu.VMEM((ROWS * HEADS, LANES), bf16),
            pltpu.VMEM((CHIPS * 32, LANES), f32),
            pltpu.VMEM((ROWS, CTX, 256), bf16),
            pltpu.VMEM((ROWS, CTX, 256), bf16),
            pltpu.SemaphoreType.DMA((2,)),
        ],
        name="attend",
    )(
        hidden_in, queries, cache_key, cache_value, new_key, new_value, lengths,
        norm_gain.reshape(HEADS, LANES), think_ids.T, source, talk_ids.T, talk_gates.T,
    )
    arrived = exchange(message, CHIP_AXES)
    tall = pl.BlockSpec((1, 2 * BLK, FH), lambda i: (0, i, 0))
    tall_out = pl.BlockSpec((2 * BLK, 2 * FH), lambda i: (i, 0))
    gate_dense, up_dense = pl.pallas_call(
        restore_tall_kernel,
        grid=(D // BLK // 2,),
        out_shape=(sds((D, 2 * FH), bf16), sds((D, 2 * FH), bf16)),
        in_specs=[SM] * 4 + [tall] * 4,
        out_specs=(tall_out, tall_out),
        cost_estimate=pl.CostEstimate(
            flops=4 * D * FH, bytes_accessed=16 * D * FH, transcendentals=0
        ),
        name="restore_tall",
    )(*own_scale[:2], *other_scale[:2], *own[:2], *other[:2])
    flat = pl.BlockSpec((1, FH, 4 * BLK), lambda i: (0, 0, i))
    flat_out = pl.BlockSpec((2 * FH, 4 * BLK), lambda i: (0, i))
    down_dense = pl.pallas_call(
        restore_flat_kernel,
        grid=(D // BLK // 4,),
        out_shape=sds((2 * FH, D), bf16),
        in_specs=[SM] * 2 + [flat] * 2,
        out_specs=flat_out,
        cost_estimate=pl.CostEstimate(
            flops=2 * D * FH, bytes_accessed=8 * D * FH, transcendentals=0
        ),
        name="restore_flat",
    )(own_scale[2], other_scale[2], own[2], other[2])
    produced = pl.pallas_call(
        expert_kernel,
        out_shape=sds((CHIPS, 32, LANES), bf16),
        in_specs=[HB] * 4,
        out_specs=VM,
        scratch_shapes=[
            pltpu.VMEM((CHIPS, MSG, LANES), bf16),
            pltpu.VMEM((CHIPS * 32, LANES), f32),
            pltpu.VMEM((2 * CHIPS, D), bf16),
            pltpu.VMEM((D, 2 * FH), bf16),
            pltpu.VMEM((D, 2 * FH), bf16),
            pltpu.VMEM((2 * FH, D), bf16),
            pltpu.VMEM((CHIPS * 32, LANES), f32),
            pltpu.SemaphoreType.DMA((4,)),
        ],
        name="experts",
    )(arrived, gate_dense, up_dense, down_dense)
    returned = exchange(produced, CHIP_AXES)
    talk_own = (talk_gate_w, talk_up_w, talk_down_w)
    talk_held = lax.optimization_barrier((*talk_own, arrived))[:3]
    talk_other = tuple(swap(w) for w in talk_held)
    whole = lambda i: (0, 0)
    thinker_out, onward = pl.pallas_call(
        combine_kernel,
        grid=(1,),
        out_shape=(sds((ROWS, D), bf16), sds((TWIDE, LANES), bf16)),
        in_specs=[
            pl.BlockSpec((CHIPS, 32, LANES), lambda i: (0, 0, 0)),
            pl.BlockSpec((ROWS, D), whole),
            pl.BlockSpec((8, ROWS), whole),
            pl.BlockSpec((8, ROWS), whole),
            pl.BlockSpec((CHIPS, 8, LANES), lambda i: (0, INFO_ROW // 8, 0)),
            pl.BlockSpec((HEADS, LANES), whole),
        ],
        out_specs=(pl.BlockSpec((ROWS, D), whole), pl.BlockSpec((TWIDE, LANES), whole)),
        scratch_shapes=[
            pltpu.VMEM((CHIPS * 32, LANES), f32),
            pltpu.VMEM((2 * CHIPS, D), bf16),
            pltpu.VMEM((CHIPS * 8, LANES), f32),
        ],
        name="combine",
    )(
        returned, residual, think_ids.T, think_gates.T, arrived,
        talker_gain.reshape(HEADS, LANES),
    )
    peers = [
        lax.ppermute(onward, "y", [(i, (i + o) % 4) for i in range(4)]) for o in (1, 2, 3)
    ]
    place = (lax.axis_index("y") * 2 + lax.axis_index("c")).astype(jnp.int32).reshape(1)
    relayed = pl.pallas_call(
        talker_kernel,
        out_shape=sds((CHIPS, 8, LANES), bf16),
        in_specs=[SM] + [VM] * 4 + [HB] * 6,
        out_specs=VM,
        scratch_shapes=[
            pltpu.VMEM((4 * ROWS, D + 2 * LANES), bf16),
            pltpu.VMEM((2, D, FH), bf16),
            pltpu.VMEM((2, D, FH), bf16),
            pltpu.VMEM((2, FH, TD), bf16),
            pltpu.VMEM((CHIPS * 8, LANES), f32),
            pltpu.SemaphoreType.DMA((6,)),
        ],
        name="talkers",
    )(place, onward, *peers, *talk_own, *talk_other)
    settled = exchange(relayed, CHIP_AXES)
    talker_out = pl.pallas_call(
        settle_kernel,
        out_shape=sds((ROWS, TD), bf16),
        in_specs=[VM, VM],
        out_specs=VM,
        scratch_shapes=[pltpu.VMEM((CHIPS * 8, LANES), f32)],
        compiler_params=SMALL,
        name="settle",
    )(settled, source)
    return (thinker_out, talker_out)


def solution(mesh):
    fine = Mesh(mesh.devices.reshape(8, 4, 4, 2), ("z", "x", "y", "c"))
    every = ("z", "x", "y", "c")
    two = P(every, None)
    three = P(every, None, None)
    talk = P(("y", "c"), None, None)
    return jax.shard_map(
        local,
        mesh=fine,
        in_specs=(
            two, two, three, three, two, two, P(every), P(),
            three, three, three, three, three, three, two, two,
            P(every), P(), talk, talk, talk, two, two,
        ),
        out_specs=(two, two),
        check_vma=False,
    )
```

time: 153 us -> 147 us (0.961)
  the two profiles are of different devices: /device:TPU:2 before, /device:TPU:1 now
where the time goes in v3:
time: 147 us; the launch traced here: 144 us
  waiting for transfers between devices  47.1 us (32%)
  Pallas kernels  38 us (26%)
  starting transfers between devices  32.2 us (22%)
  blocking collectives  22.3 us (15%)
  local copies, waits for them, and re-layouts  3.39 us (2%)
    all_to_all x2, waiting for transfers between devices, exchange(): return lax.all_to_all(value, axes, 0, 0, tiled=True)  37.1 us
    all_to_all x2, starting transfers between devices, exchange(): return lax.all_to_all(value, axes, 0, 0, tiled=True)  24.8 us
    all_to_all x1, blocking collectives, exchange(): return lax.all_to_all(value, axes, 0, 0, tiled=True)  22.3 us
    pallas_call x1, Pallas kernels, local(): pl.pallas_call(expert_kernel, out_shape=sds((CHIPS, 32, LANES), bf16), in...  8.81 us
    pallas_call x1, Pallas kernels, local(): pl.pallas_call(restore_tall_kernel, grid=(D // BLK // 2,), out_shape=(sds...  8.32 us
    ppermute x9, waiting for transfers between devices, swap(): return lax.ppermute(value, 'c', [(0, 1), (1, 0)])  6.66 us
    pallas_call x1, Pallas kernels, local(): pl.pallas_call(talker_kernel, out_shape=sds((CHIPS, 8, LANES), bf16), in_...  5.74 us
    pallas_call x1, Pallas kernels, local(): pl.pallas_call(attend_kernel, out_shape=(sds((ROWS, D), f32), sds((CHIPS,...  5.72 us
  transfers between devices with their start and end apart: 14, of which 5 were waited for; matrix products, arithmetic and copies ran while one was open for 0% of the time, Pallas kernels for 12%

profile of v3, /device:TPU:1, one launch (start us, length us, event | category | flops | bytes accessed | tf_op | source)
XLA Modules:
  0.0 143.7 jit_solution(6147309882221689144)
XLA Ops:
  0.6 5.7 %attend.1 = (f32[16,2048]{1,0:T(8,128)}, bf16[128,40,128]{2,1,0:T(8,128)(2,1)}) custom-call(bf16[16,2048]{1,0:T(8,128)(2,1)} %hidden.1, bf16[16,2048]{1,0:T(8,128)(2,1)} %queries.1, bf16[16,128,256]{2,1,0:T(8,128)(2,1)} %cache_key.1, bf16[16,128,256]{2,1,0:T(8,128)(2,1)} %cache_value.1, bf16[16,256]{1,0:T(8,128)(2,1)} %new_key.1, bf16[16,256]{1,0:T(8,128)(2,1)} %new_value.1, ...), custom_call_target="tpu_custom_call" | custom-call | tf_op jit(solution)/shard_map/attend/pallas_call | solution.py:327
  6.4 0.0 copy-start.4
  6.4 0.0 copy-start.9
  6.4 0.0 copy-start.10
  6.4 0.0 copy-start.11
  6.4 16.5 %all-to-all-start = ((bf16[128,40,128]{2,1,0:T(8,128)(2,1)}), bf16[128,40,128]{2,1,0:T(8,128)(2,1)S(1)}, u32[]{:S(2)}, u32[]{:S(2)}) async-start(bf16[128,40,128]{2,1,0:T(8,128)(2,1)} %get-tuple-element.11), calls=%async_computation | async-start | bytes 2621440 | tf_op jit(solution)/shard_map/all_to_all | solution.py:305
  22.9 1.0 collective-permute-start.5
  23.9 0.1 collective-permute-start.2
  24.0 0.4 collective-permute-start.3
  24.5 0.1 collective-permute-start.4
  24.6 0.4 collective-permute-start
  25.0 6.6 %collective-permute-done.4.ds1 = f32[3,1,16]{2,1,0:T(1,128)S(1)} collective-permute-done((f32[3,1,16]{2,1,0:T(1,128)S(1)}, f32[3,1,16]{2,1,0:T(1,128)S(1)}, u32[]{:S(2)}, u32[]{:S(2)}) %collective-permute-start.4) | collective-permute-done | bytes 224 | tf_op jit(solution)/shard_map/ppermute | solution.py:301
  31.6 0.4 collective-permute-start.1
  32.0 0.0 collective-permute-done.5.d1
  32.0 0.2 copy-done.14
  32.2 4.5 %restore_flat.1.d = bf16[768,2048]{1,0:T(8,128)(2,1)} custom-call(f32[3,1,16]{2,1,0:T(1,128)} %bitcast.18, f32[3,1,16]{2,1,0:T(1,128)} %copy-done.14, bf16[1,384,2048]{2,1,0:T(8,128)(2,1)} %d0.2, bf16[1,384,2048]{2,1,0:T(8,128)(2,1)} %collective-permute-done.5.d1), custom_call_target="tpu_custom_call" | custom-call | flops 1572864 | bytes 6291456 | tf_op jit(solution)/shard_map/restore_flat/pallas_call | solution.py:364
  36.7 0.0 collective-permute-done.gs1
  36.7 0.0 collective-permute-done.1.us1
  36.7 0.0 copy-start.13
  36.7 0.0 collective-permute-done.2.g1
  36.7 0.0 collective-permute-done.3.u1
  36.7 0.5 copy-done.12
  37.2 0.0 copy-done.13
  37.3 8.3 %restore_tall.1 = (bf16[2048,768]{1,0:T(8,128)(2,1)}, bf16[2048,768]{1,0:T(8,128)(2,1)}) custom-call(f32[3,1,16]{2,1,0:T(1,128)} %bitcast.20, f32[3,1,16]{2,1,0:T(1,128)} %bitcast.22, f32[3,1,16]{2,1,0:T(1,128)} %copy-done.12, f32[3,1,16]{2,1,0:T(1,128)} %copy-done.13, bf16[1,2048,384]{2,1,0:T(8,128)(2,1)} %g0.2, bf16[1,2048,384]{2,1,0:T(8,128)(2,1)} %u0.2, ...), custom_call_target="tpu_custom_call" | custom-call | flops 3145728 | bytes 12582912 | tf_op jit(solution)/shard_map/restore_tall/pallas_call | solution.py:351
  45.6 11.4 %all-to-all-done.arrived.owned = bf16[128,40,128]{2,1,0:T(8,128)(2,1)S(1)} async-done(((bf16[128,40,128]{2,1,0:T(8,128)(2,1)}), bf16[128,40,128]{2,1,0:T(8,128)(2,1)S(1)}, u32[]{:S(2)}, u32[]{:S(2)}) %all-to-all-start) | async-done | bytes 1310752 | tf_op jit(solution)/shard_map/all_to_all | solution.py:305
  57.0 1.0 copy-done.1
  58.0 8.8 %experts.1 = bf16[128,32,128]{2,1,0:T(8,128)(2,1)} custom-call(bf16[128,40,128]{2,1,0:T(8,128)(2,1)} %copy-done.1, bf16[2048,768]{1,0:T(8,128)(2,1)} %get-tuple-element.12.g, bf16[2048,768]{1,0:T(8,128)(2,1)} %get-tuple-element.13.u, bf16[768,2048]{1,0:T(8,128)(2,1)} %restore_flat.1.d), custom_call_target="tpu_custom_call" | custom-call | tf_op jit(solution)/shard_map/experts/pallas_call | solution.py:375
  66.9 0.0 copy-start.3
  66.9 8.4 %all-to-all-start.1 = ((bf16[128,32,128]{2,1,0:T(8,128)(2,1)}), bf16[128,32,128]{2,1,0:T(8,128)(2,1)S(1)}, u32[]{:S(2)}, u32[]{:S(2)}) async-start(bf16[128,32,128]{2,1,0:T(8,128)(2,1)} %experts.1), calls=%async_computation.1 | async-start | bytes 2097152 | tf_op jit(solution)/shard_map/all_to_all | solution.py:305
  75.2 1.7 %collective-permute-start.10 = (bf16[1,2048,384]{2,1,0:T(8,128)(2,1)}, bf16[1,2048,384]{2,1,0:T(8,128)(2,1)}, u32[]{:S(2)}, u32[]{:S(2)}) collective-permute-start(bf16[1,2048,384]{2,1,0:T(8,128)(2,1)} %u0.3), channel_id=1, source_target_pairs={{0,1},{1,0},{2,3},{3,2},{4,5},{5,4},{6,7},{7,6},{8,9},{9,8},{10,11... | collective-permute-start | bytes 4718600 | tf_op jit(solution)/shard_map/ppermute | solution.py:301
  77.0 0.1 collective-permute-start.9
  77.1 0.4 collective-permute-start.11
  77.5 25.7 %all-to-all-done.1.returned = bf16[128,32,128]{2,1,0:T(8,128)(2,1)S(1)} async-done(((bf16[128,32,128]{2,1,0:T(8,128)(2,1)}), bf16[128,32,128]{2,1,0:T(8,128)(2,1)S(1)}, u32[]{:S(2)}, u32[]{:S(2)}) %all-to-all-start.1) | async-done | bytes 1048608 | tf_op jit(solution)/shard_map/all_to_all | solution.py:305
  103.2 1.0 copy-done.2
  104.2 4.0 %combine.1 = (bf16[16,2048]{1,0:T(8,128)(2,1)}, bf16[288,128]{1,0:T(8,128)(2,1)}) custom-call(bf16[128,32,128]{2,1,0:T(8,128)(2,1)} %copy-done.2, f32[16,2048]{1,0:T(8,128)} %get-tuple-element.14.residual, s32[8,16]{1,0:T(8,128)} %bitcast.14, f32[8,16]{1,0:T(8,128)} %bitcast.16, bf16[128,40,128]{2,1,0:T(8,128)(2,1)} %copy-done.1, bf16[16,128]{1,0:T(8,128)(2,1)} %bitcast.17), custom_call_target="tpu_custom_call" | custom-call | tf_op jit(solution)/shard_map/combine/pallas_call | solution.py:397
  108.2 0.1 collective-permute-start.6
  108.3 2.2 %collective-permute-start.7 = (bf16[288,128]{1,0:T(8,128)(2,1)}, bf16[288,128]{1,0:T(8,128)(2,1)S(1)}, u32[]{:S(2)}, u32[]{:S(2)}) collective-permute-start(bf16[288,128]{1,0:T(8,128)(2,1)} %get-tuple-element.16.m0), channel_id=1, source_target_pairs={{0,4},{2,6},{4,0},{6,2},{1,5},{3,7},{5,1},{7,3},{8,12},{10,14},{12... | collective-permute-start | bytes 221192 | tf_op jit(solution)/shard_map/ppermute | solution.py:421
  110.6 0.3 collective-permute-start.8
  110.9 0.0 collective-permute-done.10.u1
  110.9 0.0 collective-permute-done.9.g1
  110.9 2.7 %collective-permute-done.6.m1 = bf16[288,128]{1,0:T(8,128)(2,1)S(1)} collective-permute-done((bf16[288,128]{1,0:T(8,128)(2,1)}, bf16[288,128]{1,0:T(8,128)(2,1)S(1)}, u32[]{:S(2)}, u32[]{:S(2)}) %collective-permute-start.6) | collective-permute-done | bytes 73760 | tf_op jit(solution)/shard_map/ppermute | solution.py:421
  113.6 0.6 collective-permute-done.8.m3
  114.2 0.0 copy-done.6
  114.3 0.0 copy-done.7
  114.3 0.5 copy-done.8
  114.8 5.7 %talkers.1 = bf16[128,8,128]{2,1,0:T(8,128)(2,1)} custom-call(s32[1]{0:T(128)} %bitcast.10.place, bf16[288,128]{1,0:T(8,128)(2,1)} %get-tuple-element.16.m0, bf16[288,128]{1,0:T(8,128)(2,1)} %copy-done.6, bf16[288,128]{1,0:T(8,128)(2,1)} %copy-done.7, bf16[288,128]{1,0:T(8,128)(2,1)} %copy-done.8, bf16[1,2048,384]{2,1,0:T(8,128)(2,1)} %g0.3, ...), custom_call_target="tpu_custom_call" | custom-call | tf_op jit(solution)/shard_map/talkers/pallas_call | solution.py:424
  120.6 22.3 %all_to_all.15.returned = bf16[128,8,128]{2,1,0:T(8,128)(2,1)S(1)} all-to-all(bf16[128,8,128]{2,1,0:T(8,128)(2,1)} %talkers.1), channel_id=1, replica_groups=mesh['z'=8,'x'=4,'y'=4,'c'=2] {'z','x','y'}, dimensions={0} | all-to-all | bytes 524288 | tf_op jit(solution)/shard_map/all_to_all | solution.py:305
  142.9 0.8 settle.1
  (18 shorter events, 0.0 us)
Async XLA Ops:
  6.4 16.5 %copy-start.4 = (bf16[1,384,2048]{2,1,0:T(8,128)(2,1)S(1)}, bf16[1,384,2048]{2,1,0:T(8,128)(2,1)}, u32[]{:S(2)}) copy-start(bf16[1,384,2048]{2,1,0:T(8,128)(2,1)} %d0.2) | copy-start | bytes 4718596
  6.4 18.1 %copy-start.9 = (f32[1,3,16]{2,0,1:T(1,128)S(1)}, f32[1,3,16]{2,0,1:T(1,128)}, u32[]{:S(2)}) copy-start(f32[1,3,16]{2,0,1:T(1,128)} %param.36) | copy-start | bytes 580
  6.4 18.2 %copy-start.10 = (f32[1,16,3]{1,0,2:T(1,128)S(1)}, f32[1,16,3]{1,0,2:T(1,128)}, u32[]{:S(2)}) copy-start(f32[1,16,3]{1,0,2:T(1,128)} %param.32) | copy-start | bytes 580
  6.4 25.2 %copy-start.11 = (f32[1,16,3]{1,0,2:T(1,128)S(1)}, f32[1,16,3]{1,0,2:T(1,128)}, u32[]{:S(2)}) copy-start(f32[1,16,3]{1,0,2:T(1,128)} %param.34) | copy-start | bytes 580
  6.4 50.6 %all-to-all-start = ((bf16[128,40,128]{2,1,0:T(8,128)(2,1)}), bf16[128,40,128]{2,1,0:T(8,128)(2,1)S(1)}, u32[]{:S(2)}, u32[]{:S(2)}) async-start(bf16[128,40,128]{2,1,0:T(8,128)(2,1)} %get-tuple-element.11), calls=%async_computation | async-start | bytes 2621440 | tf_op jit(solution)/shard_map/all_to_all | solution.py:305
  22.9 9.1 %collective-permute-start.5 = (bf16[1,384,2048]{2,1,0:T(8,128)(2,1)S(1)}, bf16[1,384,2048]{2,1,0:T(8,128)(2,1)}, u32[]{:S(2)}, u32[]{:S(2)}) collective-permute-start(bf16[1,384,2048]{2,1,0:T(8,128)(2,1)S(1)} %copy-done.4), channel_id=1, source_target_pairs={{0,1},{1,0},{2,3},{3,2},{4,5},{5,4},{6,7},{7,6},{8,9},{9,8},{10,11... | collective-permute-start | bytes 4718600 | tf_op jit(solution)/shard_map/ppermute | solution.py:301
  23.9 12.8 %collective-permute-start.2 = (bf16[1,2048,384]{2,1,0:T(8,128)(2,1)}, bf16[1,2048,384]{2,1,0:T(8,128)(2,1)}, u32[]{:S(2)}, u32[]{:S(2)}) collective-permute-start(bf16[1,2048,384]{2,1,0:T(8,128)(2,1)} %g0.2), channel_id=1, source_target_pairs={{0,1},{1,0},{2,3},{3,2},{4,5},{5,4},{6,7},{7,6},{8,9},{9,8},{10,11... | collective-permute-start | bytes 4718600 | tf_op jit(solution)/shard_map/ppermute | solution.py:301
  24.0 12.7 %collective-permute-start.3 = (bf16[1,2048,384]{2,1,0:T(8,128)(2,1)}, bf16[1,2048,384]{2,1,0:T(8,128)(2,1)}, u32[]{:S(2)}, u32[]{:S(2)}) collective-permute-start(bf16[1,2048,384]{2,1,0:T(8,128)(2,1)} %u0.2), channel_id=1, source_target_pairs={{0,1},{1,0},{2,3},{3,2},{4,5},{5,4},{6,7},{7,6},{8,9},{9,8},{10,11... | collective-permute-start | bytes 4718600 | tf_op jit(solution)/shard_map/ppermute | solution.py:301
  24.5 7.2 %collective-permute-start.4 = (f32[3,1,16]{2,1,0:T(1,128)S(1)}, f32[3,1,16]{2,1,0:T(1,128)S(1)}, u32[]{:S(2)}, u32[]{:S(2)}) collective-permute-start(f32[3,1,16]{2,1,0:T(1,128)S(1)} %bitcast.19), channel_id=1, source_target_pairs={{0,1},{1,0},{2,3},{3,2},{4,5},{5,4},{6,7},{7,6},{8,9},{9,8},{10,11... | collective-permute-start | bytes 584 | tf_op jit(solution)/shard_map/ppermute | solution.py:301
  24.6 12.1 %collective-permute-start = (f32[3,1,16]{2,1,0:T(1,128)S(1)}, f32[3,1,16]{2,1,0:T(1,128)S(1)}, u32[]{:S(2)}, u32[]{:S(2)}) collective-permute-start(f32[3,1,16]{2,1,0:T(1,128)S(1)} %bitcast.21), channel_id=1, source_target_pairs={{0,1},{1,0},{2,3},{3,2},{4,5},{5,4},{6,7},{7,6},{8,9},{9,8},{10,11... | collective-permute-start | bytes 584 | tf_op jit(solution)/shard_map/ppermute | solution.py:301
  31.6 0.6 copy-start.14
  31.6 5.1 %collective-permute-start.1 = (f32[3,1,16]{2,1,0:T(1,128)S(1)}, f32[3,1,16]{2,1,0:T(1,128)S(1)}, u32[]{:S(2)}, u32[]{:S(2)}) collective-permute-start(f32[3,1,16]{2,1,0:T(1,128)S(1)} %bitcast.23), channel_id=1, source_target_pairs={{0,1},{1,0},{2,3},{3,2},{4,5},{5,4},{6,7},{7,6},{8,9},{9,8},{10,11... | collective-permute-start | bytes 584 | tf_op jit(solution)/shard_map/ppermute | solution.py:301
  36.7 0.6 copy-start.12
  36.7 0.6 copy-start.13
  57.0 1.0 copy-start.1
  58.0 19.0 %copy-start.5 = (bf16[1,384,1024]{2,1,0:T(8,128)(2,1)S(1)}, bf16[1,384,1024]{2,1,0:T(8,128)(2,1)}, u32[]{:S(2)}) copy-start(bf16[1,384,1024]{2,1,0:T(8,128)(2,1)} %d0.3) | copy-start | bytes 2359300
  66.9 10.1 %copy-start.3 = (bf16[1,2048,384]{2,1,0:T(8,128)(2,1)S(1)}, bf16[1,2048,384]{2,1,0:T(8,128)(2,1)}, u32[]{:S(2)}) copy-start(bf16[1,2048,384]{2,1,0:T(8,128)(2,1)} %g0.3) | copy-start | bytes 4718596
  66.9 36.3 %all-to-all-start.1 = ((bf16[128,32,128]{2,1,0:T(8,128)(2,1)}), bf16[128,32,128]{2,1,0:T(8,128)(2,1)S(1)}, u32[]{:S(2)}, u32[]{:S(2)}) async-start(bf16[128,32,128]{2,1,0:T(8,128)(2,1)} %experts.1), calls=%async_computation.1 | async-start | bytes 2097152 | tf_op jit(solution)/shard_map/all_to_all | solution.py:305
  75.2 35.7 %collective-permute-start.10 = (bf16[1,2048,384]{2,1,0:T(8,128)(2,1)}, bf16[1,2048,384]{2,1,0:T(8,128)(2,1)}, u32[]{:S(2)}, u32[]{:S(2)}) collective-permute-start(bf16[1,2048,384]{2,1,0:T(8,128)(2,1)} %u0.3), channel_id=1, source_target_pairs={{0,1},{1,0},{2,3},{3,2},{4,5},{5,4},{6,7},{7,6},{8,9},{9,8},{10,11... | collective-permute-start | bytes 4718600 | tf_op jit(solution)/shard_map/ppermute | solution.py:301
  77.0 33.9 %collective-permute-start.9 = (bf16[1,2048,384]{2,1,0:T(8,128)(2,1)S(1)}, bf16[1,2048,384]{2,1,0:T(8,128)(2,1)}, u32[]{:S(2)}, u32[]{:S(2)}) collective-permute-start(bf16[1,2048,384]{2,1,0:T(8,128)(2,1)S(1)} %copy-done.3), channel_id=1, source_target_pairs={{0,1},{1,0},{2,3},{3,2},{4,5},{5,4},{6,7},{7,6},{8,9},{9,8},{10,11... | collective-permute-start | bytes 4718600 | tf_op jit(solution)/shard_map/ppermute | solution.py:301
  77.1 33.5 %collective-permute-start.11 = (bf16[1,384,1024]{2,1,0:T(8,128)(2,1)S(1)}, bf16[1,384,1024]{2,1,0:T(8,128)(2,1)}, u32[]{:S(2)}, u32[]{:S(2)}) collective-permute-start(bf16[1,384,1024]{2,1,0:T(8,128)(2,1)S(1)} %copy-done.5), channel_id=1, source_target_pairs={{0,1},{1,0},{2,3},{3,2},{4,5},{5,4},{6,7},{7,6},{8,9},{9,8},{10,11... | collective-permute-start | bytes 2359304 | tf_op jit(solution)/shard_map/ppermute | solution.py:301
  103.2 1.0 copy-start.2
  108.2 5.4 %collective-permute-start.6 = (bf16[288,128]{1,0:T(8,128)(2,1)}, bf16[288,128]{1,0:T(8,128)(2,1)S(1)}, u32[]{:S(2)}, u32[]{:S(2)}) collective-permute-start(bf16[288,128]{1,0:T(8,128)(2,1)} %get-tuple-element.16.m0), channel_id=1, source_target_pairs={{0,2},{2,4},{4,6},{6,0},{1,3},{3,5},{5,7},{7,1},{8,10},{10,12},{12... | collective-permute-start | bytes 221192 | tf_op jit(solution)/shard_map/ppermute | solution.py:421
  108.3 5.3 %collective-permute-start.7 = (bf16[288,128]{1,0:T(8,128)(2,1)}, bf16[288,128]{1,0:T(8,128)(2,1)S(1)}, u32[]{:S(2)}, u32[]{:S(2)}) collective-permute-start(bf16[288,128]{1,0:T(8,128)(2,1)} %get-tuple-element.16.m0), channel_id=1, source_target_pairs={{0,4},{2,6},{4,0},{6,2},{1,5},{3,7},{5,1},{7,3},{8,12},{10,14},{12... | collective-permute-start | bytes 221192 | tf_op jit(solution)/shard_map/ppermute | solution.py:421
  110.6 3.7 %collective-permute-start.8 = (bf16[288,128]{1,0:T(8,128)(2,1)}, bf16[288,128]{1,0:T(8,128)(2,1)S(1)}, u32[]{:S(2)}, u32[]{:S(2)}) collective-permute-start(bf16[288,128]{1,0:T(8,128)(2,1)} %get-tuple-element.16.m0), channel_id=1, source_target_pairs={{0,6},{2,0},{4,2},{6,4},{1,7},{3,1},{5,3},{7,5},{8,14},{10,8},{12,... | collective-permute-start | bytes 221192 | tf_op jit(solution)/shard_map/ppermute | solution.py:421
  113.6 0.6 copy-start.6
  113.6 0.7 copy-start.7
  114.2 0.6 copy-start.8
  114.8 28.0 %copy-start = (s32[16]{0:T(128)S(1)}, s32[16]{0:T(128)}, u32[]{:S(2)}) copy-start(s32[16]{0:T(128)} %param.39) | copy-start | bytes 196

commit v4 on v3

--- a/solution.py
+++ b/solution.py
@@ -17,8 +17,7 @@
 FH = 384
 TD = 1024
 EPSILON = 1e-06
-MSG = 40
-INFO_ROW = 32
+SLOTS = 2 * CHIPS
 TWIDE = (D + 2 * LANES) // LANES * ROWS
 
 f32 = jnp.float32
@@ -37,19 +36,18 @@
 
 
 def slots(ids):
-    expert = lax.broadcasted_iota(jnp.int32, (LANES, ROWS), 0)
-    picked = jnp.zeros((LANES, ROWS), f32)
+    line = lax.broadcasted_iota(jnp.int32, (SLOTS, ROWS), 0)
+    picked = jnp.zeros((SLOTS, ROWS), f32)
     for k in range(ids.shape[0]):
-        picked = picked + jnp.where(ids[k : k + 1, :] == expert, 1.0, 0.0)
+        picked = picked + jnp.where(ids[k : k + 1, :] == line // 2, 1.0, 0.0)
     before = lax.broadcasted_iota(jnp.int32, (ROWS, ROWS), 0) < lax.broadcasted_iota(
         jnp.int32, (ROWS, ROWS), 1
     )
     rank = jnp.dot(
         picked.astype(bf16), jnp.where(before, 1.0, 0.0).astype(bf16), preferred_element_type=f32
     )
-    first = jnp.where((picked > 0.5) & (rank < 0.5), 1.0, 0.0)
-    second = jnp.where((picked > 0.5) & (rank > 0.5) & (rank < 1.5), 1.0, 0.0)
-    return first, second
+    turn = (line % 2).astype(f32)
+    return jnp.where((picked > 0.5) & (jnp.abs(rank - turn) < 0.5), 1.0, 0.0)
 
 
 def high_low(values):
@@ -66,7 +64,7 @@
 
 def attend_kernel(
     hidden, queries, cache_key, cache_value, new_key, new_value, lengths, gain, ids, source, talk_ids, talk_gates, residual, message, asked, fresh_key, fresh_value,
-    mixed, probs, spread_out, keys, vals, sems,
+    mixed, probs, keys, vals, sems,
 ):
     k_copy = pltpu.make_async_copy(cache_key, keys, sems.at[0])
     v_copy = pltpu.make_async_copy(cache_value, vals, sems.at[1])
@@ -114,8 +112,7 @@
         squares = squares + part * part
     spread = jnp.sum(squares, axis=1, keepdims=True) * (1.0 / D)
     scale = lax.rsqrt(spread + EPSILON)
-    first, second = slots(ids[...])
-    both_slots = jnp.concatenate([first, second], axis=0).astype(bf16)
+    both_slots = slots(ids[...]).astype(bf16)
     for h in range(HEADS // 2):
         pair = []
         for k in range(2):
@@ -124,12 +121,11 @@
             pair.append((residual[:, cols] * scale * line).astype(bf16))
         sent = jnp.dot(both_slots, jnp.concatenate(pair, axis=1), preferred_element_type=f32)
         for k in range(2):
-            cols = slice(k * 128, (k + 1) * 128)
-            spread_out[pl.ds(2 * h + k, CHIPS, stride=32), :] = sent[:CHIPS, cols]
-            spread_out[pl.ds(HEADS + 2 * h + k, CHIPS, stride=32), :] = sent[CHIPS:, cols]
-    message[:, :INFO_ROW, :] = spread_out[...].reshape(CHIPS, 32, LANES).astype(bf16)
+            message[:, 2 * h + k, :, :] = (
+                sent[:, k * 128 : (k + 1) * 128].astype(bf16).reshape(CHIPS, 2, LANES)
+            )
     origin = source[...]
-    chip = lax.broadcasted_iota(jnp.int32, (CHIPS, ROWS), 0)
+    chip = lax.broadcasted_iota(jnp.int32, (SLOTS, ROWS), 0) // 2
     onehot = jnp.where((origin // 32) == chip, 1.0, 0.0).astype(bf16)
     gates = talk_gates[...]
     high = gates.astype(bf16).astype(f32)
@@ -143,9 +139,7 @@
     told = lax.dot_general(
         onehot, facts.astype(bf16), (((1,), (1,)), ((), ())), preferred_element_type=f32
     )
-    message[:, INFO_ROW:, :] = jnp.broadcast_to(
-        told.reshape(CHIPS, 1, LANES), (CHIPS, MSG - INFO_ROW, LANES)
-    ).astype(bf16)
+    message[:, HEADS, :, :] = told.astype(bf16).reshape(CHIPS, 2, LANES)
 
 
 def silu(x):
@@ -179,19 +173,15 @@
                 dw[there, near] = scaled(d[0, rows, near], ds[j, 0, 4 * i + k])
 
 
-def expert_kernel(arrived, g, u, d, produced, message, wide_in, rows_in, gw, uw, dw, out32, sems):
+def expert_kernel(arrived, g, u, d, produced, message, rows_in, gw, uw, dw, sems):
     copies = []
     for i, (src, dst) in enumerate([(arrived, message), (g, gw), (u, uw), (d, dw)]):
         copy = pltpu.make_async_copy(src, dst, sems.at[i])
         copy.start()
         copies.append(copy)
     copies[0].wait()
-    wide_in[...] = message[:, :INFO_ROW, :].astype(f32).reshape(CHIPS * 32, LANES)
-    for s in range(2):
-        for h in range(HEADS):
-            rows_in[s * CHIPS : (s + 1) * CHIPS, h * 128 : (h + 1) * 128] = wide_in[
-                pl.ds(s * HEADS + h, CHIPS, stride=32), :
-            ].astype(bf16)
+    for h in range(HEADS):
+        rows_in[:, h * 128 : (h + 1) * 128] = message[:, h, :, :].reshape(SLOTS, LANES)
     copies[1].wait()
     gated = jnp.dot(rows_in[...], gw[...], preferred_element_type=f32)
     copies[2].wait()
@@ -200,29 +190,22 @@
     copies[3].wait()
     for h in range(HEADS // 2):
         part = jnp.dot(middle, dw[:, h * 256 : (h + 1) * 256], preferred_element_type=f32)
-        for s in range(2):
-            for k in range(2):
-                spot = pl.ds(s * HEADS + 2 * h + k, CHIPS, stride=32)
-                out32[spot, :] = part[s * CHIPS : (s + 1) * CHIPS, k * 128 : (k + 1) * 128]
-    produced[...] = out32[...].reshape(CHIPS, 32, LANES).astype(bf16)
+        for k in range(2):
+            produced[:, 2 * h + k, :, :] = (
+                part[:, k * 128 : (k + 1) * 128].astype(bf16).reshape(CHIPS, 2, LANES)
+            )
 
 
 def combine_kernel(
-    returned, residual, ids, gates, owned, gain, thinker_out, onward, wide_in, rows_in, facts_in,
+    returned, residual, ids, gates, owned, gain, thinker_out, onward, rows_in,
 ):
-    wide_in[...] = returned[...].astype(f32).reshape(CHIPS * 32, LANES)
-    facts_in[...] = owned[...].astype(f32).reshape(CHIPS * 8, LANES)
-    for s in range(2):
-        for h in range(HEADS):
-            rows_in[s * CHIPS : (s + 1) * CHIPS, h * 128 : (h + 1) * 128] = wide_in[
-                pl.ds(s * HEADS + h, CHIPS, stride=32), :
-            ].astype(bf16)
-    expert = lax.broadcasted_iota(jnp.int32, (LANES, ROWS), 0)
-    weight = jnp.zeros((LANES, ROWS), f32)
+    for h in range(HEADS):
+        rows_in[:, h * 128 : (h + 1) * 128] = returned[:, h, :, :].reshape(SLOTS, LANES)
+    expert = lax.broadcasted_iota(jnp.int32, (SLOTS, ROWS), 0) // 2
+    weight = jnp.zeros((SLOTS, ROWS), f32)
     for k in range(8):
         weight = weight + jnp.where(ids[k : k + 1, :] == expert, gates[k : k + 1, :], 0.0)
-    first, second = slots(ids[...])
-    high, low = high_low(jnp.concatenate([first * weight, second * weight], axis=0))
+    high, low = high_low(slots(ids[...]) * weight)
     both = gather_t(jnp.concatenate([high, low], axis=1), rows_in[...])
     outcome = (residual[...] + both[:ROWS] + both[ROWS:]).astype(bf16)
     thinker_out[...] = outcome
@@ -233,7 +216,12 @@
     for h in range(HEADS):
         part = values[:, h * 128 : (h + 1) * 128]
         onward[tile(h), :] = (part * scale * gain[h : h + 1, :].astype(f32)).astype(bf16)
-    told = facts_in[pl.ds(0, CHIPS, stride=8), :].astype(bf16)
+    line = lax.broadcasted_iota(jnp.int32, (CHIPS, SLOTS), 0)
+    even = lax.broadcasted_iota(jnp.int32, (CHIPS, SLOTS), 1) == 2 * line
+    told = jnp.dot(
+        jnp.where(even, 1.0, 0.0).astype(bf16), owned[:, 0, :, :].reshape(SLOTS, LANES),
+        preferred_element_type=f32,
+    ).astype(bf16)
     pick = jnp.where(
         lane_iota(ROWS) == 16 + lax.broadcasted_iota(jnp.int32, (ROWS, LANES), 0), 1.0, 0.0
     ).astype(bf16)
@@ -326,7 +314,7 @@
 
     residual, message = pl.pallas_call(
         attend_kernel,
-        out_shape=(sds((ROWS, D), f32), sds((CHIPS, MSG, LANES), bf16)),
+        out_shape=(sds((ROWS, D), f32), sds((CHIPS, HEADS + 1, 2, LANES), bf16)),
         in_specs=[VM] * 2 + [HB] * 2 + [VM] * 2 + [SM] + [VM] * 5,
         out_specs=(VM, VM),
         scratch_shapes=[
@@ -335,7 +323,6 @@
             pltpu.VMEM((ROWS * HEADS, LANES), f32),
             pltpu.VMEM((ROWS * HEADS, LANES), f32),
             pltpu.VMEM((ROWS * HEADS, LANES), bf16),
-            pltpu.VMEM((CHIPS * 32, LANES), f32),
             pltpu.VMEM((ROWS, CTX, 256), bf16),
             pltpu.VMEM((ROWS, CTX, 256), bf16),
             pltpu.SemaphoreType.DMA((2,)),
@@ -374,17 +361,15 @@
     )(own_scale[2], other_scale[2], own[2], other[2])
     produced = pl.pallas_call(
         expert_kernel,
-        out_shape=sds((CHIPS, 32, LANES), bf16),
+        out_shape=sds((CHIPS, HEADS, 2, LANES), bf16),
         in_specs=[HB] * 4,
         out_specs=VM,
         scratch_shapes=[
-            pltpu.VMEM((CHIPS, MSG, LANES), bf16),
-            pltpu.VMEM((CHIPS * 32, LANES), f32),
+            pltpu.VMEM((CHIPS, HEADS + 1, 2, LANES), bf16),
             pltpu.VMEM((2 * CHIPS, D), bf16),
             pltpu.VMEM((D, 2 * FH), bf16),
             pltpu.VMEM((D, 2 * FH), bf16),
             pltpu.VMEM((2 * FH, D), bf16),
-            pltpu.VMEM((CHIPS * 32, LANES), f32),
             pltpu.SemaphoreType.DMA((4,)),
         ],
         name="experts",
@@ -399,18 +384,16 @@
         grid=(1,),
         out_shape=(sds((ROWS, D), bf16), sds((TWIDE, LANES), bf16)),
         in_specs=[
-            pl.BlockSpec((CHIPS, 32, LANES), lambda i: (0, 0, 0)),
+            pl.BlockSpec((CHIPS, HEADS, 2, LANES), lambda i: (0, 0, 0, 0)),
             pl.BlockSpec((ROWS, D), whole),
             pl.BlockSpec((8, ROWS), whole),
             pl.BlockSpec((8, ROWS), whole),
-            pl.BlockSpec((CHIPS, 8, LANES), lambda i: (0, INFO_ROW // 8, 0)),
+            pl.BlockSpec((CHIPS, 1, 2, LANES), lambda i: (0, HEADS, 0, 0)),
             pl.BlockSpec((HEADS, LANES), whole),
         ],
         out_specs=(pl.BlockSpec((ROWS, D), whole), pl.BlockSpec((TWIDE, LANES), whole)),
         scratch_shapes=[
-            pltpu.VMEM((CHIPS * 32, LANES), f32),
             pltpu.VMEM((2 * CHIPS, D), bf16),
-            pltpu.VMEM((CHIPS * 8, LANES), f32),
         ],
         name="combine",
     )(

time: 147 us -> 139 us (0.946)
  the two profiles are of different devices: /device:TPU:1 before, /device:TPU:2 now
where the time goes in v4:
time: 139 us; the launch traced here: 138 us
  waiting for transfers between devices  50.8 us (37%)
  Pallas kernels  34.9 us (25%)
  starting transfers between devices  27.4 us (20%)
  blocking collectives  20.9 us (15%)
  local copies, waits for them, and re-layouts  3.6 us (3%)
    all_to_all x2, waiting for transfers between devices, exchange(): return lax.all_to_all(value, axes, 0, 0, tiled=True)  39.7 us
    all_to_all x2, starting transfers between devices, exchange(): return lax.all_to_all(value, axes, 0, 0, tiled=True)  22.1 us
    all_to_all x1, blocking collectives, exchange(): return lax.all_to_all(value, axes, 0, 0, tiled=True)  20.9 us
    pallas_call x1, Pallas kernels, local(): pl.pallas_call(restore_tall_kernel, grid=(D // BLK // 2,), out_shape=(sds...  8.32 us
    pallas_call x1, Pallas kernels, local(): pl.pallas_call(expert_kernel, out_shape=sds((CHIPS, HEADS, 2, LANES), bf1...  7.17 us
    ppermute x9, waiting for transfers between devices, swap(): return lax.ppermute(value, 'c', [(0, 1), (1, 0)])  6.93 us
    pallas_call x1, Pallas kernels, local(): pl.pallas_call(talker_kernel, out_shape=sds((CHIPS, 8, LANES), bf16), in_...  5.74 us
    pallas_call x1, Pallas kernels, local(): pl.pallas_call(attend_kernel, out_shape=(sds((ROWS, D), f32), sds((CHIPS,...  5.01 us
  transfers between devices with their start and end apart: 14, of which 6 were waited for; matrix products, arithmetic and copies ran while one was open for 0% of the time, Pallas kernels for 12%

profile of v4, /device:TPU:2, one launch (start us, length us, event | category | flops | bytes accessed | tf_op | source)
XLA Modules:
  0.0 138.5 jit_solution(12746000150674935057)
XLA Ops:
  0.6 5.0 %attend.1 = (f32[16,2048]{1,0:T(8,128)}, bf16[128,17,2,128]{3,2,1,0:T(2,128)(2,1)}) custom-call(bf16[16,2048]{1,0:T(8,128)(2,1)} %hidden.1, bf16[16,2048]{1,0:T(8,128)(2,1)} %queries.1, bf16[16,128,256]{2,1,0:T(8,128)(2,1)} %cache_key.1, bf16[16,128,256]{2,1,0:T(8,128)(2,1)} %cache_value.1, bf16[16,256]{1,0:T(8,128)(2,1)} %new_key.1, ...), custom_call_target="tpu_custom_call" | custom-call | tf_op jit(solution)/shard_map/attend/pallas_call | solution.py:315
  5.6 0.0 copy-start.4
  5.7 0.0 copy-start.9
  5.7 0.0 copy-start.10
  5.7 0.0 copy-start.11
  5.7 15.6 %all-to-all-start = ((bf16[128,17,2,128]{3,2,1,0:T(2,128)(2,1)}), bf16[128,17,2,128]{3,2,1,0:T(2,128)(2,1)S(1)}, u32[]{:S(2)}, u32[]{:S(2)}) async-start(bf16[128,17,2,128]{3,2,1,0:T(2,128)(2,1)} %get-tuple-element.11), calls=%async_computation | async-start | bytes 2228224 | tf_op jit(solution)/shard_map/all_to_all | solution.py:293
  21.3 0.1 collective-permute-start.5
  21.4 0.5 collective-permute-start.2
  21.9 0.1 collective-permute-start.3
  22.0 0.4 collective-permute-start.4
  22.4 0.1 collective-permute-start
  22.5 6.9 %collective-permute-done.4.ds1 = f32[3,1,16]{2,1,0:T(1,128)S(1)} collective-permute-done((f32[3,1,16]{2,1,0:T(1,128)S(1)}, f32[3,1,16]{2,1,0:T(1,128)S(1)}, u32[]{:S(2)}, u32[]{:S(2)}) %collective-permute-start.4) | collective-permute-done | bytes 224 | tf_op jit(solution)/shard_map/ppermute | solution.py:289
  29.4 0.1 collective-permute-start.1
  29.6 0.0 collective-permute-done.5.d1
  29.6 0.4 copy-done.14
  30.0 4.5 %restore_flat.1.d = bf16[768,2048]{1,0:T(8,128)(2,1)} custom-call(f32[3,1,16]{2,1,0:T(1,128)} %bitcast.18, f32[3,1,16]{2,1,0:T(1,128)} %copy-done.14, bf16[1,384,2048]{2,1,0:T(8,128)(2,1)} %d0.2, bf16[1,384,2048]{2,1,0:T(8,128)(2,1)} %collective-permute-done.5.d1), custom_call_target="tpu_custom_call" | custom-call | flops 1572864 | bytes 6291456 | tf_op jit(solution)/shard_map/restore_flat/pallas_call | solution.py:351
  34.5 0.0 collective-permute-done.gs1
  34.5 0.0 collective-permute-done.1.us1
  34.5 0.0 copy-start.13
  34.5 0.0 collective-permute-done.2.g1
  34.5 0.0 collective-permute-done.3.u1
  34.6 0.5 copy-done.12
  35.1 0.0 copy-done.13
  35.1 8.3 %restore_tall.1 = (bf16[2048,768]{1,0:T(8,128)(2,1)}, bf16[2048,768]{1,0:T(8,128)(2,1)}) custom-call(f32[3,1,16]{2,1,0:T(1,128)} %bitcast.20, f32[3,1,16]{2,1,0:T(1,128)} %bitcast.22, f32[3,1,16]{2,1,0:T(1,128)} %copy-done.12, f32[3,1,16]{2,1,0:T(1,128)} %copy-done.13, bf16[1,2048,384]{2,1,0:T(8,128)(2,1)} %g0.2, bf16[1,2048,384]{2,1,0:T(8,128)(2,1)} %u0.2, ...), custom_call_target="tpu_custom_call" | custom-call | flops 3145728 | bytes 12582912 | tf_op jit(solution)/shard_map/restore_tall/pallas_call | solution.py:338
  43.4 10.3 %all-to-all-done.arrived.owned = bf16[128,17,2,128]{3,2,1,0:T(2,128)(2,1)S(1)} async-done(((bf16[128,17,2,128]{3,2,1,0:T(2,128)(2,1)}), bf16[128,17,2,128]{3,2,1,0:T(2,128)(2,1)S(1)}, u32[]{:S(2)}, u32[]{:S(2)}) %all-to-all-start) | async-done | bytes 1114144 | tf_op jit(solution)/shard_map/all_to_all | solution.py:293
  53.8 1.0 copy-done.1
  54.8 7.2 %experts.1 = bf16[128,16,2,128]{3,2,1,0:T(2,128)(2,1)} custom-call(bf16[128,17,2,128]{3,2,1,0:T(2,128)(2,1)} %copy-done.1, bf16[2048,768]{1,0:T(8,128)(2,1)} %get-tuple-element.12.g, bf16[2048,768]{1,0:T(8,128)(2,1)} %get-tuple-element.13.u, bf16[768,2048]{1,0:T(8,128)(2,1)} %restore_flat.1.d), custom_call_target="tpu_custom_call" | custom-call | tf_op jit(solution)/shard_map/experts/pallas_call | solution.py:362
  62.0 0.0 copy-start.3
  62.0 6.5 %all-to-all-start.1 = ((bf16[128,16,2,128]{3,2,1,0:T(2,128)(2,1)}), bf16[128,16,2,128]{3,2,1,0:T(2,128)(2,1)S(1)}, u32[]{:S(2)}, u32[]{:S(2)}) async-start(bf16[128,16,2,128]{3,2,1,0:T(2,128)(2,1)} %experts.1), calls=%async_computation.1 | async-start | bytes 2097152 | tf_op jit(solution)/shard_map/all_to_all | solution.py:293
  68.5 0.1 collective-permute-start.10
  68.6 0.5 collective-permute-start.9
  69.1 0.1 collective-permute-start.11
  69.2 29.4 %all-to-all-done.1.returned = bf16[128,16,2,128]{3,2,1,0:T(2,128)(2,1)S(1)} async-done(((bf16[128,16,2,128]{3,2,1,0:T(2,128)(2,1)}), bf16[128,16,2,128]{3,2,1,0:T(2,128)(2,1)S(1)}, u32[]{:S(2)}, u32[]{:S(2)}) %all-to-all-start.1) | async-done | bytes 1048608 | tf_op jit(solution)/shard_map/all_to_all | solution.py:293
  98.6 1.0 copy-done.2
  99.6 3.3 %combine.1 = (bf16[16,2048]{1,0:T(8,128)(2,1)}, bf16[288,128]{1,0:T(8,128)(2,1)}) custom-call(bf16[128,16,2,128]{3,2,1,0:T(2,128)(2,1)} %copy-done.2, f32[16,2048]{1,0:T(8,128)} %get-tuple-element.14.residual, s32[8,16]{1,0:T(8,128)} %bitcast.14, f32[8,16]{1,0:T(8,128)} %bitcast.16, bf16[128,17,2,128]{3,2,1,0:T(2,128)(2,1)} %copy-done.1, ...), custom_call_target="tpu_custom_call" | custom-call | tf_op jit(solution)/shard_map/combine/pallas_call | solution.py:382
  102.9 0.5 collective-permute-start.6
  103.4 1.0 collective-permute-start.7
  104.4 0.0 collective-permute-done.11.d1
  104.4 1.7 %collective-permute-start.8 = (bf16[288,128]{1,0:T(8,128)(2,1)}, bf16[288,128]{1,0:T(8,128)(2,1)S(1)}, u32[]{:S(2)}, u32[]{:S(2)}) collective-permute-start(bf16[288,128]{1,0:T(8,128)(2,1)} %get-tuple-element.16.m0), channel_id=1, source_target_pairs={{0,6},{2,0},{4,2},{6,4},{1,7},{3,1},{5,3},{7,5},{8,14},{10,8},{12,... | collective-permute-start | bytes 221192 | tf_op jit(solution)/shard_map/ppermute | solution.py:404
  106.1 0.0 collective-permute-done.10.u1
  106.1 0.0 collective-permute-done.9.g1
  106.1 2.5 %collective-permute-done.6.m1 = bf16[288,128]{1,0:T(8,128)(2,1)S(1)} collective-permute-done((bf16[288,128]{1,0:T(8,128)(2,1)}, bf16[288,128]{1,0:T(8,128)(2,1)S(1)}, u32[]{:S(2)}, u32[]{:S(2)}) %collective-permute-start.6) | collective-permute-done | bytes 73760 | tf_op jit(solution)/shard_map/ppermute | solution.py:404
  108.7 0.8 collective-permute-done.7.m2
  109.5 0.8 collective-permute-done.8.m3
  110.3 0.6 copy-done.8
  110.9 5.7 %talkers.1 = bf16[128,8,128]{2,1,0:T(8,128)(2,1)} custom-call(s32[1]{0:T(128)} %bitcast.10.place, bf16[288,128]{1,0:T(8,128)(2,1)} %get-tuple-element.16.m0, bf16[288,128]{1,0:T(8,128)(2,1)} %copy-done.6, bf16[288,128]{1,0:T(8,128)(2,1)} %copy-done.7, bf16[288,128]{1,0:T(8,128)(2,1)} %copy-done.8, bf16[1,2048,384]{2,1,0:T(8,128)(2,1)} %g0.3, ...), custom_call_target="tpu_custom_call" | custom-call | tf_op jit(solution)/shard_map/talkers/pallas_call | solution.py:407
  116.7 20.9 %all_to_all.15.returned = bf16[128,8,128]{2,1,0:T(8,128)(2,1)S(1)} all-to-all(bf16[128,8,128]{2,1,0:T(8,128)(2,1)} %talkers.1), channel_id=1, replica_groups=mesh['z'=8,'x'=4,'y'=4,'c'=2] {'z','x','y'}, dimensions={0} | all-to-all | bytes 524288 | tf_op jit(solution)/shard_map/all_to_all | solution.py:293
  137.6 0.8 settle.1
  (18 shorter events, 0.0 us)
Async XLA Ops:
  5.6 15.7 %copy-start.4 = (bf16[1,384,2048]{2,1,0:T(8,128)(2,1)S(1)}, bf16[1,384,2048]{2,1,0:T(8,128)(2,1)}, u32[]{:S(2)}) copy-start(bf16[1,384,2048]{2,1,0:T(8,128)(2,1)} %d0.2) | copy-start | bytes 4718596
  5.7 16.4 %copy-start.9 = (f32[1,3,16]{2,0,1:T(1,128)S(1)}, f32[1,3,16]{2,0,1:T(1,128)}, u32[]{:S(2)}) copy-start(f32[1,3,16]{2,0,1:T(1,128)} %param.36) | copy-start | bytes 580
  5.7 16.8 %copy-start.10 = (f32[1,16,3]{1,0,2:T(1,128)S(1)}, f32[1,16,3]{1,0,2:T(1,128)}, u32[]{:S(2)}) copy-start(f32[1,16,3]{1,0,2:T(1,128)} %param.32) | copy-start | bytes 580
  5.7 23.8 %copy-start.11 = (f32[1,16,3]{1,0,2:T(1,128)S(1)}, f32[1,16,3]{1,0,2:T(1,128)}, u32[]{:S(2)}) copy-start(f32[1,16,3]{1,0,2:T(1,128)} %param.34) | copy-start | bytes 580
  5.7 48.1 %all-to-all-start = ((bf16[128,17,2,128]{3,2,1,0:T(2,128)(2,1)}), bf16[128,17,2,128]{3,2,1,0:T(2,128)(2,1)S(1)}, u32[]{:S(2)}, u32[]{:S(2)}) async-start(bf16[128,17,2,128]{3,2,1,0:T(2,128)(2,1)} %get-tuple-element.11), calls=%async_computation | async-start | bytes 2228224 | tf_op jit(solution)/shard_map/all_to_all | solution.py:293
  21.3 8.3 %collective-permute-start.5 = (bf16[1,384,2048]{2,1,0:T(8,128)(2,1)S(1)}, bf16[1,384,2048]{2,1,0:T(8,128)(2,1)}, u32[]{:S(2)}, u32[]{:S(2)}) collective-permute-start(bf16[1,384,2048]{2,1,0:T(8,128)(2,1)S(1)} %copy-done.4), channel_id=1, source_target_pairs={{0,1},{1,0},{2,3},{3,2},{4,5},{5,4},{6,7},{7,6},{8,9},{9,8},{10,11... | collective-permute-start | bytes 4718600 | tf_op jit(solution)/shard_map/ppermute | solution.py:289
  21.4 13.1 %collective-permute-start.2 = (bf16[1,2048,384]{2,1,0:T(8,128)(2,1)}, bf16[1,2048,384]{2,1,0:T(8,128)(2,1)}, u32[]{:S(2)}, u32[]{:S(2)}) collective-permute-start(bf16[1,2048,384]{2,1,0:T(8,128)(2,1)} %g0.2), channel_id=1, source_target_pairs={{0,1},{1,0},{2,3},{3,2},{4,5},{5,4},{6,7},{7,6},{8,9},{9,8},{10,11... | collective-permute-start | bytes 4718600 | tf_op jit(solution)/shard_map/ppermute | solution.py:289
  21.9 12.6 %collective-permute-start.3 = (bf16[1,2048,384]{2,1,0:T(8,128)(2,1)}, bf16[1,2048,384]{2,1,0:T(8,128)(2,1)}, u32[]{:S(2)}, u32[]{:S(2)}) collective-permute-start(bf16[1,2048,384]{2,1,0:T(8,128)(2,1)} %u0.2), channel_id=1, source_target_pairs={{0,1},{1,0},{2,3},{3,2},{4,5},{5,4},{6,7},{7,6},{8,9},{9,8},{10,11... | collective-permute-start | bytes 4718600 | tf_op jit(solution)/shard_map/ppermute | solution.py:289
  22.0 7.4 %collective-permute-start.4 = (f32[3,1,16]{2,1,0:T(1,128)S(1)}, f32[3,1,16]{2,1,0:T(1,128)S(1)}, u32[]{:S(2)}, u32[]{:S(2)}) collective-permute-start(f32[3,1,16]{2,1,0:T(1,128)S(1)} %bitcast.19), channel_id=1, source_target_pairs={{0,1},{1,0},{2,3},{3,2},{4,5},{5,4},{6,7},{7,6},{8,9},{9,8},{10,11... | collective-permute-start | bytes 584 | tf_op jit(solution)/shard_map/ppermute | solution.py:289
  22.4 12.1 %collective-permute-start = (f32[3,1,16]{2,1,0:T(1,128)S(1)}, f32[3,1,16]{2,1,0:T(1,128)S(1)}, u32[]{:S(2)}, u32[]{:S(2)}) collective-permute-start(f32[3,1,16]{2,1,0:T(1,128)S(1)} %bitcast.21), channel_id=1, source_target_pairs={{0,1},{1,0},{2,3},{3,2},{4,5},{5,4},{6,7},{7,6},{8,9},{9,8},{10,11... | collective-permute-start | bytes 584 | tf_op jit(solution)/shard_map/ppermute | solution.py:289
  29.4 0.6 copy-start.14
  29.4 5.1 %collective-permute-start.1 = (f32[3,1,16]{2,1,0:T(1,128)S(1)}, f32[3,1,16]{2,1,0:T(1,128)S(1)}, u32[]{:S(2)}, u32[]{:S(2)}) collective-permute-start(f32[3,1,16]{2,1,0:T(1,128)S(1)} %bitcast.23), channel_id=1, source_target_pairs={{0,1},{1,0},{2,3},{3,2},{4,5},{5,4},{6,7},{7,6},{8,9},{9,8},{10,11... | collective-permute-start | bytes 584 | tf_op jit(solution)/shard_map/ppermute | solution.py:289
  34.5 0.6 copy-start.12
  34.5 0.6 copy-start.13
  53.8 1.0 copy-start.1
  54.8 14.3 %copy-start.5 = (bf16[1,384,1024]{2,1,0:T(8,128)(2,1)S(1)}, bf16[1,384,1024]{2,1,0:T(8,128)(2,1)}, u32[]{:S(2)}) copy-start(bf16[1,384,1024]{2,1,0:T(8,128)(2,1)} %d0.3) | copy-start | bytes 2359300
  62.0 6.6 %copy-start.3 = (bf16[1,2048,384]{2,1,0:T(8,128)(2,1)S(1)}, bf16[1,2048,384]{2,1,0:T(8,128)(2,1)}, u32[]{:S(2)}) copy-start(bf16[1,2048,384]{2,1,0:T(8,128)(2,1)} %g0.3) | copy-start | bytes 4718596
  62.0 36.6 %all-to-all-start.1 = ((bf16[128,16,2,128]{3,2,1,0:T(2,128)(2,1)}), bf16[128,16,2,128]{3,2,1,0:T(2,128)(2,1)S(1)}, u32[]{:S(2)}, u32[]{:S(2)}) async-start(bf16[128,16,2,128]{3,2,1,0:T(2,128)(2,1)} %experts.1), calls=%async_computation.1 | async-start | bytes 2097152 | tf_op jit(solution)/shard_map/all_to_all | solution.py:293
  68.5 37.6 %collective-permute-start.10 = (bf16[1,2048,384]{2,1,0:T(8,128)(2,1)}, bf16[1,2048,384]{2,1,0:T(8,128)(2,1)}, u32[]{:S(2)}, u32[]{:S(2)}) collective-permute-start(bf16[1,2048,384]{2,1,0:T(8,128)(2,1)} %u0.3), channel_id=1, source_target_pairs={{0,1},{1,0},{2,3},{3,2},{4,5},{5,4},{6,7},{7,6},{8,9},{9,8},{10,11... | collective-permute-start | bytes 4718600 | tf_op jit(solution)/shard_map/ppermute | solution.py:289
  68.6 37.5 %collective-permute-start.9 = (bf16[1,2048,384]{2,1,0:T(8,128)(2,1)S(1)}, bf16[1,2048,384]{2,1,0:T(8,128)(2,1)}, u32[]{:S(2)}, u32[]{:S(2)}) collective-permute-start(bf16[1,2048,384]{2,1,0:T(8,128)(2,1)S(1)} %copy-done.3), channel_id=1, source_target_pairs={{0,1},{1,0},{2,3},{3,2},{4,5},{5,4},{6,7},{7,6},{8,9},{9,8},{10,11... | collective-permute-start | bytes 4718600 | tf_op jit(solution)/shard_map/ppermute | solution.py:289
  69.1 35.4 %collective-permute-start.11 = (bf16[1,384,1024]{2,1,0:T(8,128)(2,1)S(1)}, bf16[1,384,1024]{2,1,0:T(8,128)(2,1)}, u32[]{:S(2)}, u32[]{:S(2)}) collective-permute-start(bf16[1,384,1024]{2,1,0:T(8,128)(2,1)S(1)} %copy-done.5), channel_id=1, source_target_pairs={{0,1},{1,0},{2,3},{3,2},{4,5},{5,4},{6,7},{7,6},{8,9},{9,8},{10,11... | collective-permute-start | bytes 2359304 | tf_op jit(solution)/shard_map/ppermute | solution.py:289
  98.6 1.0 copy-start.2
  102.9 5.8 %collective-permute-start.6 = (bf16[288,128]{1,0:T(8,128)(2,1)}, bf16[288,128]{1,0:T(8,128)(2,1)S(1)}, u32[]{:S(2)}, u32[]{:S(2)}) collective-permute-start(bf16[288,128]{1,0:T(8,128)(2,1)} %get-tuple-element.16.m0), channel_id=1, source_target_pairs={{0,2},{2,4},{4,6},{6,0},{1,3},{3,5},{5,7},{7,1},{8,10},{10,12},{12... | collective-permute-start | bytes 221192 | tf_op jit(solution)/shard_map/ppermute | solution.py:404
  103.4 6.1 %collective-permute-start.7 = (bf16[288,128]{1,0:T(8,128)(2,1)}, bf16[288,128]{1,0:T(8,128)(2,1)S(1)}, u32[]{:S(2)}, u32[]{:S(2)}) collective-permute-start(bf16[288,128]{1,0:T(8,128)(2,1)} %get-tuple-element.16.m0), channel_id=1, source_target_pairs={{0,4},{2,6},{4,0},{6,2},{1,5},{3,7},{5,1},{7,3},{8,12},{10,14},{12... | collective-permute-start | bytes 221192 | tf_op jit(solution)/shard_map/ppermute | solution.py:404
  104.4 5.9 %collective-permute-start.8 = (bf16[288,128]{1,0:T(8,128)(2,1)}, bf16[288,128]{1,0:T(8,128)(2,1)S(1)}, u32[]{:S(2)}, u32[]{:S(2)}) collective-permute-start(bf16[288,128]{1,0:T(8,128)(2,1)} %get-tuple-element.16.m0), channel_id=1, source_target_pairs={{0,6},{2,0},{4,2},{6,4},{1,7},{3,1},{5,3},{7,5},{8,14},{10,8},{12,... | collective-permute-start | bytes 221192 | tf_op jit(solution)/shard_map/ppermute | solution.py:404
  108.7 1.7 %copy-start.6 = (bf16[288,128]{1,0:T(8,128)(2,1)}, bf16[288,128]{1,0:T(8,128)(2,1)S(1)}, u32[]{:S(2)}) copy-start(bf16[288,128]{1,0:T(8,128)(2,1)S(1)} %collective-permute-done.6.m1) | copy-start | bytes 221188
  109.5 0.8 copy-start.7
  110.3 0.6 copy-start.8
  110.9 26.7 %copy-start = (s32[16]{0:T(128)S(1)}, s32[16]{0:T(128)}, u32[]{:S(2)}) copy-start(s32[16]{0:T(128)} %param.39) | copy-start | bytes 196
